TPU v7x, 256 devices: a whole 4x4x8 slice. The times are simulated.
256 devices in a mesh: bulk: 16 (over z, core), wide: 16 (over y, x).
Axes of the slice: x: 4, y: 4, z: 8, core: 2. Of those that a mesh axis runs over, the one named last changes fastest.
Arguments:
- wavefunction: float32 [16384, 512], P('wide'), may hold values from -6 to 6
- env_blocks: float32 [256, 2048, 1024], P('bulk', 'wide'), may hold values from -0.1875 to 0.1875
- right_env: float32 [32, 512, 512], P('bulk'), may hold values from -0.0625 to 0.0625
- tile_sector: int32 [128], replicated, may hold values from 0 to 31, never falling along the last dimension, each value on 1 to 8 neighbouring positions
- term_charge: int32 [32], replicated, may hold values from -1 to 1
- block_home: int32 [16, 16], replicated, may hold values from 0 to 15, as said below
Outputs:
- applied: float32 [16384, 512], P('wide', 'bulk')
Inputs may be any that keep to these rules, and one draw needn't show every extreme that they name: `tile_sector`: never falls; each sector 0 to 31 covers 1 to 8 whole tiles, one exactly 8. `term_charge`: each MPO term raises, keeps or lowers the left quantum number by one. For each pair index k the column block_home[:, k] is a permutation of the bulk indices, so every device stores exactly one block of each k; at most 2 blocks of one term owner lie on one device, and some device holds 2 of them.
All inputs are finite; a program needn't handle non-finite values.
Results may differ from a plain program's by a relative error of at most 0.0003.
Values sent between devices are 32-bit elements; how exact they have to be, the bound alone decides.
No kernel may reach another device: no remote copies, remote signals or barrier semaphores. Data moves between devices by JAX's collectives and lax.ppermute only.
A program may use at most 192 MiB of HBM per device.

v0:
```python
import jax
import jax.numpy as jnp
from jax import lax
from jax.sharding import PartitionSpec as P

TILE = 128
NW_DEV = 2
SLOT = 2
TILE_DEV = 8
SRC = 1024
PAIRS = 16
REACH = 2


precise = lax.Precision.HIGHEST


def from_behind(value, axis, steps):
    count = lax.axis_size(axis)
    initial, last = (max(0, -steps), min(count, count - steps))
    return lax.ppermute(value, axis, [(source, source + steps) for source in range(initial, last)])


def neighbour(panel, offset):
    return from_behind(panel, "wide", offset)


def window_plan(tile_sector, term_charge, tiles_of, terms_of):
    count_tiles = tile_sector.shape[0]
    labels = jnp.arange(count_tiles, dtype=jnp.int32)
    starts = jnp.sum((tile_sector[None, :] < labels[:, None]).astype(jnp.int32), axis=1)
    widths = jnp.sum((tile_sector[None, :] == labels[:, None]).astype(jnp.int32), axis=1)
    sectors = tile_sector[count_tiles - 1] + 1
    source = tile_sector[tiles_of] + term_charge[terms_of]
    usable = (source >= 0) & (source < sectors)
    clipped = jnp.clip(source, 0, count_tiles - 1)
    return (starts[clipped], jnp.where(usable, widths[clipped] * TILE, 0))


def on_device(wavefunction, env_blocks, right_env, tile_sector, term_charge, block_home):
    home_count = lax.axis_size("bulk")
    owner_index = lax.axis_index("bulk")
    column = lax.axis_index("wide")
    below_rows = [neighbour(wavefunction, offset) for offset in range(REACH, 0, -1)]
    above_rows = [neighbour(wavefunction, -offset) for offset in range(1, REACH + 1)]
    extended = jnp.concatenate(below_rows + [wavefunction] + above_rows, axis=0)
    base_tile = (column - REACH) * TILE_DEV
    window_rows = jnp.arange(SRC, dtype=jnp.int32)
    pair_ids = jnp.arange(PAIRS, dtype=jnp.int32)
    tile_local = pair_ids // NW_DEV
    term_local = pair_ids % NW_DEV
    my_tiles = column * TILE_DEV + tile_local
    earlier = pair_ids[None, :] < pair_ids[:, None]
    home_ids = jnp.arange(home_count, dtype=jnp.int32)
    stored_dest = jnp.sum(home_ids[:, None] * (block_home == owner_index).astype(jnp.int32), axis=0)
    stored_slot = jnp.sum(
        (earlier & (stored_dest[None, :] == stored_dest[:, None])).astype(jnp.int32), axis=1
    )
    matched = (stored_dest[None, None, :] == home_ids[:, None, None]) & (
        stored_slot[None, None, :] == jnp.arange(SLOT, dtype=jnp.int32)[None, :, None]
    )
    pick_index = jnp.sum(pair_ids[None, None, :] * matched.astype(jnp.int32), axis=2)
    filled = jnp.any(matched, axis=2)
    home_of = block_home[owner_index]
    slot_of = jnp.sum((earlier & (home_of[None, :] == home_of[:, None])).astype(jnp.int32), axis=1)
    arrival = home_of * SLOT + slot_of

    def contract_left(operands):
        env_block, start_row, live_rows = operands
        window = lax.dynamic_slice(extended, (start_row, jnp.int32(0)), (SRC, extended.shape[1]))
        window = jnp.where((window_rows < live_rows)[:, None], window, 0.0)
        return jnp.dot(env_block, window, precision=precise, preferred_element_type=jnp.float32)

    packed = jnp.take(env_blocks, pick_index.reshape(-1), axis=0).reshape(
        (home_count, SLOT) + env_blocks.shape[1:]
    )
    arrived = lax.all_to_all(
        jnp.where(filled[:, :, None, None], packed, 0.0),
        "bulk",
        split_axis=0,
        concat_axis=0,
        tiled=True,
    )
    blocks = arrived.reshape((home_count * SLOT,) + env_blocks.shape[1:])[arrival]
    my_terms = owner_index * NW_DEV + term_local
    first_tile, live_rows = window_plan(tile_sector, term_charge, my_tiles, my_terms)
    first_row = (first_tile - base_tile) * TILE
    left_parts = lax.map(contract_left, (blocks, first_row, live_rows))

    def contract_right(operands):
        left_part, term_index = operands
        return jnp.dot(
            left_part, right_env[term_index], precision=precise, preferred_element_type=jnp.float32
        )

    term_parts = lax.map(contract_right, (left_parts, term_local))
    summed = jnp.sum(term_parts.reshape(TILE_DEV, NW_DEV, TILE, term_parts.shape[2]), axis=1)
    summed = summed.reshape(TILE_DEV * TILE, term_parts.shape[2])
    return lax.psum_scatter(summed, "bulk", scatter_dimension=1, tiled=True)


def solution(mesh):
    return jax.shard_map(
        on_device,
        mesh=mesh,
        in_specs=(P("wide", None), P("bulk", "wide", None), P("bulk", None, None), P(), P(), P()),
        out_specs=P("wide", "bulk"),
        check_vma=False,
    )
```

profile of v0, /device:TPU:6, one launch (start us, length us, event | category | flops | bytes accessed | tf_op | source)
XLA Modules:
  0.0 698.8 jit_solution(16264479814748081253)
XLA Ops:
  6.5 0.7 select_reduce_fusion
  8.8 1.3 gather_fusion.2
  10.2 11.5 %gather_fusion = f32[32,128,1024]{2,1,0:T(8,128)} fusion(f32[16,128,1024]{2,1,0:T(8,128)} %param.11, s32[1024]{0:T(1024)S(1)} %get-tuple-element.110), kind=kCustom, calls=%fused_computation | custom fusion | bytes 33554560 | tf_op jit(solution)/shard_map/jit(_take)/gather | solution.py:74
  21.7 12.6 %select_select_fusion = f32[16,2,128,1024]{3,2,1,0:T(8,128)} fusion(f32[16,2,128,1024]{3,2,1,0:T(8,128)} %bitcast.62, pred[16,2]{1,0:T(8,128)(4,1)S(1)} %copy.9, pred[16,2]{1,0:T(8,128)(4,1)S(1)} %copy.8), kind=kLoop, calls=%fused_computation.26 | loop fusion | flops 8388608 | bytes 33554496 | tf_op jit(solution)/shard_map/jit(_where)/select_n | solution.py:78
  34.3 8.8 %all-to-all-start = ((f32[16,2,128,1024]{3,2,1,0:T(8,128)}), f32[16,2,128,1024]{3,2,1,0:T(8,128)}, u32[]{:S(2)}, u32[]{:S(2)}) async-start(f32[16,2,128,1024]{3,2,1,0:T(8,128)} %select_select_fusion), calls=%async_computation | async-start | bytes 33554432 | tf_op jit(solution)/shard_map/all_to_all | solution.py:77
  43.1 4.3 collective-permute-start
  47.4 4.0 collective-permute-start.1
  51.5 1.9 collective-permute-start.2
  53.4 5.5 collective-permute-start.3
  61.7 0.7 fusion.33
  62.6 0.7 fusion.31
  63.3 31.7 %collective-permute-done = f32[1024,512]{1,0:T(8,128)} collective-permute-done((f32[1024,512]{1,0:T(8,128)S(1)}, f32[1024,512]{1,0:T(8,128)}, u32[]{:S(2)}, u32[]{:S(2)}) %collective-permute-start) | collective-permute-done | bytes 2097184 | tf_op jit(solution)/shard_map/ppermute | solution.py:21
  95.1 3.1 constant_dynamic-update-slice_fusion.4
  98.1 40.7 %collective-permute-done.1 = f32[1024,512]{1,0:T(8,128)} collective-permute-done((f32[1024,512]{1,0:T(8,128)S(1)}, f32[1024,512]{1,0:T(8,128)}, u32[]{:S(2)}, u32[]{:S(2)}) %collective-permute-start.1) | collective-permute-done | bytes 2097184 | tf_op jit(solution)/shard_map/ppermute | solution.py:21
  138.9 3.1 constant_dynamic-update-slice_fusion.3
  142.0 1.5 constant_dynamic-update-slice_fusion.2
  143.5 3.1 constant_dynamic-update-slice_fusion.1
  146.5 38.9 %collective-permute-done.3 = f32[1024,512]{1,0:T(8,128)} collective-permute-done((f32[1024,512]{1,0:T(8,128)S(1)}, f32[1024,512]{1,0:T(8,128)}, u32[]{:S(2)}, u32[]{:S(2)}) %collective-permute-start.3) | collective-permute-done | bytes 2097184 | tf_op jit(solution)/shard_map/ppermute | solution.py:21
  185.4 3.1 constant_dynamic-update-slice_fusion
  188.5 218.5 %all-to-all-done = f32[16,2,128,1024]{3,2,1,0:T(8,128)} async-done(((f32[16,2,128,1024]{3,2,1,0:T(8,128)}), f32[16,2,128,1024]{3,2,1,0:T(8,128)}, u32[]{:S(2)}, u32[]{:S(2)}) %all-to-all-start) | async-done | bytes 16777248 | tf_op jit(solution)/shard_map/all_to_all | solution.py:77
  407.0 10.1 %gather_fusion.1 = f32[16,128,1024]{2,1,0:T(8,128)} fusion(f32[32,128,1024]{2,1,0:T(8,128)} %bitcast.6, s32[1024]{0:T(1024)S(1)} %pad_clamp_fusion.3), kind=kCustom, calls=%fused_computation.1 | custom fusion | bytes 16777280 | tf_op jit(solution)/shard_map/gather | solution.py:84
  417.1 2.5 broadcast.275.clone
  419.6 128.8 %while.22 = (s32[]{:T(128)}, f32[16,128,512]{2,1,0:T(8,128)}, f32[16,128,1024]{2,1,0:T(8,128)}, s32[16]{0:T(128)S(1)}, s32[16]{0:T(128)S(1)}, /*index=5*/f32[5120,512]{1,0:T(8,128)}, s32[]{:T(128)}, s32[]{:T(128)}, s32[]{:T(128)}) while((s32[]{:T(128)}, f32[16,128,512]{2,1,0:T(8,128)}, f32[16,128,1024]{2,1,0:T(8,128)}, ...), condition=%wide.region_8.9_spmd.clone, body=%wide.region_7.8_spmd.clone.sunk | while | flops 805831680 | bytes 2886815 | solution.py:88
  422.9 0.7 iota_compare_fusion.7
  423.6 4.0 fusion.45
  431.7 4.0 fusion.45
  439.7 4.1 fusion.45
  447.1 0.7 iota_compare_fusion.7
  447.8 4.1 fusion.45
  455.8 4.0 fusion.45
  463.2 0.7 iota_compare_fusion.7
  463.9 4.0 fusion.45
  471.9 4.1 fusion.45
  479.3 0.7 iota_compare_fusion.7
  480.0 4.0 fusion.45
  488.0 4.1 fusion.45
  496.1 4.1 fusion.45
  504.2 4.1 fusion.45
  512.2 4.0 fusion.45
  520.3 4.0 fusion.45
  528.3 4.0 fusion.45
  536.3 4.0 fusion.45
  544.4 4.1 fusion.45
  548.4 2.5 broadcast.275
  550.9 77.2 %while.21 = (s32[]{:T(128)}, f32[16,128,512]{2,1,0:T(8,128)}, f32[16,128,512]{2,1,0:T(8,128)}, s32[16]{0:T(128)S(1)}, f32[2,512,512]{2,1,0:T(8,128)S(1)}, /*index=5*/s32[]{:T(128)}, s32[]{:T(128)}, s32[]{:T(128)}) while((s32[]{:T(128)}, f32[16,128,512]{2,1,0:T(8,128)}, f32[16,128,512]{2,1,0:T(8,128)}, s32[16]{0:T(128)S(1)}, ...), condition=%wide.region_10.11_spmd, body=%wide.region_9.10_spmd.sunk | while | flops 402653184 | bytes 1574023 | solution.py:96
  553.4 2.4 fusion.42
  558.2 2.4 fusion.42
  563.0 2.4 fusion.42
  567.8 2.4 fusion.42
  572.6 2.4 fusion.42
  577.5 2.4 fusion.42
  582.3 2.4 fusion.42
  587.1 2.4 fusion.42
  591.9 2.4 fusion.42
  596.8 2.4 fusion.42
  601.6 2.4 fusion.42
  606.4 2.4 fusion.42
  611.3 2.4 fusion.42
  616.1 2.4 fusion.42
  620.9 2.4 fusion.42
  625.7 2.4 fusion.42
  628.1 3.0 bitcast_reduce_fusion
  631.1 1.9 copy.11
  633.0 59.0 %reduce-scatter.2.cloned.1.call-done = f32[1024,32]{0,1:T(8,128)} async-done(((f32[1024,512]{0,1:T(8,128)}), f32[1024,32]{0,1:T(8,128)}) %reduce-scatter.2.cloned.1.call-update) | async-done | bytes 131088 | tf_op jit(solution)/shard_map/reduce_scatter | solution.py:99
  (100 shorter events, 42.2 us)
Async XLA Ops:
  6.5 1.6 copy-start
  34.3 8.8 %copy-start.4 = (f32[1024,512]{1,0:T(8,128)S(1)}, f32[1024,512]{1,0:T(8,128)}, u32[]{:S(2)}) copy-start(f32[1024,512]{1,0:T(8,128)} %param.10) | copy-start | bytes 6291460
  34.3 24.6 %copy-start.2 = (s32[128]{0:T(128)S(1)}, s32[128]{0:T(128)}, u32[]{:S(2)}) copy-start(s32[128]{0:T(128)} %param.13) | copy-start | bytes 1540
  34.3 372.7 %all-to-all-start = ((f32[16,2,128,1024]{3,2,1,0:T(8,128)}), f32[16,2,128,1024]{3,2,1,0:T(8,128)}, u32[]{:S(2)}, u32[]{:S(2)}) async-start(f32[16,2,128,1024]{3,2,1,0:T(8,128)} %select_select_fusion), calls=%async_computation | async-start | bytes 33554432 | tf_op jit(solution)/shard_map/all_to_all | solution.py:77
  43.0 649.0 %reduce-scatter.2.cloned.1.call-start = ((), (), s32[]{:S(2)}) async-start(), calls=%async_computation.2 | async-start | bytes 2228224 | tf_op jit(solution)/shard_map/reduce_scatter | solution.py:99
  43.1 52.0 %collective-permute-start = (f32[1024,512]{1,0:T(8,128)S(1)}, f32[1024,512]{1,0:T(8,128)}, u32[]{:S(2)}, u32[]{:S(2)}) collective-permute-start(f32[1024,512]{1,0:T(8,128)S(1)} %copy-done.4), channel_id=1, source_target_pairs={{0,2},{1,3},{2,4},{3,5},{4,6},{5,7},{6,8},{7,9},{8,10},{9,11},{10,... | collective-permute-start | bytes 6291464 | tf_op jit(solution)/shard_map/ppermute | solution.py:21
  47.4 91.4 %collective-permute-start.1 = (f32[1024,512]{1,0:T(8,128)S(1)}, f32[1024,512]{1,0:T(8,128)}, u32[]{:S(2)}, u32[]{:S(2)}) collective-permute-start(f32[1024,512]{1,0:T(8,128)S(1)} %copy-done.4), channel_id=1, source_target_pairs={{0,1},{1,2},{2,3},{3,4},{4,5},{5,6},{6,7},{7,8},{8,9},{9,10},{10,1... | collective-permute-start | bytes 6291464 | tf_op jit(solution)/shard_map/ppermute | solution.py:21
  51.5 92.0 %collective-permute-start.2 = (f32[1024,512]{1,0:T(8,128)S(1)}, f32[1024,512]{1,0:T(8,128)}, u32[]{:S(2)}, u32[]{:S(2)}) collective-permute-start(f32[1024,512]{1,0:T(8,128)S(1)} %copy-done.4), channel_id=1, source_target_pairs={{1,0},{2,1},{3,2},{4,3},{5,4},{6,5},{7,6},{8,7},{9,8},{10,9},{11,1... | collective-permute-start | bytes 6291464 | tf_op jit(solution)/shard_map/ppermute | solution.py:21
  53.4 132.1 %collective-permute-start.3 = (f32[1024,512]{1,0:T(8,128)S(1)}, f32[1024,512]{1,0:T(8,128)}, u32[]{:S(2)}, u32[]{:S(2)}) collective-permute-start(f32[1024,512]{1,0:T(8,128)S(1)} %copy-done.4), channel_id=1, source_target_pairs={{2,0},{3,1},{4,2},{5,3},{6,4},{7,5},{8,6},{9,7},{10,8},{11,9},{12,... | collective-permute-start | bytes 6291464 | tf_op jit(solution)/shard_map/ppermute | solution.py:21
  548.4 2.5 copy-start.3
  628.1 63.9 %copy-start.1 = (s32[32]{0:T(128)S(1)}, s32[32]{0:T(128)}, u32[]{:S(2)}) copy-start(s32[32]{0:T(128)} %param.14) | copy-start | bytes 388
Sparse Core Ops, SparseCore 0:
  633.1 58.8 reduce-scatter.1
where the time goes:
time: 702 us; the launch traced here: 699 us
  waiting for transfers between devices  389 us (55%)
  matrix products  103 us (15%)
  local copies, waits for them, and re-layouts  77.6 us (11%)
  loops' own time  62.2 us (9%)
  other arithmetic  28.6 us (4%)
  starting transfers between devices  24.6 us (4%)
  between operations  14.2 us (2%)
    all_to_all x1, waiting for transfers between devices, on_device(): lax.all_to_all(jnp.where(filled[:, :, None, None], packed, 0.0), 'bulk',...  218 us
    ppermute x4, waiting for transfers between devices, from_behind(): lax.ppermute(value, axis, [(source, source + steps) for source in range(i...  111 us
    dot_general x16, matrix products, contract_left(): jnp.dot(env_block, window, precision=precise, preferred_element_type=jnp....  64.8 us
    reduce_scatter x1, waiting for transfers between devices, on_device(): return lax.psum_scatter(summed, 'bulk', scatter_dimension=1, tiled=True)  59 us
    dot_general x16, matrix products, contract_right(): jnp.dot(left_part, right_env[term_index], precision=precise, preferred_el...  38.1 us
    another operation x1, loops' own time, on_device(): left_parts = lax.map(contract_left, (blocks, first_row, live_rows))  32.5 us
    dynamic_slice x48, local copies, waits for them, and re-layouts, on_device(): left_parts = lax.map(contract_left, (blocks, first_row, live_rows))  30.2 us
    another operation x1, loops' own time, on_device(): term_parts = lax.map(contract_right, (left_parts, term_local))  29.7 us
  transfers between devices with their start and end apart: 6, of which 5 were waited for; matrix products, arithmetic and copies ran while one was open for 3% of the time, Pallas kernels for 0%

commit v1 on v0

v1 whole, which is shorter than its diff:
```python
import jax
import jax.numpy as jnp
from jax import lax
from jax.experimental import pallas as pl
from jax.experimental.pallas import tpu as pltpu
from jax.sharding import Mesh, PartitionSpec as P

TILE = 128
COLS = 512
HALF = COLS // 2
TILE_DEV = 8
SRC = 1024
PAIRS = 16
HOMES = 16
REACH = 2
SLABS = 2 * REACH + 1
ROWS = TILE_DEV * TILE
PART = ROWS // HOMES
SUB = 32
VMEM = 56 * 1024 * 1024

START, COUNT, TERM, CORE, PX, PY = 0, 16, 32, 48, 49, 50


def split(value):
    high = value.astype(jnp.bfloat16)
    low = (value - high.astype(jnp.float32)).astype(jnp.bfloat16)
    return high, low


def product(left, high, low):
    left_high, left_low = split(left)
    rows = left.shape[0]
    both = jnp.dot(
        jnp.concatenate([left_high, left_low], axis=0), high, preferred_element_type=jnp.float32
    )
    rest = jnp.dot(left_high, low, preferred_element_type=jnp.float32)
    return both[:rows] + both[rows:] + rest


def left_kernel(plan, own, near, env_own, env_other, out, high, low):
    pair = pl.program_id(0)

    @pl.when(pair == 0)
    def _():
        def put(row, value):
            spot = pl.ds(pl.multiple_of(row, PART), PART)
            high[spot, :], low[spot, :] = split(value)

        @pl.loop(0, HOMES)
        def _(home):
            for at, slab in enumerate(s for s in range(SLABS) if s != REACH):
                put(slab * ROWS + home * PART, near[home, at])
            put(REACH * ROWS + home * PART, own[pl.ds(pl.multiple_of(home * PART, PART), PART), :])

        tail = jnp.zeros((2 * TILE, COLS), jnp.bfloat16)
        high[SLABS * ROWS :, :] = tail
        low[SLABS * ROWS :, :] = tail

    def contract(env):
        first, count = plan[START + pair], plan[COUNT + pair]
        out[0] = jnp.zeros((TILE, COLS), jnp.float32)

        def chunk(step, carry):
            block = env[0, :, pl.ds(pl.multiple_of(step * 2 * TILE, 2 * TILE), 2 * TILE)]
            column = step * 2 * TILE + lax.broadcasted_iota(jnp.int32, block.shape, 1)
            block = jnp.where(column < count * TILE, block, 0.0)
            spot = pl.ds(pl.multiple_of((first + 2 * step) * TILE, TILE), 2 * TILE)
            out[0] += product(block, high[spot, :], low[spot, :])
            return carry

        lax.fori_loop(0, (count + 1) // 2, chunk, 0)

    @pl.when(pair % 2 == 0)
    def _():
        contract(env_own)

    @pl.when(pair % 2 == 1)
    def _():
        contract(env_other)


def left_products(plan, own, near, env, env_other):
    grid = pltpu.PrefetchScalarGridSpec(
        num_scalar_prefetch=1,
        grid=(PAIRS,),
        in_specs=[
            pl.BlockSpec((ROWS, COLS), lambda p, plan: (0, 0), pipeline_mode=pl.Buffered(1)),
            pl.BlockSpec(near.shape, lambda p, plan: (0, 0, 0, 0), pipeline_mode=pl.Buffered(1)),
            pl.BlockSpec((1, TILE, SRC), lambda p, plan: ((p // 2) * 2 + plan[CORE], 0, 0)),
            pl.BlockSpec((1, TILE, SRC), lambda p, plan: (p // 2, 0, 0)),
        ],
        out_specs=pl.BlockSpec((1, TILE, COLS), lambda p, plan: (p, 0, 0)),
        scratch_shapes=[pltpu.VMEM((SLABS * ROWS + 2 * TILE, COLS), jnp.bfloat16)] * 2,
    )
    return pl.pallas_call(
        left_kernel,
        grid_spec=grid,
        out_shape=jax.ShapeDtypeStruct((PAIRS, TILE, COLS), jnp.float32),
        compiler_params=pltpu.CompilerParams(vmem_limit_bytes=VMEM),
        cost_estimate=pl.CostEstimate(
            flops=6 * PAIRS * TILE * SRC * COLS, bytes_accessed=24 << 20, transcendentals=0
        ),
        name="left_products",
    )(plan, own, near, env, env_other)


def right_kernel(plan, left, *refs):
    parts, (keep, send, total, *halves) = refs[:10], refs[10:]
    pair = pl.program_id(0)
    core, x, y = plan[CORE], plan[PX], plan[PY]
    value = []
    for half, (major, minor) in enumerate(((y, x), (x, y))):
        here, after, across_low, across_high, before = parts[5 * half : 5 * half + 5]
        high, low = halves[2 * half : 2 * half + 2]
        pieces = [
            [here.at[i] for i in range(4)],
            [after.at[i] for i in range(4)],
            [across_low.at[0], across_low.at[1], across_high.at[0], across_high.at[1]],
            [before.at[i] for i in range(4)],
        ]
        lefts = []
        for r in range(4):
            for i in range(4):
                spot = pl.ds(pl.multiple_of(r * TILE + ((minor + i) % 4) * SUB, SUB), SUB)
                high[spot, :], low[spot, :] = split(pieces[r][i][0])
            lefts.append(left[0, :, pl.ds(pl.multiple_of(((major + r) % 4) * TILE, TILE), TILE)])
        value.append(product(jnp.concatenate(lefts, axis=1), high[...], low[...]))
    value = jnp.concatenate(value, axis=1)

    @pl.when(pair % 2 == 0)
    def _():
        total[...] = value

    @pl.when(pair % 2 == 1)
    def _():
        turned = (total[...] + value).T.reshape(HOMES // 2, 2, SUB, TILE)
        keep[...] = jnp.where(core == 0, turned[:, 0], turned[:, 1])
        send[...] = jnp.where(core == 0, turned[:, 1], turned[:, 0])


def right_products(plan, left, parts):
    def part_spec(part):
        return pl.BlockSpec((part.shape[0], 1, SUB, HALF), lambda p, plan: (0, plan[TERM + p], 0, 0))

    out = jax.ShapeDtypeStruct((HOMES // 2, SUB, ROWS), jnp.float32)
    out_spec = pl.BlockSpec((HOMES // 2, SUB, TILE), lambda p, plan: (0, 0, p // 2))
    grid = pltpu.PrefetchScalarGridSpec(
        num_scalar_prefetch=1,
        grid=(PAIRS,),
        in_specs=[pl.BlockSpec((1, TILE, COLS), lambda p, plan: (p, 0, 0))]
        + [part_spec(part) for part in parts],
        out_specs=[out_spec, out_spec],
        scratch_shapes=[pltpu.VMEM((TILE, COLS), jnp.float32)]
        + [pltpu.VMEM((COLS, HALF), jnp.bfloat16)] * 4,
    )
    return pl.pallas_call(
        right_kernel,
        grid_spec=grid,
        out_shape=[out, out],
        compiler_params=pltpu.CompilerParams(vmem_limit_bytes=VMEM),
        cost_estimate=pl.CostEstimate(
            flops=6 * PAIRS * TILE * COLS * COLS, bytes_accessed=22 << 20, transcendentals=0
        ),
        name="right_products",
    )(plan, left, *parts)


def ring(value, axis, steps):
    count = lax.axis_size(axis)
    return lax.ppermute(value, axis, [(i, (i - steps) % count) for i in range(count)])


def around(value, axis, cut):
    after, before = ring(value, axis, 1), ring(value, axis, -1)
    low = ring(lax.slice_in_dim(after, 0, cut), axis, 1)
    high = ring(lax.slice_in_dim(before, cut, value.shape[0]), axis, -1)
    return value, after, low, high, before


def wide_shift(value, steps):
    count = lax.axis_size(("y", "x"))
    return lax.ppermute(
        value, ("y", "x"), [(i, i + steps) for i in range(max(0, -steps), min(count, count - steps))]
    )


def make_plan(tile_sector, term_charge, block_home, home, core, x, y):
    base = (y * 4 + x) * TILE_DEV
    paired = block_home.reshape(HOMES, TILE_DEV, 2)
    mine = jnp.where(core == 0, paired[:, :, 0], paired[:, :, 1])
    homes = home + jnp.arange(2, dtype=jnp.int32) * (1 - 2 * core)
    owner_ids = jnp.arange(HOMES, dtype=jnp.int32)[:, None, None]
    owner = jnp.sum(
        jnp.where(mine[:, :, None] == homes[None, None, :], owner_ids, 0), axis=0
    ).reshape(PAIRS)
    term = owner * 2 + core
    term_ids = jnp.arange(2 * HOMES, dtype=jnp.int32)
    charge = jnp.sum(jnp.where(term[:, None] == term_ids[None, :], term_charge[None, :], 0), axis=1)
    tiles = lax.dynamic_slice(tile_sector, (base,), (TILE_DEV,))
    source = jnp.broadcast_to(tiles[:, None], (TILE_DEV, 2)).reshape(PAIRS) + charge
    usable = (source >= 0) & (source <= tile_sector[-1])
    first = jnp.sum((tile_sector[None, :] < source[:, None]).astype(jnp.int32), axis=1)
    count = jnp.sum((tile_sector[None, :] == source[:, None]).astype(jnp.int32), axis=1)
    first = jnp.where(usable, first - (base - REACH * TILE_DEV), 0)
    count = jnp.where(usable, count, 0)
    return jnp.concatenate([first, count, owner, jnp.stack([core, x, y])]).astype(jnp.int32)


def on_device(wavefunction, env_blocks, right_env, tile_sector, term_charge, block_home):
    z, core = lax.axis_index("z"), lax.axis_index("core")
    y, x = lax.axis_index("y"), lax.axis_index("x")
    home = 2 * z + core
    swap = [(0, 1), (1, 0)]

    by_y = lax.dynamic_slice(right_env, (0, y * TILE + x * SUB, 0), (2, SUB, HALF))
    by_x = lax.dynamic_slice(right_env, (0, x * TILE + y * SUB, HALF), (2, SUB, HALF))
    column = lax.all_gather(jnp.stack([by_y, by_x], axis=1), ("z", "core"))

    strip = lax.dynamic_slice(wavefunction, (home * PART, 0), (PART, COLS))
    near = jnp.stack([wide_shift(strip, steps) for steps in (2, 1, -1, -2)])
    near = lax.all_gather(near, ("z", "core"))

    paired = env_blocks.reshape(TILE_DEV, 2, TILE, SRC)
    env_other = lax.ppermute(
        lax.dynamic_index_in_dim(paired, 1 - core, axis=1, keepdims=False), "core", swap
    )
    plan = make_plan(tile_sector, term_charge, block_home, home, core, x, y)

    mine = lax.dynamic_index_in_dim(column, core, axis=1, keepdims=False)
    parts = []
    for at, (first, then) in enumerate((("x", "y"), ("y", "x"))):
        here, after, low, high, before = around(mine[:, at], first, HOMES // 2)
        gathered = jnp.stack([here, after, jnp.concatenate([low, high], axis=0), before])
        parts += around(gathered, then, 2)

    left = left_products(plan, wavefunction, near, env_blocks, env_other)
    keep, send = right_products(plan, left, parts)
    total = keep + lax.ppermute(send, "core", swap)
    shares = lax.all_to_all(total, "z", split_axis=0, concat_axis=0, tiled=True)
    shares = shares.reshape(HOMES // 2, SUB, ROWS)
    return jnp.sum(shares, axis=0).T


def solution(mesh):
    fine = Mesh(mesh.devices.reshape(8, 2, 4, 4), ("z", "core", "y", "x"))
    bulk, wide = ("z", "core"), ("y", "x")
    return jax.shard_map(
        on_device,
        mesh=fine,
        in_specs=(P(wide, None), P(bulk, wide, None), P(bulk, None, None), P(), P(), P()),
        out_specs=P(wide, bulk),
        check_vma=False,
    )
```

time: 702 us -> 235 us (0.33)
  waiting for transfers between devices: 389 us -> 77.1 us
  matrix products: 103 us -> 0 us
  loops' own time: 62.2 us -> 0 us
  local copies, waits for them, and re-layouts: 77.6 us -> 20.6 us
  Pallas kernels: 0 us -> 41 us
  blocking collectives: 0 us -> 35.2 us
  other arithmetic: 28.6 us -> 6.57 us
  starting transfers between devices: 24.6 us -> 38 us
    all_to_all x1 -> x0, waiting for transfers between devices: 218 us -> none  [on_device(): lax.all_to_all(jnp.where(filled[:, :, None, None], packed, 0.0), 'bulk',...]
    dot_general x32 -> x0, matrix products: 103 us -> none  [the longest x16 64.8 us: contract_left(): jnp.dot(env_block, window, precision=precise, preferred_element_type=jnp....]
    another operation x2 -> x0, loops' own time: 62.2 us -> none  [the longest x1 32.5 us: on_device(): left_parts = lax.map(contract_left, (blocks, first_row, live_rows))]
    reduce_scatter x1 -> x0, waiting for transfers between devices: 59 us -> none  [on_device(): return lax.psum_scatter(summed, 'bulk', scatter_dimension=1, tiled=True)]
    ppermute x4 -> x22, waiting for transfers between devices: 111 us -> 59.7 us  [the longest x16 51.3 us: ring(): lax.ppermute(value, axis, [(i, (i - steps) % count) for i in range(count)])]
    pallas_call x0 -> x2, Pallas kernels: none -> 41 us  [the longest x1 22.2 us: left_products(): pl.pallas_call(left_kernel, grid_spec=grid, out_shape=jax.ShapeDtypeStruc...]
    all_to_all x0 -> x1, blocking collectives: none -> 35.2 us  [on_device(): shares = lax.all_to_all(total, 'z', split_axis=0, concat_axis=0, tiled=True)]
    dynamic_slice x48 -> x2, local copies, waits for them, and re-layouts: 30.2 us -> 0.99 us  [the longest x1 0.92 us: on_device(): strip = lax.dynamic_slice(wavefunction, (home * PART, 0), (PART, COLS))]
  transfers between devices with their start and end apart: 6 -> 24, of which waited for: 5 -> 9; matrix products, arithmetic and copies ran while one was open for 3% -> 9% of each run, Pallas kernels for 0% -> 10%
where the time goes in v1:
time: 235 us; the launch traced here: 232 us
  waiting for transfers between devices  77.1 us (33%)
  Pallas kernels  41 us (17%)
  starting transfers between devices  38 us (16%)
  blocking collectives  35.2 us (15%)
  local copies, waits for them, and re-layouts  20.6 us (9%)
  between operations  13.7 us (6%)
  other arithmetic  6.57 us (3%)
    ppermute x16, waiting for transfers between devices, ring(): lax.ppermute(value, axis, [(i, (i - steps) % count) for i in range(count)])  51.3 us
    all_to_all x1, blocking collectives, on_device(): shares = lax.all_to_all(total, 'z', split_axis=0, concat_axis=0, tiled=True)  35.2 us
    ppermute x16, starting transfers between devices, ring(): lax.ppermute(value, axis, [(i, (i - steps) % count) for i in range(count)])  23.8 us
    pallas_call x1, Pallas kernels, left_products(): pl.pallas_call(left_kernel, grid_spec=grid, out_shape=jax.ShapeDtypeStruc...  22.2 us
    pallas_call x1, Pallas kernels, right_products(): pl.pallas_call(right_kernel, grid_spec=grid, out_shape=[out, out], compil...  18.8 us
    all_gather x1, waiting for transfers between devices, on_device(): column = lax.all_gather(jnp.stack([by_y, by_x], axis=1), ('z', 'core'))  17.4 us
    ppermute x4, starting transfers between devices, wide_shift(): lax.ppermute(value, ('y', 'x'), [(i, i + steps) for i in range(max(0, -st...  14.1 us
    ppermute x4, waiting for transfers between devices, wide_shift(): lax.ppermute(value, ('y', 'x'), [(i, i + steps) for i in range(max(0, -st...  5.52 us
  transfers between devices with their start and end apart: 24, of which 9 were waited for; matrix products, arithmetic and copies ran while one was open for 9% of the time, Pallas kernels for 10%

profile of v1, /device:TPU:6, one launch (start us, length us, event | category | flops | bytes accessed | tf_op | source)
XLA Modules:
  0.0 232.3 jit_solution(8984564428941303815)
XLA Ops:
  6.5 0.9 dynamic-slice_bitcast_fusion.2
  7.4 0.7 pad_maximum_fusion.3
  8.1 0.0 all-gather.7.cloned.1.call-update
  8.1 0.0 all-gather.5.cloned.1.call-start
  8.2 0.9 constant_dynamic-slice_fusion
  9.1 3.3 %collective-permute-start.3 = (f32[64,512]{1,0:T(8,128)S(1)}, f32[64,512]{1,0:T(8,128)S(1)}, u32[]{:S(2)}, u32[]{:S(2)}) collective-permute-start(f32[64,512]{1,0:T(8,128)S(1)} %constant_dynamic-slice_fusion), channel_id=1, source_target_pairs={{2,0},{3,1},{4,2},{5,3},{6,4},{7,5},{8,6},{9,7},{10,8},{11,9},{12,... | collective-permute-start | bytes 393224 | tf_op jit(solution)/shard_map/ppermute | solution.py:183
  12.4 3.6 %collective-permute-start.2 = (f32[64,512]{1,0:T(8,128)S(1)}, f32[64,512]{1,0:T(8,128)S(1)}, u32[]{:S(2)}, u32[]{:S(2)}) collective-permute-start(f32[64,512]{1,0:T(8,128)S(1)} %constant_dynamic-slice_fusion), channel_id=1, source_target_pairs={{1,0},{2,1},{3,2},{4,3},{5,4},{6,5},{7,6},{8,7},{9,8},{10,9},{11,1... | collective-permute-start | bytes 393224 | tf_op jit(solution)/shard_map/ppermute | solution.py:183
  16.0 4.4 %collective-permute-start.1 = (f32[64,512]{1,0:T(8,128)S(1)}, f32[64,512]{1,0:T(8,128)S(1)}, u32[]{:S(2)}, u32[]{:S(2)}) collective-permute-start(f32[64,512]{1,0:T(8,128)S(1)} %constant_dynamic-slice_fusion), channel_id=1, source_target_pairs={{0,1},{1,2},{2,3},{3,4},{4,5},{5,6},{6,7},{7,8},{8,9},{9,10},{10,1... | collective-permute-start | bytes 393224 | tf_op jit(solution)/shard_map/ppermute | solution.py:183
  20.4 2.8 %collective-permute-start = (f32[64,512]{1,0:T(8,128)S(1)}, f32[64,512]{1,0:T(8,128)S(1)}, u32[]{:S(2)}, u32[]{:S(2)}) collective-permute-start(f32[64,512]{1,0:T(8,128)S(1)} %constant_dynamic-slice_fusion), channel_id=1, source_target_pairs={{0,2},{1,3},{2,4},{3,5},{4,6},{5,7},{6,8},{7,9},{8,10},{9,11},{10,... | collective-permute-start | bytes 393224 | tf_op jit(solution)/shard_map/ppermute | solution.py:183
  23.2 1.1 collective-permute-done.1
  24.3 4.5 %collective-permute-done = f32[64,512]{1,0:T(8,128)S(1)} collective-permute-done((f32[64,512]{1,0:T(8,128)S(1)}, f32[64,512]{1,0:T(8,128)S(1)}, u32[]{:S(2)}, u32[]{:S(2)}) %collective-permute-start) | collective-permute-done | bytes 131104 | tf_op jit(solution)/shard_map/ppermute | solution.py:183
  28.7 0.8 pad_maximum_fusion.2
  29.6 0.0 all-gather.5.cloned.1.call-update
  29.6 4.7 %dynamic-slice_bitcast_fusion = f32[8,128,1024]{2,1,0:T(8,128)} fusion(f32[8,2,128,1024]{3,2,1,0:T(8,128)} %bitcast.40, s32[]{:T(128)S(6)} %select_n.52), kind=kLoop, calls=%fused_computation | loop fusion | bytes 8388612 | tf_op jit(solution)/shard_map/jit(dynamic_index_in_dim)/squeeze | solution.py:226
  34.3 17.4 %all-gather.7.cloned.1.call-done = f32[32,2,32,256]{3,2,1,0:T(8,128)} async-done(((f32[2,2,32,256]{3,2,1,0:T(8,128)}), f32[32,2,32,256]{3,2,1,0:T(8,128)}) %all-gather.7.cloned.1.call-update) | async-done | bytes 2097168 | tf_op jit(solution)/shard_map/all_gather | solution.py:218
  51.7 1.3 copy_bitcast_fusion
  53.0 0.1 slice_bitcast_fusion.1
  53.2 0.8 collective-permute-start.7
  53.9 1.3 collective-permute-start.5
  55.3 1.5 collective-permute-start.15
  56.8 1.8 collective-permute-start.13
  58.5 8.8 %collective-permute-done.7 = f32[16,32,256]{2,1,0:T(8,128)S(1)} collective-permute-done((f32[16,32,256]{2,1,0:T(8,128)S(1)}, f32[16,32,256]{2,1,0:T(8,128)S(1)}, u32[]{:S(2)}, u32[]{:S(2)}) %collective-permute-start.7) | collective-permute-done | bytes 524320 | tf_op jit(solution)/shard_map/ppermute | solution.py:171
  67.4 2.0 collective-permute-start.8
  69.4 0.2 collective-permute-start.6
  69.6 0.4 collective-permute-done.15
  70.0 1.1 collective-permute-start.16
  71.2 2.3 collective-permute-start.14
  73.5 1.7 collective-permute-done.8
  75.2 2.9 %collective-permute-done.6 = f32[8,32,256]{2,1,0:T(8,128)S(1)} collective-permute-done((f32[8,32,256]{2,1,0:T(8,128)S(1)}, f32[8,32,256]{2,1,0:T(8,128)S(1)}, u32[]{:S(2)}, u32[]{:S(2)}) %collective-permute-start.6) | collective-permute-done | bytes 262176 | tf_op jit(solution)/shard_map/ppermute | solution.py:171
  78.2 0.1 pad_maximum_fusion.refs_0_
  78.3 2.6 %collective-permute-start.9 = (f32[4,16,32,256]{3,2,1,0:T(8,128)S(1)}, f32[4,16,32,256]{3,2,1,0:T(8,128)}, u32[]{:S(2)}, u32[]{:S(2)}) collective-permute-start(f32[4,16,32,256]{3,2,1,0:T(8,128)S(1)} %pad_maximum_fusion.refs_0_), channel_id=1, source_target_pairs={{0,12},{4,0},{8,4},{12,8},{1,13},{5,1},{9,5},{13,9},{2,14},{6,2},{... | collective-permute-start | bytes 6291464 | tf_op jit(solution)/shard_map/ppermute | solution.py:171
  81.0 0.0 copy-start.5
  81.0 0.0 copy-start.4
  81.1 1.5 pad_maximum_fusion.1.refs_5_
  82.6 3.2 %collective-permute-start.19 = (f32[4,16,32,256]{3,2,1,0:T(8,128)}, f32[4,16,32,256]{3,2,1,0:T(8,128)}, u32[]{:S(2)}, u32[]{:S(2)}) collective-permute-start(f32[4,16,32,256]{3,2,1,0:T(8,128)} %pad_maximum_fusion.1.refs_5_), channel_id=1, source_target_pairs={{0,1},{1,2},{2,3},{3,0},{4,5},{5,6},{6,7},{7,4},{8,9},{9,10},{10,1... | collective-permute-start | bytes 6291464 | tf_op jit(solution)/shard_map/ppermute | solution.py:171
  85.8 0.6 slice.41
  86.4 0.1 dynamic_slice.20
  86.5 0.1 broadcast_in_dim.28
  86.5 0.1 reshape.33
  86.6 0.1 copy.17
  86.7 0.2 select_reduce_fusion.1
  86.9 0.1 copy.18
  87.0 0.1 reshape.35
  87.1 37.4 %collective-permute-done.9.refs_1_ = f32[4,16,32,256]{3,2,1,0:T(8,128)} collective-permute-done((f32[4,16,32,256]{3,2,1,0:T(8,128)S(1)}, f32[4,16,32,256]{3,2,1,0:T(8,128)}, u32[]{:S(2)}, u32[]{:S(2)}) %collective-permute-start.9) | collective-permute-done | bytes 2097184 | tf_op jit(solution)/shard_map/ppermute | solution.py:171
  124.5 2.3 %slice.57 = f32[2,16,32,256]{3,2,1,0:T(8,128)} slice(f32[4,16,32,256]{3,2,1,0:T(8,128)} %collective-permute-done.9.refs_1_), slice={[0:2], [0:16], [0:32], [0:256]} | slice | bytes 2097152 | tf_op jit(solution)/shard_map/slice | solution.py:176
  126.8 3.8 %collective-permute-start.10 = (f32[2,16,32,256]{3,2,1,0:T(8,128)}, f32[2,16,32,256]{3,2,1,0:T(8,128)S(1)}, u32[]{:S(2)}, u32[]{:S(2)}) collective-permute-start(f32[2,16,32,256]{3,2,1,0:T(8,128)} %slice.57), channel_id=1, source_target_pairs={{0,12},{4,0},{8,4},{12,8},{1,13},{5,1},{9,5},{13,9},{2,14},{6,2},{... | collective-permute-start | bytes 3145736 | tf_op jit(solution)/shard_map/ppermute | solution.py:171
  130.6 2.3 %slice.58 = f32[2,16,32,256]{3,2,1,0:T(8,128)} slice(f32[4,16,32,256]{3,2,1,0:T(8,128)} %collective-permute-done.11.refs_4_), slice={[2:4], [0:16], [0:32], [0:256]} | slice | bytes 2097152 | tf_op jit(solution)/shard_map/slice | solution.py:177
  133.0 2.3 %slice.62 = f32[2,16,32,256]{3,2,1,0:T(8,128)} slice(f32[4,16,32,256]{3,2,1,0:T(8,128)} %collective-permute-done.17.refs_6_), slice={[0:2], [0:16], [0:32], [0:256]} | slice | bytes 2097152 | tf_op jit(solution)/shard_map/slice | solution.py:176
  135.3 2.3 slice.63
  137.6 3.2 %collective-permute-start.20 = (f32[2,16,32,256]{3,2,1,0:T(8,128)}, f32[2,16,32,256]{3,2,1,0:T(8,128)}, u32[]{:S(2)}, u32[]{:S(2)}) collective-permute-start(f32[2,16,32,256]{3,2,1,0:T(8,128)} %slice.63), channel_id=1, source_target_pairs={{0,1},{1,2},{2,3},{3,0},{4,5},{5,6},{6,7},{7,4},{8,9},{9,10},{10,1... | collective-permute-start | bytes 3145736 | tf_op jit(solution)/shard_map/ppermute | solution.py:171
  140.9 0.2 select_reduce_fusion
  141.1 0.2 convert_reduce_fusion
  141.2 0.7 broadcast_select_fusion.1
  141.9 0.6 concatenate.9.plan
  142.5 22.2 %left_products.1.left = f32[16,128,512]{2,1,0:T(8,128)} custom-call(s32[51]{0:T(128)} %concatenate.9.plan, f32[1024,512]{1,0:T(8,128)} %own.1, f32[16,4,64,512]{3,2,1,0:T(8,128)} %bitcast.41, f32[16,128,1024]{2,1,0:T(8,128)} %env_own.1, f32[8,128,1024]{2,1,0:T(8,128)} %collective-permute-done.4.env_other), custom_call_target="tpu_custom_call" | custom-call | flops 6442450944 | bytes 25165824 | tf_op jit(solution)/shard_map/left_products/pallas_call | solution.py:96
  164.7 0.9 copy-done.1
  165.7 0.3 copy-done.2
  166.0 0.3 copy-done.3
  166.3 18.8 %right_products.1 = (f32[8,32,1024]{2,1,0:T(8,128)}, f32[8,32,1024]{2,1,0:T(8,128)}) custom-call(s32[51]{0:T(128)} %concatenate.9.plan, f32[16,128,512]{2,1,0:T(8,128)} %left_products.1.left, f32[4,16,32,256]{3,2,1,0:T(8,128)} %copy-done, f32[4,16,32,256]{3,2,1,0:T(8,128)} %collective-permute-done.9.refs_1_, f32[2,16,32,256]{3,2,1,0:T(8,128)} %copy-done.1, ...), custom_call_target="tpu_custom_call" | custom-call | flops 3221225472 | bytes 23068672 | tf_op jit(solution)/shard_map/right_products/pallas_call | solution.py:157
  185.1 0.1 collective-permute-start.21
  185.2 2.9 %collective-permute-done.21 = f32[8,32,1024]{2,1,0:T(8,128)S(1)} collective-permute-done((f32[8,32,1024]{2,1,0:T(8,128)}, f32[8,32,1024]{2,1,0:T(8,128)S(1)}, u32[]{:S(2)}, u32[]{:S(2)}) %collective-permute-start.21) | collective-permute-done | bytes 1048608 | tf_op jit(solution)/shard_map/ppermute | solution.py:239
  188.1 1.4 add.79
  189.5 35.2 %all_to_all.5 = f32[8,32,1024]{2,1,0:T(8,128)S(1)} all-to-all(f32[8,32,1024]{2,1,0:T(8,128)S(1)} %add.79), channel_id=1, replica_groups=mesh['z'=8,'core'=2,'y'=4,'x'=4] {'z'}, dimensions={0} | all-to-all | bytes 2097152 | tf_op jit(solution)/shard_map/all_to_all | solution.py:240
  224.7 0.7 reduce_sum.49
  (40 shorter events, 0.2 us)
Async XLA Ops:
  6.5 45.2 %all-gather.7.cloned.1.call-start = ((), (), s32[]{:S(2)}) async-start(), calls=%async_computation.2 | async-start | bytes 2228224 | tf_op jit(solution)/shard_map/all_gather | solution.py:218
  8.1 134.4 %all-gather.5.cloned.1.call-start = ((), (), s32[]{:S(2)}) async-start(), calls=%async_computation.1 | async-start | bytes 8912896 | tf_op jit(solution)/shard_map/all_gather | solution.py:222
  9.1 14.1 %collective-permute-start.3 = (f32[64,512]{1,0:T(8,128)S(1)}, f32[64,512]{1,0:T(8,128)S(1)}, u32[]{:S(2)}, u32[]{:S(2)}) collective-permute-start(f32[64,512]{1,0:T(8,128)S(1)} %constant_dynamic-slice_fusion), channel_id=1, source_target_pairs={{2,0},{3,1},{4,2},{5,3},{6,4},{7,5},{8,6},{9,7},{10,8},{11,9},{12,... | collective-permute-start | bytes 393224 | tf_op jit(solution)/shard_map/ppermute | solution.py:183
  12.4 10.8 %collective-permute-start.2 = (f32[64,512]{1,0:T(8,128)S(1)}, f32[64,512]{1,0:T(8,128)S(1)}, u32[]{:S(2)}, u32[]{:S(2)}) collective-permute-start(f32[64,512]{1,0:T(8,128)S(1)} %constant_dynamic-slice_fusion), channel_id=1, source_target_pairs={{1,0},{2,1},{3,2},{4,3},{5,4},{6,5},{7,6},{8,7},{9,8},{10,9},{11,1... | collective-permute-start | bytes 393224 | tf_op jit(solution)/shard_map/ppermute | solution.py:183
  16.0 8.3 %collective-permute-start.1 = (f32[64,512]{1,0:T(8,128)S(1)}, f32[64,512]{1,0:T(8,128)S(1)}, u32[]{:S(2)}, u32[]{:S(2)}) collective-permute-start(f32[64,512]{1,0:T(8,128)S(1)} %constant_dynamic-slice_fusion), channel_id=1, source_target_pairs={{0,1},{1,2},{2,3},{3,4},{4,5},{5,6},{6,7},{7,8},{8,9},{9,10},{10,1... | collective-permute-start | bytes 393224 | tf_op jit(solution)/shard_map/ppermute | solution.py:183
  20.4 8.4 %collective-permute-start = (f32[64,512]{1,0:T(8,128)S(1)}, f32[64,512]{1,0:T(8,128)S(1)}, u32[]{:S(2)}, u32[]{:S(2)}) collective-permute-start(f32[64,512]{1,0:T(8,128)S(1)} %constant_dynamic-slice_fusion), channel_id=1, source_target_pairs={{0,2},{1,3},{2,4},{3,5},{4,6},{5,7},{6,8},{7,9},{8,10},{9,11},{10,... | collective-permute-start | bytes 393224 | tf_op jit(solution)/shard_map/ppermute | solution.py:183
  34.3 108.2 %collective-permute-start.4 = (f32[8,128,1024]{2,1,0:T(8,128)}, f32[8,128,1024]{2,1,0:T(8,128)}, u32[]{:S(2)}, u32[]{:S(2)}) collective-permute-start(f32[8,128,1024]{2,1,0:T(8,128)} %dynamic-slice_bitcast_fusion), channel_id=1, source_target_pairs={{0,16},{16,0},{1,17},{17,1},{2,18},{18,2},{3,19},{19,3},{4,20},{20... | collective-permute-start | bytes 12582920 | tf_op jit(solution)/shard_map/ppermute | solution.py:225
  53.2 14.2 %collective-permute-start.7 = (f32[16,32,256]{2,1,0:T(8,128)S(1)}, f32[16,32,256]{2,1,0:T(8,128)S(1)}, u32[]{:S(2)}, u32[]{:S(2)}) collective-permute-start(f32[16,32,256]{2,1,0:T(8,128)S(1)} %get-tuple-element.14), channel_id=1, source_target_pairs={{0,1},{1,2},{2,3},{3,0},{4,5},{5,6},{6,7},{7,4},{8,9},{9,10},{10,1... | collective-permute-start | bytes 1572872 | tf_op jit(solution)/shard_map/ppermute | solution.py:171
  53.9 15.4 %collective-permute-start.5 = (f32[16,32,256]{2,1,0:T(8,128)S(1)}, f32[16,32,256]{2,1,0:T(8,128)S(1)}, u32[]{:S(2)}, u32[]{:S(2)}) collective-permute-start(f32[16,32,256]{2,1,0:T(8,128)S(1)} %get-tuple-element.14), channel_id=1, source_target_pairs={{0,3},{1,0},{2,1},{3,2},{4,7},{5,4},{6,5},{7,6},{8,11},{9,8},{10,9... | collective-permute-start | bytes 1572872 | tf_op jit(solution)/shard_map/ppermute | solution.py:171
  55.3 14.7 %collective-permute-start.15 = (f32[16,32,256]{2,1,0:T(8,128)S(1)}, f32[16,32,256]{2,1,0:T(8,128)S(1)}, u32[]{:S(2)}, u32[]{:S(2)}) collective-permute-start(f32[16,32,256]{2,1,0:T(8,128)S(1)} %get-tuple-element.15), channel_id=1, source_target_pairs={{0,4},{4,8},{8,12},{12,0},{1,5},{5,9},{9,13},{13,1},{2,6},{6,10},{... | collective-permute-start | bytes 1572872 | tf_op jit(solution)/shard_map/ppermute | solution.py:171
  56.8 14.4 %collective-permute-start.13 = (f32[16,32,256]{2,1,0:T(8,128)S(1)}, f32[16,32,256]{2,1,0:T(8,128)S(1)}, u32[]{:S(2)}, u32[]{:S(2)}) collective-permute-start(f32[16,32,256]{2,1,0:T(8,128)S(1)} %get-tuple-element.15), channel_id=1, source_target_pairs={{0,12},{4,0},{8,4},{12,8},{1,13},{5,1},{9,5},{13,9},{2,14},{6,2},{... | collective-permute-start | bytes 1572872 | tf_op jit(solution)/shard_map/ppermute | solution.py:171
  67.4 7.8 %collective-permute-start.8 = (f32[8,32,256]{2,1,0:T(8,128)S(1)}, f32[8,32,256]{2,1,0:T(8,128)S(1)}, u32[]{:S(2)}, u32[]{:S(2)}) collective-permute-start(f32[8,32,256]{2,1,0:T(8,128)S(1)} %slice.56), channel_id=1, source_target_pairs={{0,1},{1,2},{2,3},{3,0},{4,5},{5,6},{6,7},{7,4},{8,9},{9,10},{10,1... | collective-permute-start | bytes 786440 | tf_op jit(solution)/shard_map/ppermute | solution.py:171
  69.4 8.8 %collective-permute-start.6 = (f32[8,32,256]{2,1,0:T(8,128)S(1)}, f32[8,32,256]{2,1,0:T(8,128)S(1)}, u32[]{:S(2)}, u32[]{:S(2)}) collective-permute-start(f32[8,32,256]{2,1,0:T(8,128)S(1)} %slice.55), channel_id=1, source_target_pairs={{0,3},{1,0},{2,1},{3,2},{4,7},{5,4},{6,5},{7,6},{8,11},{9,8},{10,9... | collective-permute-start | bytes 786440 | tf_op jit(solution)/shard_map/ppermute | solution.py:171
  70.0 10.9 %collective-permute-start.16 = (f32[8,32,256]{2,1,0:T(8,128)S(1)}, f32[8,32,256]{2,1,0:T(8,128)S(1)}, u32[]{:S(2)}, u32[]{:S(2)}) collective-permute-start(f32[8,32,256]{2,1,0:T(8,128)S(1)} %slice.61), channel_id=1, source_target_pairs={{0,4},{4,8},{8,12},{12,0},{1,5},{5,9},{9,13},{13,1},{2,6},{6,10},{... | collective-permute-start | bytes 786440 | tf_op jit(solution)/shard_map/ppermute | solution.py:171
  71.2 9.8 %collective-permute-start.14 = (f32[8,32,256]{2,1,0:T(8,128)S(1)}, f32[8,32,256]{2,1,0:T(8,128)S(1)}, u32[]{:S(2)}, u32[]{:S(2)}) collective-permute-start(f32[8,32,256]{2,1,0:T(8,128)S(1)} %slice.60), channel_id=1, source_target_pairs={{0,12},{4,0},{8,4},{12,8},{1,13},{5,1},{9,5},{13,9},{2,14},{6,2},{... | collective-permute-start | bytes 786440 | tf_op jit(solution)/shard_map/ppermute | solution.py:171
  78.3 4.3 %copy-start = (f32[4,16,32,256]{3,2,1,0:T(8,128)}, f32[4,16,32,256]{3,2,1,0:T(8,128)S(1)}, u32[]{:S(2)}) copy-start(f32[4,16,32,256]{3,2,1,0:T(8,128)S(1)} %pad_maximum_fusion.refs_0_) | copy-start | bytes 6291460
  78.3 46.2 %collective-permute-start.9 = (f32[4,16,32,256]{3,2,1,0:T(8,128)S(1)}, f32[4,16,32,256]{3,2,1,0:T(8,128)}, u32[]{:S(2)}, u32[]{:S(2)}) collective-permute-start(f32[4,16,32,256]{3,2,1,0:T(8,128)S(1)} %pad_maximum_fusion.refs_0_), channel_id=1, source_target_pairs={{0,12},{4,0},{8,4},{12,8},{1,13},{5,1},{9,5},{13,9},{2,14},{6,2},{... | collective-permute-start | bytes 6291464 | tf_op jit(solution)/shard_map/ppermute | solution.py:171
  81.0 49.6 %collective-permute-start.11 = (f32[4,16,32,256]{3,2,1,0:T(8,128)S(1)}, f32[4,16,32,256]{3,2,1,0:T(8,128)}, u32[]{:S(2)}, u32[]{:S(2)}) collective-permute-start(f32[4,16,32,256]{3,2,1,0:T(8,128)S(1)} %pad_maximum_fusion.refs_0_), channel_id=1, source_target_pairs={{0,4},{4,8},{8,12},{12,0},{1,5},{5,9},{9,13},{13,1},{2,6},{6,10},{... | collective-permute-start | bytes 6291464 | tf_op jit(solution)/shard_map/ppermute | solution.py:171
  81.0 4.8 %copy-start.5 = (s32[128]{0:T(128)S(1)}, s32[128]{0:T(128)}, u32[]{:S(2)}) copy-start(s32[128]{0:T(128)} %param.9) | copy-start | bytes 1540
  81.0 5.6 %copy-start.4 = (s32[16,16]{1,0:T(8,128)S(1)}, s32[16,16]{1,0:T(8,128)}, u32[]{:S(2)}) copy-start(s32[16,16]{1,0:T(8,128)} %param.11) | copy-start | bytes 3076
  82.6 50.4 %collective-permute-start.17 = (f32[4,16,32,256]{3,2,1,0:T(8,128)}, f32[4,16,32,256]{3,2,1,0:T(8,128)}, u32[]{:S(2)}, u32[]{:S(2)}) collective-permute-start(f32[4,16,32,256]{3,2,1,0:T(8,128)} %pad_maximum_fusion.1.refs_5_), channel_id=1, source_target_pairs={{0,3},{1,0},{2,1},{3,2},{4,7},{5,4},{6,5},{7,6},{8,11},{9,8},{10,9... | collective-permute-start | bytes 6291464 | tf_op jit(solution)/shard_map/ppermute | solution.py:171
  82.6 52.7 %collective-permute-start.19 = (f32[4,16,32,256]{3,2,1,0:T(8,128)}, f32[4,16,32,256]{3,2,1,0:T(8,128)}, u32[]{:S(2)}, u32[]{:S(2)}) collective-permute-start(f32[4,16,32,256]{3,2,1,0:T(8,128)} %pad_maximum_fusion.1.refs_5_), channel_id=1, source_target_pairs={{0,1},{1,2},{2,3},{3,0},{4,5},{5,6},{6,7},{7,4},{8,9},{9,10},{10,1... | collective-permute-start | bytes 6291464 | tf_op jit(solution)/shard_map/ppermute | solution.py:171
  126.8 37.9 %collective-permute-start.10 = (f32[2,16,32,256]{3,2,1,0:T(8,128)}, f32[2,16,32,256]{3,2,1,0:T(8,128)S(1)}, u32[]{:S(2)}, u32[]{:S(2)}) collective-permute-start(f32[2,16,32,256]{3,2,1,0:T(8,128)} %slice.57), channel_id=1, source_target_pairs={{0,12},{4,0},{8,4},{12,8},{1,13},{5,1},{9,5},{13,9},{2,14},{6,2},{... | collective-permute-start | bytes 3145736 | tf_op jit(solution)/shard_map/ppermute | solution.py:171
  133.0 7.9 %copy-start.6 = (s32[32]{0:T(128)S(1)}, s32[32]{0:T(128)}, u32[]{:S(2)}) copy-start(s32[32]{0:T(128)} %param.10) | copy-start | bytes 388
  133.0 31.7 %collective-permute-start.12 = (f32[2,16,32,256]{3,2,1,0:T(8,128)}, f32[2,16,32,256]{3,2,1,0:T(8,128)S(1)}, u32[]{:S(2)}, u32[]{:S(2)}) collective-permute-start(f32[2,16,32,256]{3,2,1,0:T(8,128)} %slice.58), channel_id=1, source_target_pairs={{0,4},{4,8},{8,12},{12,0},{1,5},{5,9},{9,13},{13,1},{2,6},{6,10},{... | collective-permute-start | bytes 3145736 | tf_op jit(solution)/shard_map/ppermute | solution.py:171
  135.3 29.4 %collective-permute-start.18 = (f32[2,16,32,256]{3,2,1,0:T(8,128)}, f32[2,16,32,256]{3,2,1,0:T(8,128)S(1)}, u32[]{:S(2)}, u32[]{:S(2)}) collective-permute-start(f32[2,16,32,256]{3,2,1,0:T(8,128)} %slice.62), channel_id=1, source_target_pairs={{0,3},{1,0},{2,1},{3,2},{4,7},{5,4},{6,5},{7,6},{8,11},{9,8},{10,9... | collective-permute-start | bytes 3145736 | tf_op jit(solution)/shard_map/ppermute | solution.py:171
  137.6 27.1 %collective-permute-start.20 = (f32[2,16,32,256]{3,2,1,0:T(8,128)}, f32[2,16,32,256]{3,2,1,0:T(8,128)}, u32[]{:S(2)}, u32[]{:S(2)}) collective-permute-start(f32[2,16,32,256]{3,2,1,0:T(8,128)} %slice.63), channel_id=1, source_target_pairs={{0,1},{1,2},{2,3},{3,0},{4,5},{5,6},{6,7},{7,4},{8,9},{9,10},{10,1... | collective-permute-start | bytes 3145736 | tf_op jit(solution)/shard_map/ppermute | solution.py:171
  164.7 1.0 copy-start.1
  164.7 1.3 copy-start.2
  164.7 1.6 copy-start.3
  185.1 3.0 %collective-permute-start.21 = (f32[8,32,1024]{2,1,0:T(8,128)}, f32[8,32,1024]{2,1,0:T(8,128)S(1)}, u32[]{:S(2)}, u32[]{:S(2)}) collective-permute-start(f32[8,32,1024]{2,1,0:T(8,128)} %get-tuple-element.8), channel_id=1, source_target_pairs={{0,16},{16,0},{1,17},{17,1},{2,18},{18,2},{3,19},{19,3},{4,20},{20... | collective-permute-start | bytes 3145736 | tf_op jit(solution)/shard_map/ppermute | solution.py:239
Sparse Core Ops, SparseCore 0:
  9.2 42.4 all-gather.6
  53.5 54.3 all-gather.4

commit v2 on v1

--- a/solution.py
+++ b/solution.py
@@ -105,65 +105,111 @@
     )(plan, own, near, env, env_other)
 
 
-def right_kernel(plan, left, *refs):
-    parts, (keep, send, total, *halves) = refs[:10], refs[10:]
-    pair = pl.program_id(0)
-    core, x, y = plan[CORE], plan[PX], plan[PY]
+def gather_left(left, major, steps):
+    return [
+        left[pair, :, pl.ds(pl.multiple_of(((major + r) % 4) * TILE, TILE), TILE)]
+        for pair in range(2)
+        for r in steps
+    ]
+
+
+def multiply(plan, left, parts, halves, steps):
+    per_half = 4 * len(steps)
     value = []
-    for half, (major, minor) in enumerate(((y, x), (x, y))):
-        here, after, across_low, across_high, before = parts[5 * half : 5 * half + 5]
+    for half, (major, minor) in enumerate(((plan[PY], plan[PX]), (plan[PX], plan[PY]))):
         high, low = halves[2 * half : 2 * half + 2]
-        pieces = [
-            [here.at[i] for i in range(4)],
-            [after.at[i] for i in range(4)],
-            [across_low.at[0], across_low.at[1], across_high.at[0], across_high.at[1]],
-            [before.at[i] for i in range(4)],
-        ]
-        lefts = []
-        for r in range(4):
-            for i in range(4):
-                spot = pl.ds(pl.multiple_of(r * TILE + ((minor + i) % 4) * SUB, SUB), SUB)
-                high[spot, :], low[spot, :] = split(pieces[r][i][0])
-            lefts.append(left[0, :, pl.ds(pl.multiple_of(((major + r) % 4) * TILE, TILE), TILE)])
-        value.append(product(jnp.concatenate(lefts, axis=1), high[...], low[...]))
-    value = jnp.concatenate(value, axis=1)
-
-    @pl.when(pair % 2 == 0)
-    def _():
-        total[...] = value
-
-    @pl.when(pair % 2 == 1)
-    def _():
-        turned = (total[...] + value).T.reshape(HOMES // 2, 2, SUB, TILE)
-        keep[...] = jnp.where(core == 0, turned[:, 0], turned[:, 1])
-        send[...] = jnp.where(core == 0, turned[:, 1], turned[:, 0])
+        strips = parts[per_half * half : per_half * half + per_half]
+        for pair in range(2):
+            for at in range(len(steps)):
+                for i in range(4):
+                    strip = strips[(pair * len(steps) + at) * 2 + i // 2][i % 2, 0]
+                    row = (pair * len(steps) + at) * TILE + ((minor + i) % 4) * SUB
+                    spot = pl.ds(pl.multiple_of(row, SUB), SUB)
+                    high[spot, :], low[spot, :] = split(strip)
+        lefts = jnp.concatenate(gather_left(left, major, steps), axis=1)
+        value.append(product(lefts, high[...], low[...]))
+    return jnp.concatenate(value, axis=1)
+
+
+NEAR_STEPS, FAR_STEPS = (0, 1, 3), (2,)
+
+
+def first_kernel(plan, left, *refs):
+    count = 8 * len(NEAR_STEPS)
+    refs[count][0] = multiply(plan, left, refs[:count], refs[count + 1 :], NEAR_STEPS)
+
+
+def second_kernel(plan, left, part, *refs):
+    count = 8 * len(FAR_STEPS)
+    keep, send = refs[count : count + 2]
+    total = part[0] + multiply(plan, left, refs[:count], refs[count + 2 :], FAR_STEPS)
+    turned = total.T.reshape(HOMES // 2, 2, SUB, TILE)
+    keep[...] = jnp.where(plan[CORE] == 0, turned[:, 0], turned[:, 1])
+    send[...] = jnp.where(plan[CORE] == 0, turned[:, 1], turned[:, 0])
+
+
+def pair_specs(parts, steps):
+    specs, arrays = [], []
+    for half in parts:
+        for pair in range(2):
+            for step in steps:
+                for array in half[step]:
+                    specs.append(
+                        pl.BlockSpec(
+                            (2, 1, SUB, HALF),
+                            lambda t, plan, pair=pair: (0, plan[TERM + 2 * t + pair], 0, 0),
+                        )
+                    )
+                    arrays.append(array)
+    return specs, arrays
 
 
 def right_products(plan, left, parts):
-    def part_spec(part):
-        return pl.BlockSpec((part.shape[0], 1, SUB, HALF), lambda p, plan: (0, plan[TERM + p], 0, 0))
-
+    left_spec = pl.BlockSpec((2, TILE, COLS), lambda t, plan: (t, 0, 0))
+    tile_spec = pl.BlockSpec((1, TILE, COLS), lambda t, plan: (t, 0, 0))
+
+    def cost(steps):
+        return pl.CostEstimate(
+            flops=6 * PAIRS * TILE * COLS * TILE * len(steps),
+            bytes_accessed=(6 + 4 * len(steps)) << 20,
+            transcendentals=0,
+        )
+
+    def scratch(steps):
+        return [pltpu.VMEM((2 * len(steps) * TILE, HALF), jnp.bfloat16)] * 4
+
+    specs, arrays = pair_specs(parts, NEAR_STEPS)
+    first = pl.pallas_call(
+        first_kernel,
+        grid_spec=pltpu.PrefetchScalarGridSpec(
+            num_scalar_prefetch=1,
+            grid=(TILE_DEV,),
+            in_specs=[left_spec] + specs,
+            out_specs=tile_spec,
+            scratch_shapes=scratch(NEAR_STEPS),
+        ),
+        out_shape=jax.ShapeDtypeStruct((TILE_DEV, TILE, COLS), jnp.float32),
+        compiler_params=pltpu.CompilerParams(vmem_limit_bytes=VMEM),
+        cost_estimate=cost(NEAR_STEPS),
+        name="right_near",
+    )(plan, left, *arrays)
+    specs, arrays = pair_specs(parts, FAR_STEPS)
     out = jax.ShapeDtypeStruct((HOMES // 2, SUB, ROWS), jnp.float32)
-    out_spec = pl.BlockSpec((HOMES // 2, SUB, TILE), lambda p, plan: (0, 0, p // 2))
-    grid = pltpu.PrefetchScalarGridSpec(
-        num_scalar_prefetch=1,
-        grid=(PAIRS,),
-        in_specs=[pl.BlockSpec((1, TILE, COLS), lambda p, plan: (p, 0, 0))]
-        + [part_spec(part) for part in parts],
-        out_specs=[out_spec, out_spec],
-        scratch_shapes=[pltpu.VMEM((TILE, COLS), jnp.float32)]
-        + [pltpu.VMEM((COLS, HALF), jnp.bfloat16)] * 4,
-    )
+    out_spec = pl.BlockSpec((HOMES // 2, SUB, TILE), lambda t, plan: (0, 0, t))
     return pl.pallas_call(
-        right_kernel,
-        grid_spec=grid,
+        second_kernel,
+        grid_spec=pltpu.PrefetchScalarGridSpec(
+            num_scalar_prefetch=1,
+            grid=(TILE_DEV,),
+            in_specs=[left_spec, tile_spec] + specs,
+            out_specs=[out_spec, out_spec],
+            scratch_shapes=scratch(FAR_STEPS),
+        ),
         out_shape=[out, out],
         compiler_params=pltpu.CompilerParams(vmem_limit_bytes=VMEM),
-        cost_estimate=pl.CostEstimate(
-            flops=6 * PAIRS * TILE * COLS * COLS, bytes_accessed=22 << 20, transcendentals=0
-        ),
-        name="right_products",
-    )(plan, left, *parts)
+        cost_estimate=cost(FAR_STEPS),
+        name="right_far",
+    )(plan, left, first, *arrays)
 
 
 def ring(value, axis, steps):
@@ -204,7 +250,8 @@
     count = jnp.sum((tile_sector[None, :] == source[:, None]).astype(jnp.int32), axis=1)
     first = jnp.where(usable, first - (base - REACH * TILE_DEV), 0)
     count = jnp.where(usable, count, 0)
-    return jnp.concatenate([first, count, owner, jnp.stack([core, x, y])]).astype(jnp.int32)
+    slot = (owner // 2) * 2 + (owner + core) % 2
+    return jnp.concatenate([first, count, slot, jnp.stack([core, x, y])]).astype(jnp.int32)
 
 
 def on_device(wavefunction, env_blocks, right_env, tile_sector, term_charge, block_home):
@@ -215,7 +262,11 @@
 
     by_y = lax.dynamic_slice(right_env, (0, y * TILE + x * SUB, 0), (2, SUB, HALF))
     by_x = lax.dynamic_slice(right_env, (0, x * TILE + y * SUB, HALF), (2, SUB, HALF))
-    column = lax.all_gather(jnp.stack([by_y, by_x], axis=1), ("z", "core"))
+    strips = jnp.stack([by_y, by_x], axis=1)
+    kept = lax.dynamic_index_in_dim(strips, core, axis=0, keepdims=False)
+    given = lax.dynamic_index_in_dim(strips, 1 - core, axis=0, keepdims=False)
+    column = lax.all_gather(jnp.stack([kept, lax.ppermute(given, "core", swap)]), "z")
+    column = column.reshape(HOMES, 2, SUB, HALF)
 
     strip = lax.dynamic_slice(wavefunction, (home * PART, 0), (PART, COLS))
     near = jnp.stack([wide_shift(strip, steps) for steps in (2, 1, -1, -2)])
@@ -227,12 +278,17 @@
     )
     plan = make_plan(tile_sector, term_charge, block_home, home, core, x, y)
 
-    mine = lax.dynamic_index_in_dim(column, core, axis=1, keepdims=False)
     parts = []
     for at, (first, then) in enumerate((("x", "y"), ("y", "x"))):
-        here, after, low, high, before = around(mine[:, at], first, HOMES // 2)
-        gathered = jnp.stack([here, after, jnp.concatenate([low, high], axis=0), before])
-        parts += around(gathered, then, 2)
+        here, after, low, high, before = around(column[:, at], first, HOMES // 2)
+        ahead = jnp.stack([here, after])
+        behind = jnp.stack([jnp.concatenate([low, high], axis=0), before])
+        ahead_after, behind_before = ring(ahead, then, 1), ring(behind, then, -1)
+        behind_after, ahead_before = ring(behind, then, 1), ring(ahead, then, -1)
+        across = ring(ahead_after, then, 1), ring(behind_before, then, -1)
+        parts.append(
+            ((ahead, behind), (ahead_after, behind_after), across, (ahead_before, behind_before))
+        )
 
     left = left_products(plan, wavefunction, near, env_blocks, env_other)
     keep, send = right_products(plan, left, parts)

time: 235 us -> 246 us (1.047)
  waiting for transfers between devices: 77.1 us -> 99.7 us
  local copies, waits for them, and re-layouts: 20.6 us -> 10.7 us
  Pallas kernels: 41 us -> 46.4 us
  blocking collectives: 35.2 us -> 32.3 us
  starting transfers between devices: 38 us -> 35.4 us
    ppermute x16 -> x20, waiting for transfers between devices: 51.3 us -> 74.5 us  [ring(): lax.ppermute(value, axis, [(i, (i - steps) % count) for i in range(count)])]
    slice x4 -> x2, local copies, waits for them, and re-layouts: 4.72 us -> 0.04 us  [around(): low = ring(lax.slice_in_dim(after, 0, cut), axis, 1)]
    slice x4 -> x2, local copies, waits for them, and re-layouts: 4.7 us -> 0.04 us  [around(): high = ring(lax.slice_in_dim(before, cut, value.shape[0]), axis, -1)]
    pallas_call x1 -> x2, Pallas kernels: 18.8 us -> 22.2 us  [the longest x1 13 us: right_products(): pl.pallas_call(first_kernel, grid_spec=pltpu.PrefetchScalarGridSpec(num_s...]
    all_to_all x1, blocking collectives: 35.2 us -> 32.3 us  [on_device(): shares = lax.all_to_all(total, 'z', split_axis=0, concat_axis=0, tiled=True)]
    ppermute x16 -> x20, starting transfers between devices: 23.8 us -> 21.1 us  [ring(): lax.ppermute(value, axis, [(i, (i - steps) % count) for i in range(count)])]
  transfers between devices with their start and end apart: 24 -> 29, of which waited for: 9 -> 13; matrix products, arithmetic and copies ran while one was open for 9% -> 5% of each run, Pallas kernels for 10% -> 15%
where the time goes in v2:
time: 246 us; the launch traced here: 245 us
  waiting for transfers between devices  99.7 us (41%)
  Pallas kernels  46.4 us (19%)
  starting transfers between devices  35.4 us (14%)
  blocking collectives  32.3 us (13%)
  between operations  13.7 us (6%)
  local copies, waits for them, and re-layouts  10.7 us (4%)
  other arithmetic  6.3 us (3%)
    ppermute x20, waiting for transfers between devices, ring(): lax.ppermute(value, axis, [(i, (i - steps) % count) for i in range(count)])  74.5 us
    all_to_all x1, blocking collectives, on_device(): shares = lax.all_to_all(total, 'z', split_axis=0, concat_axis=0, tiled=True)  32.3 us
    pallas_call x1, Pallas kernels, left_products(): pl.pallas_call(left_kernel, grid_spec=grid, out_shape=jax.ShapeDtypeStruc...  24.2 us
    ppermute x20, starting transfers between devices, ring(): lax.ppermute(value, axis, [(i, (i - steps) % count) for i in range(count)])  21.1 us
    all_gather x1, waiting for transfers between devices, on_device(): lax.all_gather(jnp.stack([kept, lax.ppermute(given, 'core', swap)]), 'z')  15.6 us
    ppermute x4, starting transfers between devices, wide_shift(): lax.ppermute(value, ('y', 'x'), [(i, i + steps) for i in range(max(0, -st...  14.1 us
    pallas_call x1, Pallas kernels, right_products(): pl.pallas_call(first_kernel, grid_spec=pltpu.PrefetchScalarGridSpec(num_s...  13 us
    pallas_call x1, Pallas kernels, right_products(): pl.pallas_call(second_kernel, grid_spec=pltpu.PrefetchScalarGridSpec(num_...  9.19 us
  transfers between devices with their start and end apart: 29, of which 13 were waited for; matrix products, arithmetic and copies ran while one was open for 5% of the time, Pallas kernels for 15%

profile of v2, /device:TPU:6, one launch (start us, length us, event | category | flops | bytes accessed | tf_op | source)
XLA Modules:
  0.0 244.6 jit_solution(3982596050163820944)
XLA Ops:
  6.5 0.9 dynamic-slice_bitcast_fusion.1
  7.4 0.1 collective-permute-start.5
  7.5 1.2 collective-permute-done.5
  8.8 0.7 pad_maximum_fusion.5
  9.5 0.9 constant_dynamic-slice_fusion
  10.5 3.3 %collective-permute-start.3 = (f32[64,512]{1,0:T(8,128)S(1)}, f32[64,512]{1,0:T(8,128)S(1)}, u32[]{:S(2)}, u32[]{:S(2)}) collective-permute-start(f32[64,512]{1,0:T(8,128)S(1)} %constant_dynamic-slice_fusion), channel_id=1, source_target_pairs={{2,0},{3,1},{4,2},{5,3},{6,4},{7,5},{8,6},{9,7},{10,8},{11,9},{12,... | collective-permute-start | bytes 393224 | tf_op jit(solution)/shard_map/ppermute | solution.py:229
  13.8 3.6 %collective-permute-start.2 = (f32[64,512]{1,0:T(8,128)S(1)}, f32[64,512]{1,0:T(8,128)S(1)}, u32[]{:S(2)}, u32[]{:S(2)}) collective-permute-start(f32[64,512]{1,0:T(8,128)S(1)} %constant_dynamic-slice_fusion), channel_id=1, source_target_pairs={{1,0},{2,1},{3,2},{4,3},{5,4},{6,5},{7,6},{8,7},{9,8},{10,9},{11,1... | collective-permute-start | bytes 393224 | tf_op jit(solution)/shard_map/ppermute | solution.py:229
  17.4 4.4 %collective-permute-start.1 = (f32[64,512]{1,0:T(8,128)S(1)}, f32[64,512]{1,0:T(8,128)S(1)}, u32[]{:S(2)}, u32[]{:S(2)}) collective-permute-start(f32[64,512]{1,0:T(8,128)S(1)} %constant_dynamic-slice_fusion), channel_id=1, source_target_pairs={{0,1},{1,2},{2,3},{3,4},{4,5},{5,6},{6,7},{7,8},{8,9},{9,10},{10,1... | collective-permute-start | bytes 393224 | tf_op jit(solution)/shard_map/ppermute | solution.py:229
  21.8 2.8 %collective-permute-start = (f32[64,512]{1,0:T(8,128)S(1)}, f32[64,512]{1,0:T(8,128)S(1)}, u32[]{:S(2)}, u32[]{:S(2)}) collective-permute-start(f32[64,512]{1,0:T(8,128)S(1)} %constant_dynamic-slice_fusion), channel_id=1, source_target_pairs={{0,2},{1,3},{2,4},{3,5},{4,6},{5,7},{6,8},{7,9},{8,10},{9,11},{10,... | collective-permute-start | bytes 393224 | tf_op jit(solution)/shard_map/ppermute | solution.py:229
  24.6 5.5 %collective-permute-done = f32[64,512]{1,0:T(8,128)S(1)} collective-permute-done((f32[64,512]{1,0:T(8,128)S(1)}, f32[64,512]{1,0:T(8,128)S(1)}, u32[]{:S(2)}, u32[]{:S(2)}) %collective-permute-start) | collective-permute-done | bytes 131104 | tf_op jit(solution)/shard_map/ppermute | solution.py:229
  30.1 0.8 pad_maximum_fusion.4
  31.0 4.7 %dynamic-slice_bitcast_fusion = f32[8,128,1024]{2,1,0:T(8,128)} fusion(f32[8,2,128,1024]{3,2,1,0:T(8,128)} %bitcast.40, s32[]{:T(128)S(6)} %select_n.67), kind=kLoop, calls=%fused_computation | loop fusion | bytes 8388612 | tf_op jit(solution)/shard_map/jit(dynamic_index_in_dim)/squeeze | solution.py:277
  35.7 15.6 %all-gather.7.cloned.1.call-done = f32[16,2,32,256]{3,2,0,1:T(8,128)} async-done(((f32[2,2,32,256]{3,2,0,1:T(8,128)}), f32[16,2,32,256]{3,2,0,1:T(8,128)}) %all-gather.7.cloned.1.call-update) | async-done | bytes 1048592 | tf_op jit(solution)/shard_map/all_gather | solution.py:268
  51.3 1.5 slice_bitcast_fusion.1
  52.7 0.6 collective-permute-start.8
  53.4 1.5 collective-permute-start.6
  54.9 2.5 %collective-permute-start.14 = (f32[16,32,256]{2,1,0:T(8,128)S(1)}, f32[16,32,256]{2,1,0:T(8,128)S(1)}, u32[]{:S(2)}, u32[]{:S(2)}) collective-permute-start(f32[16,32,256]{2,1,0:T(8,128)S(1)} %get-tuple-element.15), channel_id=1, source_target_pairs={{0,12},{4,0},{8,4},{12,8},{1,13},{5,1},{9,5},{13,9},{2,14},{6,2},{... | collective-permute-start | bytes 1572872 | tf_op jit(solution)/shard_map/ppermute | solution.py:217
  57.3 7.5 %collective-permute-done.8 = f32[16,32,256]{2,1,0:T(8,128)S(1)} collective-permute-done((f32[16,32,256]{2,1,0:T(8,128)S(1)}, f32[16,32,256]{2,1,0:T(8,128)S(1)}, u32[]{:S(2)}, u32[]{:S(2)}) %collective-permute-start.8) | collective-permute-done | bytes 524320 | tf_op jit(solution)/shard_map/ppermute | solution.py:217
  64.8 1.5 collective-permute-start.9
  66.3 0.1 collective-permute-done.6
  66.4 0.6 collective-permute-start.7
  67.0 0.1 pad_maximum_fusion.refs_0_.refs_6_
  67.2 2.6 %collective-permute-start.10 = (f32[2,16,32,256]{3,2,1,0:T(8,128)S(1)}, f32[2,16,32,256]{3,2,1,0:T(8,128)S(1)}, u32[]{:S(2)}, u32[]{:S(2)}) collective-permute-start(f32[2,16,32,256]{3,2,1,0:T(8,128)S(1)} %pad_maximum_fusion.refs_0_.refs_6_), channel_id=1, source_target_pairs={{0,12},{4,0},{8,4},{12,8},{1,13},{5,1},{9,5},{13,9},{2,14},{6,2},{... | collective-permute-start | bytes 3145736 | tf_op jit(solution)/shard_map/ppermute | solution.py:217
  69.7 0.1 pad_maximum_fusion.2.refs_12_.refs_18_
  69.9 0.1 collective-permute-start.12
  70.0 1.3 collective-permute-done.9
  71.3 0.7 collective-permute-start.18
  72.1 4.9 %collective-permute-done.7 = f32[8,32,256]{2,1,0:T(8,128)S(1)} collective-permute-done((f32[8,32,256]{2,1,0:T(8,128)S(1)}, f32[8,32,256]{2,1,0:T(8,128)S(1)}, u32[]{:S(2)}, u32[]{:S(2)}) %collective-permute-start.7) | collective-permute-done | bytes 262176 | tf_op jit(solution)/shard_map/ppermute | solution.py:217
  76.9 0.8 collective-permute-start.17
  77.7 18.1 %collective-permute-done.17 = f32[8,32,256]{2,1,0:T(8,128)S(1)} collective-permute-done((f32[8,32,256]{2,1,0:T(8,128)S(1)}, f32[8,32,256]{2,1,0:T(8,128)S(1)}, u32[]{:S(2)}, u32[]{:S(2)}) %collective-permute-start.17) | collective-permute-done | bytes 262176 | tf_op jit(solution)/shard_map/ppermute | solution.py:217
  95.9 0.1 pad_maximum_fusion.1.refs_1_.refs_7_
  96.0 8.5 %collective-permute-done.15 = f32[8,32,256]{2,1,0:T(8,128)S(1)} collective-permute-done((f32[8,32,256]{2,1,0:T(8,128)S(1)}, f32[8,32,256]{2,1,0:T(8,128)S(1)}, u32[]{:S(2)}, u32[]{:S(2)}) %collective-permute-start.15) | collective-permute-done | bytes 262176 | tf_op jit(solution)/shard_map/ppermute | solution.py:217
  104.5 2.5 %collective-permute-start.20 = (f32[2,16,32,256]{3,2,1,0:T(8,128)S(1)}, f32[2,16,32,256]{3,2,1,0:T(8,128)}, u32[]{:S(2)}, u32[]{:S(2)}) collective-permute-start(f32[2,16,32,256]{3,2,1,0:T(8,128)S(1)} %pad_maximum_fusion.2.refs_12_.refs_18_), channel_id=1, source_target_pairs={{0,1},{1,2},{2,3},{3,0},{4,5},{5,6},{6,7},{7,4},{8,9},{9,10},{10,1... | collective-permute-start | bytes 3145736 | tf_op jit(solution)/shard_map/ppermute | solution.py:217
  107.1 1.1 pad_maximum_fusion.3.refs_13_.refs_19_
  108.2 1.1 collective-permute-start.11
  109.3 1.2 collective-permute-start.13
  110.5 1.0 copy-done.4
  111.5 0.2 collective-permute-start.21
  111.6 0.6 slice.29
  112.2 0.1 dynamic_slice.23
  112.3 0.1 broadcast_in_dim.28
  112.4 0.1 reshape.36
  112.5 0.2 select_reduce_fusion.1
  112.7 0.1 copy.16
  112.8 0.1 reshape.38
  112.9 17.8 %collective-permute-done.20.refs_16_.refs_22_ = f32[2,16,32,256]{3,2,1,0:T(8,128)} collective-permute-done((f32[2,16,32,256]{3,2,1,0:T(8,128)S(1)}, f32[2,16,32,256]{3,2,1,0:T(8,128)}, u32[]{:S(2)}, u32[]{:S(2)}) %collective-permute-start.20) | collective-permute-done | bytes 1048608 | tf_op jit(solution)/shard_map/ppermute | solution.py:217
  130.7 0.5 collective-permute-start.19
  131.2 0.2 select_reduce_fusion
  131.4 0.2 convert_reduce_fusion
  131.6 0.2 collective-permute-done.11.refs_3_.refs_9_
  131.8 0.9 collective-permute-start.22
  132.7 1.3 collective-permute-start.24
  134.0 16.1 %collective-permute-done.21.refs_17_.refs_23_ = f32[2,16,32,256]{3,2,1,0:T(8,128)} collective-permute-done((f32[2,16,32,256]{3,2,1,0:T(8,128)}, f32[2,16,32,256]{3,2,1,0:T(8,128)}, u32[]{:S(2)}, u32[]{:S(2)}) %collective-permute-start.21) | collective-permute-done | bytes 1048608 | tf_op jit(solution)/shard_map/ppermute | solution.py:217
  150.1 2.5 %collective-permute-start.25 = (f32[2,16,32,256]{3,2,1,0:T(8,128)}, f32[2,16,32,256]{3,2,1,0:T(8,128)}, u32[]{:S(2)}, u32[]{:S(2)}) collective-permute-start(f32[2,16,32,256]{3,2,1,0:T(8,128)} %collective-permute-done.21.refs_17_.refs_23_), channel_id=1, source_target_pairs={{0,1},{1,2},{2,3},{3,0},{4,5},{5,6},{6,7},{7,4},{8,9},{9,10},{10,1... | collective-permute-start | bytes 3145736 | tf_op jit(solution)/shard_map/ppermute | solution.py:217
  152.6 0.6 broadcast_select_fusion.1
  153.3 0.6 concatenate.9.plan
  153.9 24.2 %left_products.1.left = f32[16,128,512]{2,1,0:T(8,128)} custom-call(s32[51]{0:T(128)} %concatenate.9.plan, f32[1024,512]{1,0:T(8,128)} %own.1, f32[16,4,64,512]{3,2,1,0:T(8,128)} %bitcast.41, f32[16,128,1024]{2,1,0:T(8,128)} %env_own.1, f32[8,128,1024]{2,1,0:T(8,128)} %collective-permute-done.4.env_other), custom_call_target="tpu_custom_call" | custom-call | flops 6442450944 | bytes 25165824 | tf_op jit(solution)/shard_map/left_products/pallas_call | solution.py:96
  178.1 13.0 %right_near.1.part = f32[8,128,512]{2,1,0:T(8,128)} custom-call(s32[51]{0:T(128)} %concatenate.9.plan, f32[16,128,512]{2,1,0:T(8,128)} %left_products.1.left, f32[2,16,32,256]{3,2,1,0:T(8,128)} %copy-done, f32[2,16,32,256]{3,2,1,0:T(8,128)} %copy-done.2, f32[2,16,32,256]{3,2,1,0:T(8,128)} %copy-done.3, ...), custom_call_target="tpu_custom_call" | custom-call | flops 2415919104 | bytes 18874368 | tf_op jit(solution)/shard_map/right_near/pallas_call | solution.py:182
  191.2 9.2 %right_far.1 = (f32[8,32,1024]{2,1,0:T(8,128)}, f32[8,32,1024]{2,1,0:T(8,128)}) custom-call(s32[51]{0:T(128)} %concatenate.9.plan, f32[16,128,512]{2,1,0:T(8,128)} %left_products.1.left, f32[8,128,512]{2,1,0:T(8,128)} %right_near.1.part, f32[2,16,32,256]{3,2,1,0:T(8,128)} %collective-permute-done.22.refs_0_.refs_2_, ...), custom_call_target="tpu_custom_call" | custom-call | flops 805306368 | bytes 10485760 | tf_op jit(solution)/shard_map/right_far/pallas_call | solution.py:199
  200.4 0.1 collective-permute-start.26
  200.5 2.9 %collective-permute-done.26 = f32[8,32,1024]{2,1,0:T(8,128)S(1)} collective-permute-done((f32[8,32,1024]{2,1,0:T(8,128)}, f32[8,32,1024]{2,1,0:T(8,128)S(1)}, u32[]{:S(2)}, u32[]{:S(2)}) %collective-permute-start.26) | collective-permute-done | bytes 1048608 | tf_op jit(solution)/shard_map/ppermute | solution.py:295
  203.3 1.4 add.97
  204.7 32.3 %all_to_all.5 = f32[8,32,1024]{2,1,0:T(8,128)S(1)} all-to-all(f32[8,32,1024]{2,1,0:T(8,128)S(1)} %add.97), channel_id=1, replica_groups=mesh['z'=8,'core'=2,'y'=4,'x'=4] {'z'}, dimensions={0} | all-to-all | bytes 2097152 | tf_op jit(solution)/shard_map/all_to_all | solution.py:296
  237.0 0.7 reduce_sum.49
  (53 shorter events, 0.4 us)
Async XLA Ops:
  6.5 44.7 %all-gather.7.cloned.1.call-start = ((), (), s32[]{:S(2)}) async-start(), calls=%async_computation.2 | async-start | bytes 1179648 | tf_op jit(solution)/shard_map/all_gather | solution.py:268
  7.4 1.3 collective-permute-start.5
  9.5 144.4 %all-gather.5.cloned.1.call-start = ((), (), s32[]{:S(2)}) async-start(), calls=%async_computation.1 | async-start | bytes 8912896 | tf_op jit(solution)/shard_map/all_gather | solution.py:273
  10.5 14.1 %collective-permute-start.3 = (f32[64,512]{1,0:T(8,128)S(1)}, f32[64,512]{1,0:T(8,128)S(1)}, u32[]{:S(2)}, u32[]{:S(2)}) collective-permute-start(f32[64,512]{1,0:T(8,128)S(1)} %constant_dynamic-slice_fusion), channel_id=1, source_target_pairs={{2,0},{3,1},{4,2},{5,3},{6,4},{7,5},{8,6},{9,7},{10,8},{11,9},{12,... | collective-permute-start | bytes 393224 | tf_op jit(solution)/shard_map/ppermute | solution.py:229
  13.8 10.8 %collective-permute-start.2 = (f32[64,512]{1,0:T(8,128)S(1)}, f32[64,512]{1,0:T(8,128)S(1)}, u32[]{:S(2)}, u32[]{:S(2)}) collective-permute-start(f32[64,512]{1,0:T(8,128)S(1)} %constant_dynamic-slice_fusion), channel_id=1, source_target_pairs={{1,0},{2,1},{3,2},{4,3},{5,4},{6,5},{7,6},{8,7},{9,8},{10,9},{11,1... | collective-permute-start | bytes 393224 | tf_op jit(solution)/shard_map/ppermute | solution.py:229
  17.4 7.2 %collective-permute-start.1 = (f32[64,512]{1,0:T(8,128)S(1)}, f32[64,512]{1,0:T(8,128)S(1)}, u32[]{:S(2)}, u32[]{:S(2)}) collective-permute-start(f32[64,512]{1,0:T(8,128)S(1)} %constant_dynamic-slice_fusion), channel_id=1, source_target_pairs={{0,1},{1,2},{2,3},{3,4},{4,5},{5,6},{6,7},{7,8},{8,9},{9,10},{10,1... | collective-permute-start | bytes 393224 | tf_op jit(solution)/shard_map/ppermute | solution.py:229
  21.8 8.4 %collective-permute-start = (f32[64,512]{1,0:T(8,128)S(1)}, f32[64,512]{1,0:T(8,128)S(1)}, u32[]{:S(2)}, u32[]{:S(2)}) collective-permute-start(f32[64,512]{1,0:T(8,128)S(1)} %constant_dynamic-slice_fusion), channel_id=1, source_target_pairs={{0,2},{1,3},{2,4},{3,5},{4,6},{5,7},{6,8},{7,9},{8,10},{9,11},{10,... | collective-permute-start | bytes 393224 | tf_op jit(solution)/shard_map/ppermute | solution.py:229
  35.7 114.4 %collective-permute-start.4 = (f32[8,128,1024]{2,1,0:T(8,128)}, f32[8,128,1024]{2,1,0:T(8,128)}, u32[]{:S(2)}, u32[]{:S(2)}) collective-permute-start(f32[8,128,1024]{2,1,0:T(8,128)} %dynamic-slice_bitcast_fusion), channel_id=1, source_target_pairs={{0,16},{16,0},{1,17},{17,1},{2,18},{18,2},{3,19},{19,3},{4,20},{20... | collective-permute-start | bytes 12582920 | tf_op jit(solution)/shard_map/ppermute | solution.py:276
  52.7 12.1 %collective-permute-start.8 = (f32[16,32,256]{2,1,0:T(8,128)S(1)}, f32[16,32,256]{2,1,0:T(8,128)S(1)}, u32[]{:S(2)}, u32[]{:S(2)}) collective-permute-start(f32[16,32,256]{2,1,0:T(8,128)S(1)} %get-tuple-element.14), channel_id=1, source_target_pairs={{0,1},{1,2},{2,3},{3,0},{4,5},{5,6},{6,7},{7,4},{8,9},{9,10},{10,1... | collective-permute-start | bytes 1572872 | tf_op jit(solution)/shard_map/ppermute | solution.py:217
  53.4 13.0 %collective-permute-start.6 = (f32[16,32,256]{2,1,0:T(8,128)S(1)}, f32[16,32,256]{2,1,0:T(8,128)S(1)}, u32[]{:S(2)}, u32[]{:S(2)}) collective-permute-start(f32[16,32,256]{2,1,0:T(8,128)S(1)} %get-tuple-element.14), channel_id=1, source_target_pairs={{0,3},{1,0},{2,1},{3,2},{4,7},{5,4},{6,5},{7,6},{8,11},{9,8},{10,9... | collective-permute-start | bytes 1572872 | tf_op jit(solution)/shard_map/ppermute | solution.py:217
  54.9 12.3 %collective-permute-start.14 = (f32[16,32,256]{2,1,0:T(8,128)S(1)}, f32[16,32,256]{2,1,0:T(8,128)S(1)}, u32[]{:S(2)}, u32[]{:S(2)}) collective-permute-start(f32[16,32,256]{2,1,0:T(8,128)S(1)} %get-tuple-element.15), channel_id=1, source_target_pairs={{0,12},{4,0},{8,4},{12,8},{1,13},{5,1},{9,5},{13,9},{2,14},{6,2},{... | collective-permute-start | bytes 1572872 | tf_op jit(solution)/shard_map/ppermute | solution.py:217
  57.3 12.5 %collective-permute-start.16 = (f32[16,32,256]{2,1,0:T(8,128)S(1)}, f32[16,32,256]{2,1,0:T(8,128)S(1)}, u32[]{:S(2)}, u32[]{:S(2)}) collective-permute-start(f32[16,32,256]{2,1,0:T(8,128)S(1)} %get-tuple-element.15), channel_id=1, source_target_pairs={{0,4},{4,8},{8,12},{12,0},{1,5},{5,9},{9,13},{13,1},{2,6},{6,10},{... | collective-permute-start | bytes 1572872 | tf_op jit(solution)/shard_map/ppermute | solution.py:217
  64.8 6.4 %collective-permute-start.9 = (f32[8,32,256]{2,1,0:T(8,128)S(1)}, f32[8,32,256]{2,1,0:T(8,128)S(1)}, u32[]{:S(2)}, u32[]{:S(2)}) collective-permute-start(f32[8,32,256]{2,1,0:T(8,128)S(1)} %slice.40), channel_id=1, source_target_pairs={{0,1},{1,2},{2,3},{3,0},{4,5},{5,6},{6,7},{7,4},{8,9},{9,10},{10,1... | collective-permute-start | bytes 786440 | tf_op jit(solution)/shard_map/ppermute | solution.py:217
  66.4 10.5 %collective-permute-start.7 = (f32[8,32,256]{2,1,0:T(8,128)S(1)}, f32[8,32,256]{2,1,0:T(8,128)S(1)}, u32[]{:S(2)}, u32[]{:S(2)}) collective-permute-start(f32[8,32,256]{2,1,0:T(8,128)S(1)} %slice.39), channel_id=1, source_target_pairs={{0,3},{1,0},{2,1},{3,2},{4,7},{5,4},{6,5},{7,6},{8,11},{9,8},{10,9... | collective-permute-start | bytes 786440 | tf_op jit(solution)/shard_map/ppermute | solution.py:217
  67.2 41.0 %copy-start = (f32[2,16,32,256]{3,2,1,0:T(8,128)}, f32[2,16,32,256]{3,2,1,0:T(8,128)S(1)}, u32[]{:S(2)}) copy-start(f32[2,16,32,256]{3,2,1,0:T(8,128)S(1)} %pad_maximum_fusion.refs_0_.refs_6_) | copy-start | bytes 3145732
  67.2 41.0 %collective-permute-start.10 = (f32[2,16,32,256]{3,2,1,0:T(8,128)S(1)}, f32[2,16,32,256]{3,2,1,0:T(8,128)S(1)}, u32[]{:S(2)}, u32[]{:S(2)}) collective-permute-start(f32[2,16,32,256]{3,2,1,0:T(8,128)S(1)} %pad_maximum_fusion.refs_0_.refs_6_), channel_id=1, source_target_pairs={{0,12},{4,0},{8,4},{12,8},{1,13},{5,1},{9,5},{13,9},{2,14},{6,2},{... | collective-permute-start | bytes 3145736 | tf_op jit(solution)/shard_map/ppermute | solution.py:217
  69.8 108.2 %copy-start.1 = (f32[2,16,32,256]{3,2,1,0:T(8,128)}, f32[2,16,32,256]{3,2,1,0:T(8,128)S(1)}, u32[]{:S(2)}) copy-start(f32[2,16,32,256]{3,2,1,0:T(8,128)S(1)} %pad_maximum_fusion.2.refs_12_.refs_18_) | copy-start | bytes 3145732
  69.8 41.8 %copy-start.7 = (s32[128]{0:T(128)S(1)}, s32[128]{0:T(128)}, u32[]{:S(2)}) copy-start(s32[128]{0:T(128)} %param.9) | copy-start | bytes 1540
  69.8 42.6 %copy-start.6 = (s32[16,16]{1,0:T(8,128)S(1)}, s32[16,16]{1,0:T(8,128)}, u32[]{:S(2)}) copy-start(s32[16,16]{1,0:T(8,128)} %param.11) | copy-start | bytes 3076
  69.9 61.4 %copy-start.8 = (s32[32]{0:T(128)S(1)}, s32[32]{0:T(128)}, u32[]{:S(2)}) copy-start(s32[32]{0:T(128)} %param.10) | copy-start | bytes 388
  69.9 39.4 %collective-permute-start.12 = (f32[2,16,32,256]{3,2,1,0:T(8,128)S(1)}, f32[2,16,32,256]{3,2,1,0:T(8,128)S(1)}, u32[]{:S(2)}, u32[]{:S(2)}) collective-permute-start(f32[2,16,32,256]{3,2,1,0:T(8,128)S(1)} %pad_maximum_fusion.refs_0_.refs_6_), channel_id=1, source_target_pairs={{0,4},{4,8},{8,12},{12,0},{1,5},{5,9},{9,13},{13,1},{2,6},{6,10},{... | collective-permute-start | bytes 3145736 | tf_op jit(solution)/shard_map/ppermute | solution.py:217
  71.3 39.2 %collective-permute-start.18 = (f32[2,16,32,256]{3,2,1,0:T(8,128)S(1)}, f32[2,16,32,256]{3,2,1,0:T(8,128)S(1)}, u32[]{:S(2)}, u32[]{:S(2)}) collective-permute-start(f32[2,16,32,256]{3,2,1,0:T(8,128)S(1)} %pad_maximum_fusion.2.refs_12_.refs_18_), channel_id=1, source_target_pairs={{0,3},{1,0},{2,1},{3,2},{4,7},{5,4},{6,5},{7,6},{8,11},{9,8},{10,9... | collective-permute-start | bytes 3145736 | tf_op jit(solution)/shard_map/ppermute | solution.py:217
  76.9 18.9 %collective-permute-start.17 = (f32[8,32,256]{2,1,0:T(8,128)S(1)}, f32[8,32,256]{2,1,0:T(8,128)S(1)}, u32[]{:S(2)}, u32[]{:S(2)}) collective-permute-start(f32[8,32,256]{2,1,0:T(8,128)S(1)} %slice.43), channel_id=1, source_target_pairs={{0,4},{4,8},{8,12},{12,0},{1,5},{5,9},{9,13},{13,1},{2,6},{6,10},{... | collective-permute-start | bytes 786440 | tf_op jit(solution)/shard_map/ppermute | solution.py:217
  95.8 8.7 %collective-permute-start.15 = (f32[8,32,256]{2,1,0:T(8,128)S(1)}, f32[8,32,256]{2,1,0:T(8,128)S(1)}, u32[]{:S(2)}, u32[]{:S(2)}) collective-permute-start(f32[8,32,256]{2,1,0:T(8,128)S(1)} %slice.42), channel_id=1, source_target_pairs={{0,12},{4,0},{8,4},{12,8},{1,13},{5,1},{9,5},{13,9},{2,14},{6,2},{... | collective-permute-start | bytes 786440 | tf_op jit(solution)/shard_map/ppermute | solution.py:217
  96.0 82.1 %copy-start.2 = (f32[2,16,32,256]{3,2,1,0:T(8,128)}, f32[2,16,32,256]{3,2,1,0:T(8,128)S(1)}, u32[]{:S(2)}) copy-start(f32[2,16,32,256]{3,2,1,0:T(8,128)S(1)} %pad_maximum_fusion.1.refs_1_.refs_7_) | copy-start | bytes 3145732
  104.5 26.2 %collective-permute-start.20 = (f32[2,16,32,256]{3,2,1,0:T(8,128)S(1)}, f32[2,16,32,256]{3,2,1,0:T(8,128)}, u32[]{:S(2)}, u32[]{:S(2)}) collective-permute-start(f32[2,16,32,256]{3,2,1,0:T(8,128)S(1)} %pad_maximum_fusion.2.refs_12_.refs_18_), channel_id=1, source_target_pairs={{0,1},{1,2},{2,3},{3,0},{4,5},{5,6},{6,7},{7,4},{8,9},{9,10},{10,1... | collective-permute-start | bytes 3145736 | tf_op jit(solution)/shard_map/ppermute | solution.py:217
  108.2 69.9 %copy-start.3 = (f32[2,16,32,256]{3,2,1,0:T(8,128)}, f32[2,16,32,256]{3,2,1,0:T(8,128)S(1)}, u32[]{:S(2)}) copy-start(f32[2,16,32,256]{3,2,1,0:T(8,128)S(1)} %collective-permute-done.10.refs_2_.refs_8_) | copy-start | bytes 3145732
  108.2 23.6 %collective-permute-start.11 = (f32[2,16,32,256]{3,2,1,0:T(8,128)S(1)}, f32[2,16,32,256]{3,2,1,0:T(8,128)}, u32[]{:S(2)}, u32[]{:S(2)}) collective-permute-start(f32[2,16,32,256]{3,2,1,0:T(8,128)S(1)} %pad_maximum_fusion.1.refs_1_.refs_7_), channel_id=1, source_target_pairs={{0,12},{4,0},{8,4},{12,8},{1,13},{5,1},{9,5},{13,9},{2,14},{6,2},{... | collective-permute-start | bytes 3145736 | tf_op jit(solution)/shard_map/ppermute | solution.py:217
  109.3 1.2 copy-start.5
  109.3 23.3 %collective-permute-start.13 = (f32[2,16,32,256]{3,2,1,0:T(8,128)S(1)}, f32[2,16,32,256]{3,2,1,0:T(8,128)}, u32[]{:S(2)}, u32[]{:S(2)}) collective-permute-start(f32[2,16,32,256]{3,2,1,0:T(8,128)S(1)} %pad_maximum_fusion.1.refs_1_.refs_7_), channel_id=1, source_target_pairs={{0,4},{4,8},{8,12},{12,0},{1,5},{5,9},{9,13},{13,1},{2,6},{6,10},{... | collective-permute-start | bytes 3145736 | tf_op jit(solution)/shard_map/ppermute | solution.py:217
  110.5 1.0 copy-start.4
  111.5 38.6 %collective-permute-start.21 = (f32[2,16,32,256]{3,2,1,0:T(8,128)}, f32[2,16,32,256]{3,2,1,0:T(8,128)}, u32[]{:S(2)}, u32[]{:S(2)}) collective-permute-start(f32[2,16,32,256]{3,2,1,0:T(8,128)} %pad_maximum_fusion.3.refs_13_.refs_19_), channel_id=1, source_target_pairs={{0,1},{1,2},{2,3},{3,0},{4,5},{5,6},{6,7},{7,4},{8,9},{9,10},{10,1... | collective-permute-start | bytes 3145736 | tf_op jit(solution)/shard_map/ppermute | solution.py:217
  130.7 47.4 %collective-permute-start.19 = (f32[2,16,32,256]{3,2,1,0:T(8,128)}, f32[2,16,32,256]{3,2,1,0:T(8,128)}, u32[]{:S(2)}, u32[]{:S(2)}) collective-permute-start(f32[2,16,32,256]{3,2,1,0:T(8,128)} %pad_maximum_fusion.3.refs_13_.refs_19_), channel_id=1, source_target_pairs={{0,3},{1,0},{2,1},{3,2},{4,7},{5,4},{6,5},{7,6},{8,11},{9,8},{10,9... | collective-permute-start | bytes 3145736 | tf_op jit(solution)/shard_map/ppermute | solution.py:217
  131.8 59.4 %collective-permute-start.22 = (f32[2,16,32,256]{3,2,1,0:T(8,128)S(1)}, f32[2,16,32,256]{3,2,1,0:T(8,128)}, u32[]{:S(2)}, u32[]{:S(2)}) collective-permute-start(f32[2,16,32,256]{3,2,1,0:T(8,128)S(1)} %collective-permute-done.10.refs_2_.refs_8_), channel_id=1, source_target_pairs={{0,12},{4,0},{8,4},{12,8},{1,13},{5,1},{9,5},{13,9},{2,14},{6,2},{... | collective-permute-start | bytes 3145736 | tf_op jit(solution)/shard_map/ppermute | solution.py:217
  132.7 58.5 %collective-permute-start.24 = (f32[2,16,32,256]{3,2,1,0:T(8,128)}, f32[2,16,32,256]{3,2,1,0:T(8,128)}, u32[]{:S(2)}, u32[]{:S(2)}) collective-permute-start(f32[2,16,32,256]{3,2,1,0:T(8,128)} %copy-done.4), channel_id=1, source_target_pairs={{0,3},{1,0},{2,1},{3,2},{4,7},{5,4},{6,5},{7,6},{8,11},{9,8},{10,9... | collective-permute-start | bytes 3145736 | tf_op jit(solution)/shard_map/ppermute | solution.py:217
  150.1 41.1 %collective-permute-start.23 = (f32[2,16,32,256]{3,2,1,0:T(8,128)}, f32[2,16,32,256]{3,2,1,0:T(8,128)}, u32[]{:S(2)}, u32[]{:S(2)}) collective-permute-start(f32[2,16,32,256]{3,2,1,0:T(8,128)} %collective-permute-done.13.refs_5_.refs_11_), channel_id=1, source_target_pairs={{0,4},{4,8},{8,12},{12,0},{1,5},{5,9},{9,13},{13,1},{2,6},{6,10},{... | collective-permute-start | bytes 3145736 | tf_op jit(solution)/shard_map/ppermute | solution.py:217
  150.1 41.1 %collective-permute-start.25 = (f32[2,16,32,256]{3,2,1,0:T(8,128)}, f32[2,16,32,256]{3,2,1,0:T(8,128)}, u32[]{:S(2)}, u32[]{:S(2)}) collective-permute-start(f32[2,16,32,256]{3,2,1,0:T(8,128)} %collective-permute-done.21.refs_17_.refs_23_), channel_id=1, source_target_pairs={{0,1},{1,2},{2,3},{3,0},{4,5},{5,6},{6,7},{7,4},{8,9},{9,10},{10,1... | collective-permute-start | bytes 3145736 | tf_op jit(solution)/shard_map/ppermute | solution.py:217
  200.4 3.0 %collective-permute-start.26 = (f32[8,32,1024]{2,1,0:T(8,128)}, f32[8,32,1024]{2,1,0:T(8,128)S(1)}, u32[]{:S(2)}, u32[]{:S(2)}) collective-permute-start(f32[8,32,1024]{2,1,0:T(8,128)} %get-tuple-element.8), channel_id=1, source_target_pairs={{0,16},{16,0},{1,17},{17,1},{2,18},{18,2},{3,19},{19,3},{4,20},{20... | collective-permute-start | bytes 3145736 | tf_op jit(solution)/shard_map/ppermute | solution.py:295
Sparse Core Ops, SparseCore 0:
  9.6 41.6 all-gather.6
  53.1 54.2 all-gather.4

commit v3 on v2

--- a/solution.py
+++ b/solution.py
@@ -250,7 +250,7 @@
     count = jnp.sum((tile_sector[None, :] == source[:, None]).astype(jnp.int32), axis=1)
     first = jnp.where(usable, first - (base - REACH * TILE_DEV), 0)
     count = jnp.where(usable, count, 0)
-    slot = (owner // 2) * 2 + (owner + core) % 2
+    slot = ((owner // 2 - home // 2) % (HOMES // 2)) * 2 + (owner + core) % 2
     return jnp.concatenate([first, count, slot, jnp.stack([core, x, y])]).astype(jnp.int32)
 
 
@@ -265,8 +265,10 @@
     strips = jnp.stack([by_y, by_x], axis=1)
     kept = lax.dynamic_index_in_dim(strips, core, axis=0, keepdims=False)
     given = lax.dynamic_index_in_dim(strips, 1 - core, axis=0, keepdims=False)
-    column = lax.all_gather(jnp.stack([kept, lax.ppermute(given, "core", swap)]), "z")
-    column = column.reshape(HOMES, 2, SUB, HALF)
+    strip = jnp.stack([kept, lax.ppermute(given, "core", swap)])
+    column = {0: strip}
+    for steps in (1, -1, 2, -2, 3, -3, 4):
+        column[steps % 8] = ring(strip, "z", steps)
 
     strip = lax.dynamic_slice(wavefunction, (home * PART, 0), (PART, COLS))
     near = jnp.stack([wide_shift(strip, steps) for steps in (2, 1, -1, -2)])
@@ -278,14 +280,19 @@
     )
     plan = make_plan(tile_sector, term_charge, block_home, home, core, x, y)
 
+    env_other, column = lax.optimization_barrier((env_other, column))
     parts = []
     for at, (first, then) in enumerate((("x", "y"), ("y", "x"))):
-        here, after, low, high, before = around(column[:, at], first, HOMES // 2)
+        here, after, low, high, before = around(
+            jnp.concatenate([column[steps][:, at] for steps in range(8)]), first, HOMES // 2
+        )
         ahead = jnp.stack([here, after])
         behind = jnp.stack([jnp.concatenate([low, high], axis=0), before])
         ahead_after, behind_before = ring(ahead, then, 1), ring(behind, then, -1)
-        behind_after, ahead_before = ring(behind, then, 1), ring(ahead, then, -1)
         across = ring(ahead_after, then, 1), ring(behind_before, then, -1)
+        behind_late, ahead_after = lax.optimization_barrier((behind, ahead_after))
+        ahead_late, behind_before = lax.optimization_barrier((ahead, behind_before))
+        behind_after, ahead_before = ring(behind_late, then, 1), ring(ahead_late, then, -1)
         parts.append(
             ((ahead, behind), (ahead_after, behind_after), across, (ahead_before, behind_before))
         )

time: 246 us -> 265 us (1.077)
  starting transfers between devices: 35.4 us -> 55.9 us
    ppermute x20 -> x27, starting transfers between devices: 21.1 us -> 41.1 us  [ring(): lax.ppermute(value, axis, [(i, (i - steps) % count) for i in range(count)])]
    all_gather x1 -> x0, waiting for transfers between devices: 15.6 us -> none  [on_device(): lax.all_gather(jnp.stack([kept, lax.ppermute(given, 'core', swap)]), 'z')]
    ppermute x20 -> x27, waiting for transfers between devices: 74.5 us -> 84.8 us  [ring(): lax.ppermute(value, axis, [(i, (i - steps) % count) for i in range(count)])]
    ppermute x1, waiting for transfers between devices: 1.24 us -> 5.74 us  [on_device(): strip = jnp.stack([kept, lax.ppermute(given, 'core', swap)])]
  transfers between devices with their start and end apart: 29 -> 35, of which waited for: 13 -> 15; matrix products, arithmetic and copies ran while one was open for 5% -> 4% of each run, Pallas kernels for 15% -> 13%
where the time goes in v3:
time: 265 us; the launch traced here: 264 us
  waiting for transfers between devices  99 us (37%)
  starting transfers between devices  55.9 us (21%)
  Pallas kernels  44.8 us (17%)
  blocking collectives  34.7 us (13%)
  between operations  13.8 us (5%)
  local copies, waits for them, and re-layouts  10.6 us (4%)
  other arithmetic  5.64 us (2%)
    ppermute x27, waiting for transfers between devices, ring(): lax.ppermute(value, axis, [(i, (i - steps) % count) for i in range(count)])  84.8 us
    ppermute x27, starting transfers between devices, ring(): lax.ppermute(value, axis, [(i, (i - steps) % count) for i in range(count)])  41.1 us
    all_to_all x1, blocking collectives, on_device(): shares = lax.all_to_all(total, 'z', split_axis=0, concat_axis=0, tiled=True)  34.7 us
    pallas_call x1, Pallas kernels, left_products(): pl.pallas_call(left_kernel, grid_spec=grid, out_shape=jax.ShapeDtypeStruc...  22.5 us
    ppermute x4, starting transfers between devices, wide_shift(): lax.ppermute(value, ('y', 'x'), [(i, i + steps) for i in range(max(0, -st...  14.1 us
    pallas_call x1, Pallas kernels, right_products(): pl.pallas_call(first_kernel, grid_spec=pltpu.PrefetchScalarGridSpec(num_s...  13 us
    pallas_call x1, Pallas kernels, right_products(): pl.pallas_call(second_kernel, grid_spec=pltpu.PrefetchScalarGridSpec(num_...  9.21 us
    ppermute x1, waiting for transfers between devices, on_device(): strip = jnp.stack([kept, lax.ppermute(given, 'core', swap)])  5.74 us
  transfers between devices with their start and end apart: 35, of which 15 were waited for; matrix products, arithmetic and copies ran while one was open for 4% of the time, Pallas kernels for 13%

profile of v3, /device:TPU:6, one launch (start us, length us, event | category | flops | bytes accessed | tf_op | source)
XLA Modules:
  0.0 264.3 jit_solution(11377146305179901576)
XLA Ops:
  6.5 0.9 constant_dynamic-slice_fusion
  7.5 3.3 %collective-permute-start.3 = (f32[64,512]{1,0:T(8,128)S(1)}, f32[64,512]{1,0:T(8,128)S(1)}, u32[]{:S(2)}, u32[]{:S(2)}) collective-permute-start(f32[64,512]{1,0:T(8,128)S(1)} %constant_dynamic-slice_fusion), channel_id=1, source_target_pairs={{2,0},{3,1},{4,2},{5,3},{6,4},{7,5},{8,6},{9,7},{10,8},{11,9},{12,... | collective-permute-start | bytes 393224 | tf_op jit(solution)/shard_map/ppermute | solution.py:229
  10.8 3.6 %collective-permute-start.2 = (f32[64,512]{1,0:T(8,128)S(1)}, f32[64,512]{1,0:T(8,128)S(1)}, u32[]{:S(2)}, u32[]{:S(2)}) collective-permute-start(f32[64,512]{1,0:T(8,128)S(1)} %constant_dynamic-slice_fusion), channel_id=1, source_target_pairs={{1,0},{2,1},{3,2},{4,3},{5,4},{6,5},{7,6},{8,7},{9,8},{10,9},{11,1... | collective-permute-start | bytes 393224 | tf_op jit(solution)/shard_map/ppermute | solution.py:229
  14.4 4.4 %collective-permute-start.1 = (f32[64,512]{1,0:T(8,128)S(1)}, f32[64,512]{1,0:T(8,128)S(1)}, u32[]{:S(2)}, u32[]{:S(2)}) collective-permute-start(f32[64,512]{1,0:T(8,128)S(1)} %constant_dynamic-slice_fusion), channel_id=1, source_target_pairs={{0,1},{1,2},{2,3},{3,4},{4,5},{5,6},{6,7},{7,8},{8,9},{9,10},{10,1... | collective-permute-start | bytes 393224 | tf_op jit(solution)/shard_map/ppermute | solution.py:229
  18.7 2.8 %collective-permute-start = (f32[64,512]{1,0:T(8,128)S(1)}, f32[64,512]{1,0:T(8,128)S(1)}, u32[]{:S(2)}, u32[]{:S(2)}) collective-permute-start(f32[64,512]{1,0:T(8,128)S(1)} %constant_dynamic-slice_fusion), channel_id=1, source_target_pairs={{0,2},{1,3},{2,4},{3,5},{4,6},{5,7},{6,8},{7,9},{8,10},{9,11},{10,... | collective-permute-start | bytes 393224 | tf_op jit(solution)/shard_map/ppermute | solution.py:229
  21.6 1.1 collective-permute-done.1
  22.6 4.5 %collective-permute-done = f32[64,512]{1,0:T(8,128)S(1)} collective-permute-done((f32[64,512]{1,0:T(8,128)S(1)}, f32[64,512]{1,0:T(8,128)S(1)}, u32[]{:S(2)}, u32[]{:S(2)}) %collective-permute-start) | collective-permute-done | bytes 131104 | tf_op jit(solution)/shard_map/ppermute | solution.py:229
  27.1 0.8 pad_maximum_fusion.4
  28.0 4.8 %dynamic-slice_bitcast_fusion = f32[8,128,1024]{2,1,0:T(8,128)} fusion(f32[8,2,128,1024]{3,2,1,0:T(8,128)} %bitcast.66, s32[]{:T(128)S(6)} %select_n.77), kind=kLoop, calls=%fused_computation | loop fusion | bytes 8388612 | tf_op jit(solution)/shard_map/jit(dynamic_index_in_dim)/squeeze | solution.py:279
  32.8 0.9 dynamic-slice_bitcast_fusion.1
  33.7 0.6 collective-permute-start.5
  34.3 5.7 %collective-permute-done.5 = f32[2,32,256]{2,1,0:T(8,128)S(1)} collective-permute-done((f32[2,32,256]{2,1,0:T(8,128)S(1)}, f32[2,32,256]{2,1,0:T(8,128)S(1)}, u32[]{:S(2)}, u32[]{:S(2)}) %collective-permute-start.5) | collective-permute-done | bytes 65568 | tf_op jit(solution)/shard_map/ppermute | solution.py:268
  40.1 6.0 %collective-permute-start.6 = (f32[2,2,32,256]{3,2,0,1:T(8,128)S(1)}, f32[2,2,32,256]{3,2,0,1:T(8,128)S(1)}, u32[]{:S(2)}, u32[]{:S(2)}) collective-permute-start(f32[2,2,32,256]{3,2,0,1:T(8,128)S(1)} %pad_maximum_fusion.5), channel_id=1, source_target_pairs={{0,224},{32,0},{64,32},{96,64},{128,96},{160,128},{192,160},{224,1... | collective-permute-start | bytes 393224 | tf_op jit(solution)/shard_map/ppermute | solution.py:217
  46.1 1.4 collective-permute-start.7
  47.4 0.4 collective-permute-start.8
  47.9 5.1 %collective-permute-start.9 = (f32[2,2,32,256]{3,2,0,1:T(8,128)S(1)}, f32[2,2,32,256]{3,2,0,1:T(8,128)S(1)}, u32[]{:S(2)}, u32[]{:S(2)}) collective-permute-start(f32[2,2,32,256]{3,2,0,1:T(8,128)S(1)} %pad_maximum_fusion.5), channel_id=1, source_target_pairs={{0,128},{32,160},{64,192},{96,224},{128,0},{160,32},{192,64},{224,... | collective-permute-start | bytes 393224 | tf_op jit(solution)/shard_map/ppermute | solution.py:217
  53.0 1.2 collective-permute-done.6
  54.3 0.4 collective-permute-start.10
  54.6 9.7 %collective-permute-done.7 = f32[2,2,32,256]{3,2,0,1:T(8,128)S(1)} collective-permute-done((f32[2,2,32,256]{3,2,0,1:T(8,128)S(1)}, f32[2,2,32,256]{3,2,0,1:T(8,128)S(1)}, u32[]{:S(2)}, u32[]{:S(2)}) %collective-permute-start.7) | collective-permute-done | bytes 131104 | tf_op jit(solution)/shard_map/ppermute | solution.py:217
  64.3 13.1 %collective-permute-done.8 = f32[2,2,32,256]{3,2,0,1:T(8,128)S(1)} collective-permute-done((f32[2,2,32,256]{3,2,0,1:T(8,128)S(1)}, f32[2,2,32,256]{3,2,0,1:T(8,128)S(1)}, u32[]{:S(2)}, u32[]{:S(2)}) %collective-permute-start.8) | collective-permute-done | bytes 131104 | tf_op jit(solution)/shard_map/ppermute | solution.py:217
  77.4 6.1 %collective-permute-done.11 = f32[2,2,32,256]{3,2,0,1:T(8,128)S(1)} collective-permute-done((f32[2,2,32,256]{3,2,0,1:T(8,128)S(1)}, f32[2,2,32,256]{3,2,0,1:T(8,128)S(1)}, u32[]{:S(2)}, u32[]{:S(2)}) %collective-permute-start.11) | collective-permute-done | bytes 131104 | tf_op jit(solution)/shard_map/ppermute | solution.py:217
  83.5 4.2 %collective-permute-done.12 = f32[2,2,32,256]{3,2,0,1:T(8,128)S(1)} collective-permute-done((f32[2,2,32,256]{3,2,0,1:T(8,128)S(1)}, f32[2,2,32,256]{3,2,0,1:T(8,128)S(1)}, u32[]{:S(2)}, u32[]{:S(2)}) %collective-permute-start.12) | collective-permute-done | bytes 131104 | tf_op jit(solution)/shard_map/ppermute | solution.py:217
  87.9 0.1 collective-permute-start.15
  88.0 2.0 collective-permute-start.13
  90.0 1.8 collective-permute-start.21
  91.8 0.2 collective-permute-start.23
  92.0 8.8 %collective-permute-done.15 = f32[16,32,256]{2,1,0:T(8,128)S(1)} collective-permute-done((f32[16,32,256]{2,1,0:T(8,128)S(1)}, f32[16,32,256]{2,1,0:T(8,128)S(1)}, u32[]{:S(2)}, u32[]{:S(2)}) %collective-permute-start.15) | collective-permute-done | bytes 524320 | tf_op jit(solution)/shard_map/ppermute | solution.py:217
  100.8 1.6 collective-permute-start.16
  102.4 0.6 collective-permute-start.14
  103.1 3.3 %collective-permute-start.17 = (f32[2,16,32,256]{3,2,1,0:T(8,128)S(1)}, f32[2,16,32,256]{3,2,1,0:T(8,128)S(1)}, u32[]{:S(2)}, u32[]{:S(2)}) collective-permute-start(f32[2,16,32,256]{3,2,1,0:T(8,128)S(1)} %pad_maximum_fusion.refs_0_.refs_6_), channel_id=1, source_target_pairs={{0,12},{4,0},{8,4},{12,8},{1,13},{5,1},{9,5},{13,9},{2,14},{6,2},{... | collective-permute-start | bytes 3145736 | tf_op jit(solution)/shard_map/ppermute | solution.py:217
  106.6 0.7 collective-permute-done.16
  107.3 5.0 %collective-permute-done.14 = f32[8,32,256]{2,1,0:T(8,128)S(1)} collective-permute-done((f32[8,32,256]{2,1,0:T(8,128)S(1)}, f32[8,32,256]{2,1,0:T(8,128)S(1)}, u32[]{:S(2)}, u32[]{:S(2)}) %collective-permute-start.14) | collective-permute-done | bytes 262176 | tf_op jit(solution)/shard_map/ppermute | solution.py:217
  112.4 2.9 %collective-permute-start.19 = (f32[2,16,32,256]{3,2,1,0:T(8,128)S(1)}, f32[2,16,32,256]{3,2,1,0:T(8,128)S(1)}, u32[]{:S(2)}, u32[]{:S(2)}) collective-permute-start(f32[2,16,32,256]{3,2,1,0:T(8,128)S(1)} %pad_maximum_fusion.1.refs_1_.refs_7_), channel_id=1, source_target_pairs={{0,4},{4,8},{8,12},{12,0},{1,5},{5,9},{9,13},{13,1},{2,6},{6,10},{... | collective-permute-start | bytes 3145736 | tf_op jit(solution)/shard_map/ppermute | solution.py:217
  115.3 1.5 collective-permute-start.24
  116.9 1.9 collective-permute-start.22
  118.7 20.9 %collective-permute-done.24 = f32[8,32,256]{2,1,0:T(8,128)S(1)} collective-permute-done((f32[8,32,256]{2,1,0:T(8,128)S(1)}, f32[8,32,256]{2,1,0:T(8,128)S(1)}, u32[]{:S(2)}, u32[]{:S(2)}) %collective-permute-start.24) | collective-permute-done | bytes 262176 | tf_op jit(solution)/shard_map/ppermute | solution.py:217
  139.7 1.1 pad_maximum_fusion.3.refs_13_.refs_19_
  140.8 0.4 collective-permute-start.27
  141.3 1.7 collective-permute-start.18
  143.0 1.6 collective-permute-start.26
  144.6 1.0 copy-done.5
  145.6 0.3 collective-permute-start.20
  145.9 0.6 slice.71
  146.8 0.2 select_reduce_fusion.1
  147.1 0.1 copy.16
  147.3 15.0 %collective-permute-done.27.refs_17_.refs_23_ = f32[2,16,32,256]{3,2,1,0:T(8,128)} collective-permute-done((f32[2,16,32,256]{3,2,1,0:T(8,128)}, f32[2,16,32,256]{3,2,1,0:T(8,128)}, u32[]{:S(2)}, u32[]{:S(2)}) %collective-permute-start.27) | collective-permute-done | bytes 1048608 | tf_op jit(solution)/shard_map/ppermute | solution.py:217
  162.2 2.0 collective-permute-start.28
  164.2 0.2 select_reduce_fusion
  164.4 0.2 convert_reduce_fusion
  164.6 2.4 collective-permute-start.29
  167.0 1.6 collective-permute-start.31
  168.6 0.1 collective-permute-done.20.refs_4_.refs_10_
  168.7 1.8 collective-permute-start.32
  170.5 0.7 broadcast_select_fusion.1
  171.2 0.7 concatenate.15.plan
  171.9 22.5 %left_products.1.left = f32[16,128,512]{2,1,0:T(8,128)} custom-call(s32[51]{0:T(128)} %concatenate.15.plan, f32[1024,512]{1,0:T(8,128)} %own.1, f32[16,4,64,512]{3,2,1,0:T(8,128)} %bitcast.67, f32[16,128,1024]{2,1,0:T(8,128)} %env_own.1, f32[8,128,1024]{2,1,0:T(8,128)} %collective-permute-done.4.env_other), custom_call_target="tpu_custom_call" | custom-call | flops 6442450944 | bytes 25165824 | tf_op jit(solution)/shard_map/left_products/pallas_call | solution.py:96
  194.4 13.0 %right_near.1.part = f32[8,128,512]{2,1,0:T(8,128)} custom-call(s32[51]{0:T(128)} %concatenate.15.plan, f32[16,128,512]{2,1,0:T(8,128)} %left_products.1.left, f32[2,16,32,256]{3,2,1,0:T(8,128)} %copy-done, f32[2,16,32,256]{3,2,1,0:T(8,128)} %copy-done.2, f32[2,16,32,256]{3,2,1,0:T(8,128)} %copy-done.3, ...), custom_call_target="tpu_custom_call" | custom-call | flops 2415919104 | bytes 18874368 | tf_op jit(solution)/shard_map/right_near/pallas_call | solution.py:182
  207.5 1.0 copy-done.6
  208.5 9.2 %right_far.1 = (f32[8,32,1024]{2,1,0:T(8,128)}, f32[8,32,1024]{2,1,0:T(8,128)}) custom-call(s32[51]{0:T(128)} %concatenate.15.plan, f32[16,128,512]{2,1,0:T(8,128)} %left_products.1.left, f32[8,128,512]{2,1,0:T(8,128)} %right_near.1.part, f32[2,16,32,256]{3,2,1,0:T(8,128)} %collective-permute-done.29.refs_0_.refs_2_, ...), custom_call_target="tpu_custom_call" | custom-call | flops 805306368 | bytes 10485760 | tf_op jit(solution)/shard_map/right_far/pallas_call | solution.py:199
  217.7 0.1 collective-permute-start.33
  217.8 2.9 %collective-permute-done.33 = f32[8,32,1024]{2,1,0:T(8,128)S(1)} collective-permute-done((f32[8,32,1024]{2,1,0:T(8,128)}, f32[8,32,1024]{2,1,0:T(8,128)S(1)}, u32[]{:S(2)}, u32[]{:S(2)}) %collective-permute-start.33) | collective-permute-done | bytes 1048608 | tf_op jit(solution)/shard_map/ppermute | solution.py:302
  220.7 1.4 add.103
  222.1 34.7 %all_to_all.5 = f32[8,32,1024]{2,1,0:T(8,128)S(1)} all-to-all(f32[8,32,1024]{2,1,0:T(8,128)S(1)} %add.103), channel_id=1, replica_groups=mesh['z'=8,'core'=2,'y'=4,'x'=4] {'z'}, dimensions={0} | all-to-all | bytes 2097152 | tf_op jit(solution)/shard_map/all_to_all | solution.py:303
  256.8 0.7 reduce_sum.49
  (73 shorter events, 1.1 us)
Async XLA Ops:
  6.5 165.3 %all-gather.3.cloned.1.call-start = ((), (), s32[]{:S(2)}) async-start(), calls=%async_computation.1 | async-start | bytes 8912896 | tf_op jit(solution)/shard_map/all_gather | solution.py:275
  7.5 14.1 %collective-permute-start.3 = (f32[64,512]{1,0:T(8,128)S(1)}, f32[64,512]{1,0:T(8,128)S(1)}, u32[]{:S(2)}, u32[]{:S(2)}) collective-permute-start(f32[64,512]{1,0:T(8,128)S(1)} %constant_dynamic-slice_fusion), channel_id=1, source_target_pairs={{2,0},{3,1},{4,2},{5,3},{6,4},{7,5},{8,6},{9,7},{10,8},{11,9},{12,... | collective-permute-start | bytes 393224 | tf_op jit(solution)/shard_map/ppermute | solution.py:229
  10.8 10.8 %collective-permute-start.2 = (f32[64,512]{1,0:T(8,128)S(1)}, f32[64,512]{1,0:T(8,128)S(1)}, u32[]{:S(2)}, u32[]{:S(2)}) collective-permute-start(f32[64,512]{1,0:T(8,128)S(1)} %constant_dynamic-slice_fusion), channel_id=1, source_target_pairs={{1,0},{2,1},{3,2},{4,3},{5,4},{6,5},{7,6},{8,7},{9,8},{10,9},{11,1... | collective-permute-start | bytes 393224 | tf_op jit(solution)/shard_map/ppermute | solution.py:229
  14.4 8.3 %collective-permute-start.1 = (f32[64,512]{1,0:T(8,128)S(1)}, f32[64,512]{1,0:T(8,128)S(1)}, u32[]{:S(2)}, u32[]{:S(2)}) collective-permute-start(f32[64,512]{1,0:T(8,128)S(1)} %constant_dynamic-slice_fusion), channel_id=1, source_target_pairs={{0,1},{1,2},{2,3},{3,4},{4,5},{5,6},{6,7},{7,8},{8,9},{9,10},{10,1... | collective-permute-start | bytes 393224 | tf_op jit(solution)/shard_map/ppermute | solution.py:229
  18.7 8.4 %collective-permute-start = (f32[64,512]{1,0:T(8,128)S(1)}, f32[64,512]{1,0:T(8,128)S(1)}, u32[]{:S(2)}, u32[]{:S(2)}) collective-permute-start(f32[64,512]{1,0:T(8,128)S(1)} %constant_dynamic-slice_fusion), channel_id=1, source_target_pairs={{0,2},{1,3},{2,4},{3,5},{4,6},{5,7},{6,8},{7,9},{8,10},{9,11},{10,... | collective-permute-start | bytes 393224 | tf_op jit(solution)/shard_map/ppermute | solution.py:229
  32.8 54.9 %collective-permute-start.4 = (f32[8,128,1024]{2,1,0:T(8,128)}, f32[8,128,1024]{2,1,0:T(8,128)}, u32[]{:S(2)}, u32[]{:S(2)}) collective-permute-start(f32[8,128,1024]{2,1,0:T(8,128)} %dynamic-slice_bitcast_fusion), channel_id=1, source_target_pairs={{0,16},{16,0},{1,17},{17,1},{2,18},{18,2},{3,19},{19,3},{4,20},{20... | collective-permute-start | bytes 12582920 | tf_op jit(solution)/shard_map/ppermute | solution.py:278
  33.7 6.3 %collective-permute-start.5 = (f32[2,32,256]{2,1,0:T(8,128)S(1)}, f32[2,32,256]{2,1,0:T(8,128)S(1)}, u32[]{:S(2)}, u32[]{:S(2)}) collective-permute-start(f32[2,32,256]{2,1,0:T(8,128)S(1)} %get-tuple-element.64), channel_id=1, source_target_pairs={{0,16},{16,0},{1,17},{17,1},{2,18},{18,2},{3,19},{19,3},{4,20},{20... | collective-permute-start | bytes 196616 | tf_op jit(solution)/shard_map/ppermute | solution.py:268
  40.1 14.2 %collective-permute-start.6 = (f32[2,2,32,256]{3,2,0,1:T(8,128)S(1)}, f32[2,2,32,256]{3,2,0,1:T(8,128)S(1)}, u32[]{:S(2)}, u32[]{:S(2)}) collective-permute-start(f32[2,2,32,256]{3,2,0,1:T(8,128)S(1)} %pad_maximum_fusion.5), channel_id=1, source_target_pairs={{0,224},{32,0},{64,32},{96,64},{128,96},{160,128},{192,160},{224,1... | collective-permute-start | bytes 393224 | tf_op jit(solution)/shard_map/ppermute | solution.py:217
  46.1 18.3 %collective-permute-start.7 = (f32[2,2,32,256]{3,2,0,1:T(8,128)S(1)}, f32[2,2,32,256]{3,2,0,1:T(8,128)S(1)}, u32[]{:S(2)}, u32[]{:S(2)}) collective-permute-start(f32[2,2,32,256]{3,2,0,1:T(8,128)S(1)} %pad_maximum_fusion.5), channel_id=1, source_target_pairs={{0,192},{32,224},{64,0},{96,32},{128,64},{160,96},{192,128},{224,1... | collective-permute-start | bytes 393224 | tf_op jit(solution)/shard_map/ppermute | solution.py:217
  47.4 30.0 %collective-permute-start.8 = (f32[2,2,32,256]{3,2,0,1:T(8,128)S(1)}, f32[2,2,32,256]{3,2,0,1:T(8,128)S(1)}, u32[]{:S(2)}, u32[]{:S(2)}) collective-permute-start(f32[2,2,32,256]{3,2,0,1:T(8,128)S(1)} %pad_maximum_fusion.5), channel_id=1, source_target_pairs={{0,160},{32,192},{64,224},{96,0},{128,32},{160,64},{192,96},{224,1... | collective-permute-start | bytes 393224 | tf_op jit(solution)/shard_map/ppermute | solution.py:217
  47.9 29.5 %collective-permute-start.9 = (f32[2,2,32,256]{3,2,0,1:T(8,128)S(1)}, f32[2,2,32,256]{3,2,0,1:T(8,128)S(1)}, u32[]{:S(2)}, u32[]{:S(2)}) collective-permute-start(f32[2,2,32,256]{3,2,0,1:T(8,128)S(1)} %pad_maximum_fusion.5), channel_id=1, source_target_pairs={{0,128},{32,160},{64,192},{96,224},{128,0},{160,32},{192,64},{224,... | collective-permute-start | bytes 393224 | tf_op jit(solution)/shard_map/ppermute | solution.py:217
  54.3 23.2 %collective-permute-start.10 = (f32[2,2,32,256]{3,2,0,1:T(8,128)S(1)}, f32[2,2,32,256]{3,2,0,1:T(8,128)S(1)}, u32[]{:S(2)}, u32[]{:S(2)}) collective-permute-start(f32[2,2,32,256]{3,2,0,1:T(8,128)S(1)} %pad_maximum_fusion.5), channel_id=1, source_target_pairs={{0,96},{32,128},{64,160},{96,192},{128,224},{160,0},{192,32},{224,... | collective-permute-start | bytes 393224 | tf_op jit(solution)/shard_map/ppermute | solution.py:217
  64.3 19.2 %collective-permute-start.11 = (f32[2,2,32,256]{3,2,0,1:T(8,128)S(1)}, f32[2,2,32,256]{3,2,0,1:T(8,128)S(1)}, u32[]{:S(2)}, u32[]{:S(2)}) collective-permute-start(f32[2,2,32,256]{3,2,0,1:T(8,128)S(1)} %pad_maximum_fusion.5), channel_id=1, source_target_pairs={{0,64},{32,96},{64,128},{96,160},{128,192},{160,224},{192,0},{224,... | collective-permute-start | bytes 393224 | tf_op jit(solution)/shard_map/ppermute | solution.py:217
  77.4 10.3 %collective-permute-start.12 = (f32[2,2,32,256]{3,2,0,1:T(8,128)S(1)}, f32[2,2,32,256]{3,2,0,1:T(8,128)S(1)}, u32[]{:S(2)}, u32[]{:S(2)}) collective-permute-start(f32[2,2,32,256]{3,2,0,1:T(8,128)S(1)} %pad_maximum_fusion.5), channel_id=1, source_target_pairs={{0,32},{32,64},{64,96},{96,128},{128,160},{160,192},{192,224},{224... | collective-permute-start | bytes 393224 | tf_op jit(solution)/shard_map/ppermute | solution.py:217
  87.9 12.9 %collective-permute-start.15 = (f32[16,32,256]{2,1,0:T(8,128)S(1)}, f32[16,32,256]{2,1,0:T(8,128)S(1)}, u32[]{:S(2)}, u32[]{:S(2)}) collective-permute-start(f32[16,32,256]{2,1,0:T(8,128)S(1)} %get-tuple-element.48), channel_id=1, source_target_pairs={{0,1},{1,2},{2,3},{3,0},{4,5},{5,6},{6,7},{7,4},{8,9},{9,10},{10,1... | collective-permute-start | bytes 1572872 | tf_op jit(solution)/shard_map/ppermute | solution.py:217
  88.0 14.4 %collective-permute-start.13 = (f32[16,32,256]{2,1,0:T(8,128)S(1)}, f32[16,32,256]{2,1,0:T(8,128)S(1)}, u32[]{:S(2)}, u32[]{:S(2)}) collective-permute-start(f32[16,32,256]{2,1,0:T(8,128)S(1)} %get-tuple-element.48), channel_id=1, source_target_pairs={{0,3},{1,0},{2,1},{3,2},{4,7},{5,4},{6,5},{7,6},{8,11},{9,8},{10,9... | collective-permute-start | bytes 1572872 | tf_op jit(solution)/shard_map/ppermute | solution.py:217
  90.0 16.4 %collective-permute-start.21 = (f32[16,32,256]{2,1,0:T(8,128)S(1)}, f32[16,32,256]{2,1,0:T(8,128)S(1)}, u32[]{:S(2)}, u32[]{:S(2)}) collective-permute-start(f32[16,32,256]{2,1,0:T(8,128)S(1)} %get-tuple-element.47), channel_id=1, source_target_pairs={{0,12},{4,0},{8,4},{12,8},{1,13},{5,1},{9,5},{13,9},{2,14},{6,2},{... | collective-permute-start | bytes 1572872 | tf_op jit(solution)/shard_map/ppermute | solution.py:217
  91.8 23.5 %collective-permute-start.23 = (f32[16,32,256]{2,1,0:T(8,128)S(1)}, f32[16,32,256]{2,1,0:T(8,128)S(1)}, u32[]{:S(2)}, u32[]{:S(2)}) collective-permute-start(f32[16,32,256]{2,1,0:T(8,128)S(1)} %get-tuple-element.47), channel_id=1, source_target_pairs={{0,4},{4,8},{8,12},{12,0},{1,5},{5,9},{9,13},{13,1},{2,6},{6,10},{... | collective-permute-start | bytes 1572872 | tf_op jit(solution)/shard_map/ppermute | solution.py:217
  100.8 6.5 %collective-permute-start.16 = (f32[8,32,256]{2,1,0:T(8,128)S(1)}, f32[8,32,256]{2,1,0:T(8,128)S(1)}, u32[]{:S(2)}, u32[]{:S(2)}) collective-permute-start(f32[8,32,256]{2,1,0:T(8,128)S(1)} %slice.95), channel_id=1, source_target_pairs={{0,1},{1,2},{2,3},{3,0},{4,5},{5,6},{6,7},{7,4},{8,9},{9,10},{10,1... | collective-permute-start | bytes 786440 | tf_op jit(solution)/shard_map/ppermute | solution.py:217
  102.4 9.9 %collective-permute-start.14 = (f32[8,32,256]{2,1,0:T(8,128)S(1)}, f32[8,32,256]{2,1,0:T(8,128)S(1)}, u32[]{:S(2)}, u32[]{:S(2)}) collective-permute-start(f32[8,32,256]{2,1,0:T(8,128)S(1)} %slice.94), channel_id=1, source_target_pairs={{0,3},{1,0},{2,1},{3,2},{4,7},{5,4},{6,5},{7,6},{8,11},{9,8},{10,9... | collective-permute-start | bytes 786440 | tf_op jit(solution)/shard_map/ppermute | solution.py:217
  103.1 41.5 %copy-start = (f32[2,16,32,256]{3,2,1,0:T(8,128)}, f32[2,16,32,256]{3,2,1,0:T(8,128)S(1)}, u32[]{:S(2)}) copy-start(f32[2,16,32,256]{3,2,1,0:T(8,128)S(1)} %pad_maximum_fusion.refs_0_.refs_6_) | copy-start | bytes 3145732
  103.1 38.1 %collective-permute-start.17 = (f32[2,16,32,256]{3,2,1,0:T(8,128)S(1)}, f32[2,16,32,256]{3,2,1,0:T(8,128)S(1)}, u32[]{:S(2)}, u32[]{:S(2)}) collective-permute-start(f32[2,16,32,256]{3,2,1,0:T(8,128)S(1)} %pad_maximum_fusion.refs_0_.refs_6_), channel_id=1, source_target_pairs={{0,12},{4,0},{8,4},{12,8},{1,13},{5,1},{9,5},{13,9},{2,14},{6,2},{... | collective-permute-start | bytes 3145736 | tf_op jit(solution)/shard_map/ppermute | solution.py:217
  106.5 87.9 %copy-start.1 = (f32[2,16,32,256]{3,2,1,0:T(8,128)}, f32[2,16,32,256]{3,2,1,0:T(8,128)S(1)}, u32[]{:S(2)}) copy-start(f32[2,16,32,256]{3,2,1,0:T(8,128)S(1)} %pad_maximum_fusion.2.refs_12_.refs_18_) | copy-start | bytes 3145732
  106.5 39.4 %copy-start.8 = (s32[128]{0:T(128)S(1)}, s32[128]{0:T(128)}, u32[]{:S(2)}) copy-start(s32[128]{0:T(128)} %param.9) | copy-start | bytes 1540
  106.5 40.3 %copy-start.7 = (s32[16,16]{1,0:T(8,128)S(1)}, s32[16,16]{1,0:T(8,128)}, u32[]{:S(2)}) copy-start(s32[16,16]{1,0:T(8,128)} %param.11) | copy-start | bytes 3076
  106.5 57.7 %copy-start.9 = (s32[32]{0:T(128)S(1)}, s32[32]{0:T(128)}, u32[]{:S(2)}) copy-start(s32[32]{0:T(128)} %param.10) | copy-start | bytes 388
  106.5 36.5 %collective-permute-start.25 = (f32[2,16,32,256]{3,2,1,0:T(8,128)S(1)}, f32[2,16,32,256]{3,2,1,0:T(8,128)S(1)}, u32[]{:S(2)}, u32[]{:S(2)}) collective-permute-start(f32[2,16,32,256]{3,2,1,0:T(8,128)S(1)} %pad_maximum_fusion.2.refs_12_.refs_18_), channel_id=1, source_target_pairs={{0,3},{1,0},{2,1},{3,2},{4,7},{5,4},{6,5},{7,6},{8,11},{9,8},{10,9... | collective-permute-start | bytes 3145736 | tf_op jit(solution)/shard_map/ppermute | solution.py:217
  112.4 82.0 %copy-start.2 = (f32[2,16,32,256]{3,2,1,0:T(8,128)}, f32[2,16,32,256]{3,2,1,0:T(8,128)S(1)}, u32[]{:S(2)}) copy-start(f32[2,16,32,256]{3,2,1,0:T(8,128)S(1)} %pad_maximum_fusion.1.refs_1_.refs_7_) | copy-start | bytes 3145732
  112.4 32.2 %collective-permute-start.19 = (f32[2,16,32,256]{3,2,1,0:T(8,128)S(1)}, f32[2,16,32,256]{3,2,1,0:T(8,128)S(1)}, u32[]{:S(2)}, u32[]{:S(2)}) collective-permute-start(f32[2,16,32,256]{3,2,1,0:T(8,128)S(1)} %pad_maximum_fusion.1.refs_1_.refs_7_), channel_id=1, source_target_pairs={{0,4},{4,8},{8,12},{12,0},{1,5},{5,9},{9,13},{13,1},{2,6},{6,10},{... | collective-permute-start | bytes 3145736 | tf_op jit(solution)/shard_map/ppermute | solution.py:217
  115.3 24.3 %collective-permute-start.24 = (f32[8,32,256]{2,1,0:T(8,128)S(1)}, f32[8,32,256]{2,1,0:T(8,128)S(1)}, u32[]{:S(2)}, u32[]{:S(2)}) collective-permute-start(f32[8,32,256]{2,1,0:T(8,128)S(1)} %slice.97), channel_id=1, source_target_pairs={{0,4},{4,8},{8,12},{12,0},{1,5},{5,9},{9,13},{13,1},{2,6},{6,10},{... | collective-permute-start | bytes 786440 | tf_op jit(solution)/shard_map/ppermute | solution.py:217
  116.9 22.8 %collective-permute-start.22 = (f32[8,32,256]{2,1,0:T(8,128)S(1)}, f32[8,32,256]{2,1,0:T(8,128)S(1)}, u32[]{:S(2)}, u32[]{:S(2)}) collective-permute-start(f32[8,32,256]{2,1,0:T(8,128)S(1)} %slice.96), channel_id=1, source_target_pairs={{0,12},{4,0},{8,4},{12,8},{1,13},{5,1},{9,5},{13,9},{2,14},{6,2},{... | collective-permute-start | bytes 786440 | tf_op jit(solution)/shard_map/ppermute | solution.py:217
  140.8 21.4 %collective-permute-start.27 = (f32[2,16,32,256]{3,2,1,0:T(8,128)}, f32[2,16,32,256]{3,2,1,0:T(8,128)}, u32[]{:S(2)}, u32[]{:S(2)}) collective-permute-start(f32[2,16,32,256]{3,2,1,0:T(8,128)} %pad_maximum_fusion.3.refs_13_.refs_19_), channel_id=1, source_target_pairs={{0,1},{1,2},{2,3},{3,0},{4,5},{5,6},{6,7},{7,4},{8,9},{9,10},{10,1... | collective-permute-start | bytes 3145736 | tf_op jit(solution)/shard_map/ppermute | solution.py:217
  141.3 3.3 %copy-start.3 = (f32[2,16,32,256]{3,2,1,0:T(8,128)}, f32[2,16,32,256]{3,2,1,0:T(8,128)S(1)}, u32[]{:S(2)}) copy-start(f32[2,16,32,256]{3,2,1,0:T(8,128)S(1)} %collective-permute-done.17.refs_2_.refs_8_) | copy-start | bytes 3145732
  141.3 25.7 %collective-permute-start.18 = (f32[2,16,32,256]{3,2,1,0:T(8,128)S(1)}, f32[2,16,32,256]{3,2,1,0:T(8,128)}, u32[]{:S(2)}, u32[]{:S(2)}) collective-permute-start(f32[2,16,32,256]{3,2,1,0:T(8,128)S(1)} %pad_maximum_fusion.1.refs_1_.refs_7_), channel_id=1, source_target_pairs={{0,12},{4,0},{8,4},{12,8},{1,13},{5,1},{9,5},{13,9},{2,14},{6,2},{... | collective-permute-start | bytes 3145736 | tf_op jit(solution)/shard_map/ppermute | solution.py:217
  143.0 1.6 copy-start.4
  143.0 25.5 %collective-permute-start.26 = (f32[2,16,32,256]{3,2,1,0:T(8,128)}, f32[2,16,32,256]{3,2,1,0:T(8,128)}, u32[]{:S(2)}, u32[]{:S(2)}) collective-permute-start(f32[2,16,32,256]{3,2,1,0:T(8,128)} %pad_maximum_fusion.3.refs_13_.refs_19_), channel_id=1, source_target_pairs={{0,3},{1,0},{2,1},{3,2},{4,7},{5,4},{6,5},{7,6},{8,11},{9,8},{10,9... | collective-permute-start | bytes 3145736 | tf_op jit(solution)/shard_map/ppermute | solution.py:217
  144.6 1.0 copy-start.5
  145.6 23.1 %collective-permute-start.20 = (f32[2,16,32,256]{3,2,1,0:T(8,128)S(1)}, f32[2,16,32,256]{3,2,1,0:T(8,128)}, u32[]{:S(2)}, u32[]{:S(2)}) collective-permute-start(f32[2,16,32,256]{3,2,1,0:T(8,128)S(1)} %pad_maximum_fusion.refs_0_.refs_6_), channel_id=1, source_target_pairs={{0,4},{4,8},{8,12},{12,0},{1,5},{5,9},{9,13},{13,1},{2,6},{6,10},{... | collective-permute-start | bytes 3145736 | tf_op jit(solution)/shard_map/ppermute | solution.py:217
  162.2 32.2 %collective-permute-start.28 = (f32[2,16,32,256]{3,2,1,0:T(8,128)S(1)}, f32[2,16,32,256]{3,2,1,0:T(8,128)}, u32[]{:S(2)}, u32[]{:S(2)}) collective-permute-start(f32[2,16,32,256]{3,2,1,0:T(8,128)S(1)} %pad_maximum_fusion.2.refs_12_.refs_18_), channel_id=1, source_target_pairs={{0,1},{1,2},{2,3},{3,0},{4,5},{5,6},{6,7},{7,4},{8,9},{9,10},{10,1... | collective-permute-start | bytes 3145736 | tf_op jit(solution)/shard_map/ppermute | solution.py:217
  164.6 42.9 %collective-permute-start.29 = (f32[2,16,32,256]{3,2,1,0:T(8,128)}, f32[2,16,32,256]{3,2,1,0:T(8,128)}, u32[]{:S(2)}, u32[]{:S(2)}) collective-permute-start(f32[2,16,32,256]{3,2,1,0:T(8,128)} %copy-done.3), channel_id=1, source_target_pairs={{0,12},{4,0},{8,4},{12,8},{1,13},{5,1},{9,5},{13,9},{2,14},{6,2},{... | collective-permute-start | bytes 3145736 | tf_op jit(solution)/shard_map/ppermute | solution.py:217
  167.0 40.5 %collective-permute-start.31 = (f32[2,16,32,256]{3,2,1,0:T(8,128)}, f32[2,16,32,256]{3,2,1,0:T(8,128)}, u32[]{:S(2)}, u32[]{:S(2)}) collective-permute-start(f32[2,16,32,256]{3,2,1,0:T(8,128)} %copy-done.4), channel_id=1, source_target_pairs={{0,3},{1,0},{2,1},{3,2},{4,7},{5,4},{6,5},{7,6},{8,11},{9,8},{10,9... | collective-permute-start | bytes 3145736 | tf_op jit(solution)/shard_map/ppermute | solution.py:217
  168.5 39.0 %collective-permute-start.30 = (f32[2,16,32,256]{3,2,1,0:T(8,128)}, f32[2,16,32,256]{3,2,1,0:T(8,128)}, u32[]{:S(2)}, u32[]{:S(2)}) collective-permute-start(f32[2,16,32,256]{3,2,1,0:T(8,128)} %copy-done.5), channel_id=1, source_target_pairs={{0,4},{4,8},{8,12},{12,0},{1,5},{5,9},{9,13},{13,1},{2,6},{6,10},{... | collective-permute-start | bytes 3145736 | tf_op jit(solution)/shard_map/ppermute | solution.py:217
  168.7 38.8 %collective-permute-start.32 = (f32[2,16,32,256]{3,2,1,0:T(8,128)}, f32[2,16,32,256]{3,2,1,0:T(8,128)S(1)}, u32[]{:S(2)}, u32[]{:S(2)}) collective-permute-start(f32[2,16,32,256]{3,2,1,0:T(8,128)} %collective-permute-done.27.refs_17_.refs_23_), channel_id=1, source_target_pairs={{0,1},{1,2},{2,3},{3,0},{4,5},{5,6},{6,7},{7,4},{8,9},{9,10},{10,1... | collective-permute-start | bytes 3145736 | tf_op jit(solution)/shard_map/ppermute | solution.py:217
  207.5 1.0 copy-start.6
  217.7 3.0 %collective-permute-start.33 = (f32[8,32,1024]{2,1,0:T(8,128)}, f32[8,32,1024]{2,1,0:T(8,128)S(1)}, u32[]{:S(2)}, u32[]{:S(2)}) collective-permute-start(f32[8,32,1024]{2,1,0:T(8,128)} %get-tuple-element.42), channel_id=1, source_target_pairs={{0,16},{16,0},{1,17},{17,1},{2,18},{18,2},{3,19},{19,3},{4,20},{20... | collective-permute-start | bytes 3145736 | tf_op jit(solution)/shard_map/ppermute | solution.py:302
Sparse Core Ops, SparseCore 0:
  28.1 81.0 all-gather.2

commit v4 on v1

--- a/solution.py
+++ b/solution.py
@@ -17,9 +17,12 @@
 ROWS = TILE_DEV * TILE
 PART = ROWS // HOMES
 SUB = 32
+DIRECT = 128
+PACE = (COLS - DIRECT) // 4
+STRIP = PACE // 4
 VMEM = 56 * 1024 * 1024
 
-START, COUNT, TERM, CORE, PX, PY = 0, 16, 32, 48, 49, 50
+START, COUNT, TERM, SLOT, CORE, PX, PY = 0, 16, 32, 48, 64, 65, 66
 
 
 def split(value):
@@ -105,28 +108,26 @@
     )(plan, own, near, env, env_other)
 
 
-def right_kernel(plan, left, *refs):
-    parts, (keep, send, total, *halves) = refs[:10], refs[10:]
+def right_kernel(plan, left, direct, *refs):
+    parts, (keep, send, total, whole) = refs[:10], refs[10:]
     pair = pl.program_id(0)
     core, x, y = plan[CORE], plan[PX], plan[PY]
-    value = []
     for half, (major, minor) in enumerate(((y, x), (x, y))):
         here, after, across_low, across_high, before = parts[5 * half : 5 * half + 5]
-        high, low = halves[2 * half : 2 * half + 2]
         pieces = [
             [here.at[i] for i in range(4)],
             [after.at[i] for i in range(4)],
             [across_low.at[0], across_low.at[1], across_high.at[0], across_high.at[1]],
             [before.at[i] for i in range(4)],
         ]
-        lefts = []
         for r in range(4):
             for i in range(4):
-                spot = pl.ds(pl.multiple_of(r * TILE + ((minor + i) % 4) * SUB, SUB), SUB)
-                high[spot, :], low[spot, :] = split(pieces[r][i][0])
-            lefts.append(left[0, :, pl.ds(pl.multiple_of(((major + r) % 4) * TILE, TILE), TILE)])
-        value.append(product(jnp.concatenate(lefts, axis=1), high[...], low[...]))
-    value = jnp.concatenate(value, axis=1)
+                row = ((major + r) % 4) * PACE + ((minor + i) % 4) * STRIP
+                spot = pl.ds(pl.multiple_of(row, 8), STRIP)
+                whole[spot, half * HALF : (half + 1) * HALF] = pieces[r][i][0]
+    whole[COLS - DIRECT :, :] = direct[0]
+    high, low = split(whole[...])
+    value = product(left[0], high, low)
 
     @pl.when(pair % 2 == 0)
     def _():
@@ -139,20 +140,25 @@
         send[...] = jnp.where(core == 0, turned[:, 1], turned[:, 0])
 
 
-def right_products(plan, left, parts):
+def right_products(plan, left, direct, parts):
     def part_spec(part):
-        return pl.BlockSpec((part.shape[0], 1, SUB, HALF), lambda p, plan: (0, plan[TERM + p], 0, 0))
+        return pl.BlockSpec((part.shape[0], 1, STRIP, HALF), lambda p, plan: (0, plan[TERM + p], 0, 0))
 
     out = jax.ShapeDtypeStruct((HOMES // 2, SUB, ROWS), jnp.float32)
     out_spec = pl.BlockSpec((HOMES // 2, SUB, TILE), lambda p, plan: (0, 0, p // 2))
     grid = pltpu.PrefetchScalarGridSpec(
         num_scalar_prefetch=1,
         grid=(PAIRS,),
-        in_specs=[pl.BlockSpec((1, TILE, COLS), lambda p, plan: (p, 0, 0))]
+        in_specs=[
+            pl.BlockSpec((1, TILE, COLS), lambda p, plan: (p, 0, 0)),
+            pl.BlockSpec((1, DIRECT, COLS), lambda p, plan: (plan[SLOT + p], 0, 0)),
+        ]
         + [part_spec(part) for part in parts],
         out_specs=[out_spec, out_spec],
-        scratch_shapes=[pltpu.VMEM((TILE, COLS), jnp.float32)]
-        + [pltpu.VMEM((COLS, HALF), jnp.bfloat16)] * 4,
+        scratch_shapes=[
+            pltpu.VMEM((TILE, COLS), jnp.float32),
+            pltpu.VMEM((COLS, COLS), jnp.float32),
+        ],
     )
     return pl.pallas_call(
         right_kernel,
@@ -163,7 +169,7 @@
             flops=6 * PAIRS * TILE * COLS * COLS, bytes_accessed=22 << 20, transcendentals=0
         ),
         name="right_products",
-    )(plan, left, *parts)
+    )(plan, left, direct, *parts)
 
 
 def ring(value, axis, steps):
@@ -204,7 +210,8 @@
     count = jnp.sum((tile_sector[None, :] == source[:, None]).astype(jnp.int32), axis=1)
     first = jnp.where(usable, first - (base - REACH * TILE_DEV), 0)
     count = jnp.where(usable, count, 0)
-    return jnp.concatenate([first, count, owner, jnp.stack([core, x, y])]).astype(jnp.int32)
+    slot = (owner // 2) * 2 + (owner + core) % 2
+    return jnp.concatenate([first, count, owner, slot, jnp.stack([core, x, y])]).astype(jnp.int32)
 
 
 def on_device(wavefunction, env_blocks, right_env, tile_sector, term_charge, block_home):
@@ -213,13 +220,19 @@
     home = 2 * z + core
     swap = [(0, 1), (1, 0)]
 
-    by_y = lax.dynamic_slice(right_env, (0, y * TILE + x * SUB, 0), (2, SUB, HALF))
-    by_x = lax.dynamic_slice(right_env, (0, x * TILE + y * SUB, HALF), (2, SUB, HALF))
+    by_y = lax.dynamic_slice(right_env, (0, y * PACE + x * STRIP, 0), (2, STRIP, HALF))
+    by_x = lax.dynamic_slice(right_env, (0, x * PACE + y * STRIP, HALF), (2, STRIP, HALF))
     column = lax.all_gather(jnp.stack([by_y, by_x], axis=1), ("z", "core"))
 
     strip = lax.dynamic_slice(wavefunction, (home * PART, 0), (PART, COLS))
     near = jnp.stack([wide_shift(strip, steps) for steps in (2, 1, -1, -2)])
+    near, column = lax.optimization_barrier((near, column))
     near = lax.all_gather(near, ("z", "core"))
+
+    rest = right_env[:, COLS - DIRECT :, :]
+    kept = lax.dynamic_index_in_dim(rest, core, axis=0, keepdims=False)
+    given = lax.dynamic_index_in_dim(rest, 1 - core, axis=0, keepdims=False)
+    direct = jnp.stack([kept, lax.ppermute(given, "core", swap)])
 
     paired = env_blocks.reshape(TILE_DEV, 2, TILE, SRC)
     env_other = lax.ppermute(
@@ -231,11 +244,14 @@
     parts = []
     for at, (first, then) in enumerate((("x", "y"), ("y", "x"))):
         here, after, low, high, before = around(mine[:, at], first, HOMES // 2)
+        if at == 0:
+            direct, after = lax.optimization_barrier((direct, after))
+            direct = lax.all_gather(direct, "z").reshape(HOMES, DIRECT, COLS)
         gathered = jnp.stack([here, after, jnp.concatenate([low, high], axis=0), before])
         parts += around(gathered, then, 2)
 
     left = left_products(plan, wavefunction, near, env_blocks, env_other)
-    keep, send = right_products(plan, left, parts)
+    keep, send = right_products(plan, left, direct, parts)
     total = keep + lax.ppermute(send, "core", swap)
     shares = lax.all_to_all(total, "z", split_axis=0, concat_axis=0, tiled=True)
     shares = shares.reshape(HOMES // 2, SUB, ROWS)

time: 235 us -> 235 us (level)
  the two profiles are of different devices: /device:TPU:6 before, /device:TPU:30 now
where the time goes in v4:
time: 235 us; the launch traced here: 230 us
  waiting for transfers between devices  89.2 us (38%)
  Pallas kernels  40.9 us (17%)
  blocking collectives  33.3 us (14%)
  starting transfers between devices  28.7 us (12%)
  local copies, waits for them, and re-layouts  18.6 us (8%)
  between operations  13.4 us (6%)
  other arithmetic  5.95 us (3%)
    ppermute x16, waiting for transfers between devices, ring(): lax.ppermute(value, axis, [(i, (i - steps) % count) for i in range(count)])  51.6 us
    all_to_all x1, blocking collectives, on_device(): shares = lax.all_to_all(total, 'z', split_axis=0, concat_axis=0, tiled=True)  33.3 us
    all_gather x1, waiting for transfers between devices, on_device(): column = lax.all_gather(jnp.stack([by_y, by_x], axis=1), ('z', 'core'))  24.6 us
    pallas_call x1, Pallas kernels, left_products(): pl.pallas_call(left_kernel, grid_spec=grid, out_shape=jax.ShapeDtypeStruc...  22.4 us
    ppermute x16, starting transfers between devices, ring(): lax.ppermute(value, axis, [(i, (i - steps) % count) for i in range(count)])  20.7 us
    pallas_call x1, Pallas kernels, right_products(): pl.pallas_call(right_kernel, grid_spec=grid, out_shape=[out, out], compil...  18.6 us
    ppermute x4, waiting for transfers between devices, wide_shift(): lax.ppermute(value, ('y', 'x'), [(i, i + steps) for i in range(max(0, -st...  8.55 us
    ppermute x4, starting transfers between devices, wide_shift(): lax.ppermute(value, ('y', 'x'), [(i, i + steps) for i in range(max(0, -st...  7.74 us
  transfers between devices with their start and end apart: 26, of which 11 were waited for; matrix products, arithmetic and copies ran while one was open for 8% of the time, Pallas kernels for 10%

profile of v4, /device:TPU:30, one launch (start us, length us, event | category | flops | bytes accessed | tf_op | source)
XLA Modules:
  0.0 230.1 jit_solution(15027534258833875878)
XLA Ops:
  6.5 0.8 dynamic-slice_bitcast_fusion.3
  7.4 0.6 pad_maximum_fusion.4
  8.1 0.9 constant_dynamic-slice_fusion.1
  9.0 3.3 %collective-permute-start.3 = (f32[64,512]{1,0:T(8,128)S(1)}, f32[64,512]{1,0:T(8,128)S(1)}, u32[]{:S(2)}, u32[]{:S(2)}) collective-permute-start(f32[64,512]{1,0:T(8,128)S(1)} %constant_dynamic-slice_fusion.1), channel_id=1, source_target_pairs={{2,0},{3,1},{4,2},{5,3},{6,4},{7,5},{8,6},{9,7},{10,8},{11,9},{12,... | collective-permute-start | bytes 393224 | tf_op jit(solution)/shard_map/ppermute | solution.py:189
  12.3 1.8 collective-permute-start.2
  14.2 1.3 collective-permute-start.1
  15.5 1.3 collective-permute-start
  16.8 1.1 collective-permute-done.2
  17.9 3.5 %collective-permute-done.1 = f32[64,512]{1,0:T(8,128)S(1)} collective-permute-done((f32[64,512]{1,0:T(8,128)S(1)}, f32[64,512]{1,0:T(8,128)S(1)}, u32[]{:S(2)}, u32[]{:S(2)}) %collective-permute-start.1) | collective-permute-done | bytes 131104 | tf_op jit(solution)/shard_map/ppermute | solution.py:189
  21.4 4.0 %collective-permute-done = f32[64,512]{1,0:T(8,128)S(1)} collective-permute-done((f32[64,512]{1,0:T(8,128)S(1)}, f32[64,512]{1,0:T(8,128)S(1)}, u32[]{:S(2)}, u32[]{:S(2)}) %collective-permute-start) | collective-permute-done | bytes 131104 | tf_op jit(solution)/shard_map/ppermute | solution.py:189
  25.4 0.8 pad_maximum_fusion.2
  26.2 24.6 %all-gather.7.cloned.1.call-done = f32[32,2,24,256]{3,2,1,0:T(8,128)} async-done(((f32[2,2,24,256]{3,2,1,0:T(8,128)}), f32[32,2,24,256]{3,2,1,0:T(8,128)}) %all-gather.7.cloned.1.call-update) | async-done | bytes 1572880 | tf_op jit(solution)/shard_map/all_gather | solution.py:225
  50.9 1.3 copy-done.5
  52.3 0.1 slice_bitcast_fusion.1
  52.4 1.1 collective-permute-start.6
  53.6 0.1 collective-permute-start.5
  53.7 1.5 collective-permute-done.5
  55.2 0.8 pad_maximum_fusion.3
  56.1 8.9 %collective-permute-done.6 = f32[16,24,256]{2,1,0:T(8,128)S(1)} collective-permute-done((f32[16,24,256]{2,1,0:T(8,128)S(1)}, f32[16,24,256]{2,1,0:T(8,128)S(1)}, u32[]{:S(2)}, u32[]{:S(2)}) %collective-permute-start.6) | collective-permute-done | bytes 393248 | tf_op jit(solution)/shard_map/ppermute | solution.py:177
  65.0 4.7 %dynamic-slice_bitcast_fusion = f32[8,128,1024]{2,1,0:T(8,128)} fusion(f32[8,2,128,1024]{3,2,1,0:T(8,128)} %bitcast.43, s32[]{:T(128)S(6)} %select_n.71), kind=kLoop, calls=%fused_computation | loop fusion | bytes 8388612 | tf_op jit(solution)/shard_map/jit(dynamic_index_in_dim)/squeeze | solution.py:239
  69.7 0.7 collective-permute-start.16
  70.5 1.3 collective-permute-start.14
  71.8 9.5 %collective-permute-done.8 = f32[16,24,256]{2,1,0:T(8,128)S(1)} collective-permute-done((f32[16,24,256]{2,1,0:T(8,128)S(1)}, f32[16,24,256]{2,1,0:T(8,128)S(1)}, u32[]{:S(2)}, u32[]{:S(2)}) %collective-permute-start.8) | collective-permute-done | bytes 393248 | tf_op jit(solution)/shard_map/ppermute | solution.py:177
  81.3 1.6 collective-permute-start.9
  82.9 0.6 collective-permute-start.7
  83.5 0.8 collective-permute-start.17
  84.3 1.4 collective-permute-start.15
  85.7 2.3 collective-permute-done.9
  88.0 2.7 %collective-permute-done.7 = f32[8,24,256]{2,1,0:T(8,128)S(1)} collective-permute-done((f32[8,24,256]{2,1,0:T(8,128)S(1)}, f32[8,24,256]{2,1,0:T(8,128)S(1)}, u32[]{:S(2)}, u32[]{:S(2)}) %collective-permute-start.7) | collective-permute-done | bytes 196640 | tf_op jit(solution)/shard_map/ppermute | solution.py:177
  90.8 0.1 pad_maximum_fusion.refs_0_
  90.9 1.1 collective-permute-start.10
  92.0 2.2 collective-permute-start.12
  94.3 0.1 pad_maximum_fusion.1.refs_5_
  94.4 0.1 collective-permute-start.18
  94.5 3.2 %collective-permute-start.20 = (f32[4,16,24,256]{3,2,1,0:T(8,128)S(1)}, f32[4,16,24,256]{3,2,1,0:T(8,128)}, u32[]{:S(2)}, u32[]{:S(2)}) collective-permute-start(f32[4,16,24,256]{3,2,1,0:T(8,128)S(1)} %pad_maximum_fusion.1.refs_5_), channel_id=1, source_target_pairs={{0,1},{1,2},{2,3},{3,0},{4,5},{5,6},{6,7},{7,4},{8,9},{9,10},{10,1... | collective-permute-start | bytes 4718600 | tf_op jit(solution)/shard_map/ppermute | solution.py:177
  97.8 0.6 slice.44
  98.3 0.1 dynamic_slice.27
  98.4 0.1 broadcast_in_dim.28
  98.5 0.1 reshape.36
  98.6 0.1 copy.17
  98.7 0.2 select_reduce_fusion.1
  98.9 0.1 copy.18
  98.9 0.1 reshape.38
  99.1 0.2 select_reduce_fusion
  99.3 0.2 convert_reduce_fusion
  99.4 28.1 %collective-permute-done.10.refs_1_ = f32[4,16,24,256]{3,2,1,0:T(8,128)} collective-permute-done((f32[4,16,24,256]{3,2,1,0:T(8,128)S(1)}, f32[4,16,24,256]{3,2,1,0:T(8,128)}, u32[]{:S(2)}, u32[]{:S(2)}) %collective-permute-start.10) | collective-permute-done | bytes 1572896 | tf_op jit(solution)/shard_map/ppermute | solution.py:177
  127.6 2.1 slice.61
  129.7 2.1 slice.62
  131.8 3.2 %collective-permute-start.13 = (f32[2,16,24,256]{3,2,1,0:T(8,128)}, f32[2,16,24,256]{3,2,1,0:T(8,128)S(1)}, u32[]{:S(2)}, u32[]{:S(2)}) collective-permute-start(f32[2,16,24,256]{3,2,1,0:T(8,128)} %slice.62), channel_id=1, source_target_pairs={{0,4},{4,8},{8,12},{12,0},{1,5},{5,9},{9,13},{13,1},{2,6},{6,10},{... | collective-permute-start | bytes 2359304 | tf_op jit(solution)/shard_map/ppermute | solution.py:177
  135.0 2.1 slice.66
  137.1 1.2 slice.67
  138.3 3.3 %collective-permute-start.21 = (f32[2,16,24,256]{3,2,1,0:T(8,128)S(1)}, f32[2,16,24,256]{3,2,1,0:T(8,128)S(1)}, u32[]{:S(2)}, u32[]{:S(2)}) collective-permute-start(f32[2,16,24,256]{3,2,1,0:T(8,128)S(1)} %slice.67), channel_id=1, source_target_pairs={{0,1},{1,2},{2,3},{3,0},{4,5},{5,6},{6,7},{7,4},{8,9},{9,10},{10,1... | collective-permute-start | bytes 2359304 | tf_op jit(solution)/shard_map/ppermute | solution.py:177
  141.6 0.6 broadcast_select_fusion.1
  142.3 0.6 concatenate.9.plan
  142.9 22.4 %left_products.1.left = f32[16,128,512]{2,1,0:T(8,128)} custom-call(s32[67]{0:T(128)} %concatenate.9.plan, f32[1024,512]{1,0:T(8,128)} %own.1, f32[16,4,64,512]{3,2,1,0:T(8,128)} %bitcast.44, f32[16,128,1024]{2,1,0:T(8,128)} %env_own.1, f32[8,128,1024]{2,1,0:T(8,128)} %collective-permute-done.4.env_other), custom_call_target="tpu_custom_call" | custom-call | flops 6442450944 | bytes 25165824 | tf_op jit(solution)/shard_map/left_products/pallas_call | solution.py:99
  165.4 0.8 copy-done.2
  166.2 0.3 copy-done.3
  166.5 0.3 copy-done.4
  166.7 18.6 %right_products.1 = (f32[8,32,1024]{2,1,0:T(8,128)}, f32[8,32,1024]{2,1,0:T(8,128)}) custom-call(s32[67]{0:T(128)} %concatenate.9.plan, f32[16,128,512]{2,1,0:T(8,128)} %left_products.1.left, f32[16,128,512]{2,1,0:T(8,128)} %all-gather.11.cloned.1.call-done.direct, f32[4,16,24,256]{3,2,1,0:T(8,128)} %copy-done, ...), custom_call_target="tpu_custom_call" | custom-call | flops 3221225472 | bytes 23068672 | tf_op jit(solution)/shard_map/right_products/pallas_call | solution.py:163
  185.3 0.1 collective-permute-start.22
  185.4 2.9 %collective-permute-done.22 = f32[8,32,1024]{2,1,0:T(8,128)S(1)} collective-permute-done((f32[8,32,1024]{2,1,0:T(8,128)}, f32[8,32,1024]{2,1,0:T(8,128)S(1)}, u32[]{:S(2)}, u32[]{:S(2)}) %collective-permute-start.22) | collective-permute-done | bytes 1048608 | tf_op jit(solution)/shard_map/ppermute | solution.py:255
  188.2 1.4 add.99
  189.6 33.3 %all_to_all.5 = f32[8,32,1024]{2,1,0:T(8,128)S(1)} all-to-all(f32[8,32,1024]{2,1,0:T(8,128)S(1)} %add.99), channel_id=1, replica_groups=mesh['z'=8,'core'=2,'y'=4,'x'=4] {'z'}, dimensions={0} | all-to-all | bytes 2097152 | tf_op jit(solution)/shard_map/all_to_all | solution.py:256
  222.9 0.7 reduce_sum.49
  (53 shorter events, 0.5 us)
Async XLA Ops:
  6.5 44.3 %all-gather.7.cloned.1.call-start = ((), (), s32[]{:S(2)}) async-start(), calls=%async_computation.1 | async-start | bytes 1671168 | tf_op jit(solution)/shard_map/all_gather | solution.py:225
  8.0 134.9 %all-gather.9.cloned.1.call-start = ((), (), s32[]{:S(2)}) async-start(), calls=%async_computation.2 | async-start | bytes 8912896 | tf_op jit(solution)/shard_map/all_gather | solution.py:230
  9.0 7.8 %collective-permute-start.3 = (f32[64,512]{1,0:T(8,128)S(1)}, f32[64,512]{1,0:T(8,128)S(1)}, u32[]{:S(2)}, u32[]{:S(2)}) collective-permute-start(f32[64,512]{1,0:T(8,128)S(1)} %constant_dynamic-slice_fusion.1), channel_id=1, source_target_pairs={{2,0},{3,1},{4,2},{5,3},{6,4},{7,5},{8,6},{9,7},{10,8},{11,9},{12,... | collective-permute-start | bytes 393224 | tf_op jit(solution)/shard_map/ppermute | solution.py:189
  12.3 5.5 %collective-permute-start.2 = (f32[64,512]{1,0:T(8,128)S(1)}, f32[64,512]{1,0:T(8,128)S(1)}, u32[]{:S(2)}, u32[]{:S(2)}) collective-permute-start(f32[64,512]{1,0:T(8,128)S(1)} %constant_dynamic-slice_fusion.1), channel_id=1, source_target_pairs={{1,0},{2,1},{3,2},{4,3},{5,4},{6,5},{7,6},{8,7},{9,8},{10,9},{11,1... | collective-permute-start | bytes 393224 | tf_op jit(solution)/shard_map/ppermute | solution.py:189
  14.2 7.2 %collective-permute-start.1 = (f32[64,512]{1,0:T(8,128)S(1)}, f32[64,512]{1,0:T(8,128)S(1)}, u32[]{:S(2)}, u32[]{:S(2)}) collective-permute-start(f32[64,512]{1,0:T(8,128)S(1)} %constant_dynamic-slice_fusion.1), channel_id=1, source_target_pairs={{0,1},{1,2},{2,3},{3,4},{4,5},{5,6},{6,7},{7,8},{8,9},{9,10},{10,1... | collective-permute-start | bytes 393224 | tf_op jit(solution)/shard_map/ppermute | solution.py:189
  15.5 9.9 %collective-permute-start = (f32[64,512]{1,0:T(8,128)S(1)}, f32[64,512]{1,0:T(8,128)S(1)}, u32[]{:S(2)}, u32[]{:S(2)}) collective-permute-start(f32[64,512]{1,0:T(8,128)S(1)} %constant_dynamic-slice_fusion.1), channel_id=1, source_target_pairs={{0,2},{1,3},{2,4},{3,5},{4,6},{5,7},{6,8},{7,9},{8,10},{9,11},{10,... | collective-permute-start | bytes 393224 | tf_op jit(solution)/shard_map/ppermute | solution.py:189
  50.8 1.4 copy-start.5
  50.8 114.5 %all-gather.11.cloned.1.call-start = ((), (), s32[]{:S(2)}) async-start(), calls=%async_computation.3 | async-start | bytes 4718592 | tf_op jit(solution)/shard_map/all_gather | solution.py:249
  52.3 1.3 slice-start
  52.4 12.6 %collective-permute-start.6 = (f32[16,24,256]{2,1,0:T(8,128)S(1)}, f32[16,24,256]{2,1,0:T(8,128)S(1)}, u32[]{:S(2)}, u32[]{:S(2)}) collective-permute-start(f32[16,24,256]{2,1,0:T(8,128)S(1)} %get-tuple-element.24), channel_id=1, source_target_pairs={{0,3},{1,0},{2,1},{3,2},{4,7},{5,4},{6,5},{7,6},{8,11},{9,8},{10,9... | collective-permute-start | bytes 1179656 | tf_op jit(solution)/shard_map/ppermute | solution.py:177
  53.6 1.6 collective-permute-start.5
  69.7 73.2 %collective-permute-start.4 = (f32[8,128,1024]{2,1,0:T(8,128)}, f32[8,128,1024]{2,1,0:T(8,128)}, u32[]{:S(2)}, u32[]{:S(2)}) collective-permute-start(f32[8,128,1024]{2,1,0:T(8,128)} %dynamic-slice_bitcast_fusion), channel_id=1, source_target_pairs={{0,16},{16,0},{1,17},{17,1},{2,18},{18,2},{3,19},{19,3},{4,20},{20... | collective-permute-start | bytes 12582920 | tf_op jit(solution)/shard_map/ppermute | solution.py:238
  69.7 11.5 %collective-permute-start.8 = (f32[16,24,256]{2,1,0:T(8,128)S(1)}, f32[16,24,256]{2,1,0:T(8,128)S(1)}, u32[]{:S(2)}, u32[]{:S(2)}) collective-permute-start(f32[16,24,256]{2,1,0:T(8,128)S(1)} %get-tuple-element.24), channel_id=1, source_target_pairs={{0,1},{1,2},{2,3},{3,0},{4,5},{5,6},{6,7},{7,4},{8,9},{9,10},{10,1... | collective-permute-start | bytes 1179656 | tf_op jit(solution)/shard_map/ppermute | solution.py:177
  69.7 13.7 %collective-permute-start.16 = (f32[16,24,256]{2,1,0:T(8,128)S(1)}, f32[16,24,256]{2,1,0:T(8,128)S(1)}, u32[]{:S(2)}, u32[]{:S(2)}) collective-permute-start(f32[16,24,256]{2,1,0:T(8,128)S(1)} %get-tuple-element.23), channel_id=1, source_target_pairs={{0,4},{4,8},{8,12},{12,0},{1,5},{5,9},{9,13},{13,1},{2,6},{6,10},{... | collective-permute-start | bytes 1179656 | tf_op jit(solution)/shard_map/ppermute | solution.py:177
  70.5 13.8 %collective-permute-start.14 = (f32[16,24,256]{2,1,0:T(8,128)S(1)}, f32[16,24,256]{2,1,0:T(8,128)S(1)}, u32[]{:S(2)}, u32[]{:S(2)}) collective-permute-start(f32[16,24,256]{2,1,0:T(8,128)S(1)} %get-tuple-element.23), channel_id=1, source_target_pairs={{0,12},{4,0},{8,4},{12,8},{1,13},{5,1},{9,5},{13,9},{2,14},{6,2},{... | collective-permute-start | bytes 1179656 | tf_op jit(solution)/shard_map/ppermute | solution.py:177
  81.3 6.7 %collective-permute-start.9 = (f32[8,24,256]{2,1,0:T(8,128)S(1)}, f32[8,24,256]{2,1,0:T(8,128)S(1)}, u32[]{:S(2)}, u32[]{:S(2)}) collective-permute-start(f32[8,24,256]{2,1,0:T(8,128)S(1)} %slice.60), channel_id=1, source_target_pairs={{0,1},{1,2},{2,3},{3,0},{4,5},{5,6},{6,7},{7,4},{8,9},{9,10},{10,1... | collective-permute-start | bytes 589832 | tf_op jit(solution)/shard_map/ppermute | solution.py:177
  82.9 7.8 %collective-permute-start.7 = (f32[8,24,256]{2,1,0:T(8,128)S(1)}, f32[8,24,256]{2,1,0:T(8,128)S(1)}, u32[]{:S(2)}, u32[]{:S(2)}) collective-permute-start(f32[8,24,256]{2,1,0:T(8,128)S(1)} %slice.59), channel_id=1, source_target_pairs={{0,3},{1,0},{2,1},{3,2},{4,7},{5,4},{6,5},{7,6},{8,11},{9,8},{10,9... | collective-permute-start | bytes 589832 | tf_op jit(solution)/shard_map/ppermute | solution.py:177
  83.5 10.7 %collective-permute-start.17 = (f32[8,24,256]{2,1,0:T(8,128)S(1)}, f32[8,24,256]{2,1,0:T(8,128)S(1)}, u32[]{:S(2)}, u32[]{:S(2)}) collective-permute-start(f32[8,24,256]{2,1,0:T(8,128)S(1)} %slice.65), channel_id=1, source_target_pairs={{0,4},{4,8},{8,12},{12,0},{1,5},{5,9},{9,13},{13,1},{2,6},{6,10},{... | collective-permute-start | bytes 589832 | tf_op jit(solution)/shard_map/ppermute | solution.py:177
  84.3 9.9 %collective-permute-start.15 = (f32[8,24,256]{2,1,0:T(8,128)S(1)}, f32[8,24,256]{2,1,0:T(8,128)S(1)}, u32[]{:S(2)}, u32[]{:S(2)}) collective-permute-start(f32[8,24,256]{2,1,0:T(8,128)S(1)} %slice.64), channel_id=1, source_target_pairs={{0,12},{4,0},{8,4},{12,8},{1,13},{5,1},{9,5},{13,9},{2,14},{6,2},{... | collective-permute-start | bytes 589832 | tf_op jit(solution)/shard_map/ppermute | solution.py:177
  90.9 3.5 %copy-start = (f32[4,16,24,256]{3,2,1,0:T(8,128)}, f32[4,16,24,256]{3,2,1,0:T(8,128)S(1)}, u32[]{:S(2)}) copy-start(f32[4,16,24,256]{3,2,1,0:T(8,128)S(1)} %pad_maximum_fusion.refs_0_) | copy-start | bytes 4718596
  90.9 36.7 %collective-permute-start.10 = (f32[4,16,24,256]{3,2,1,0:T(8,128)S(1)}, f32[4,16,24,256]{3,2,1,0:T(8,128)}, u32[]{:S(2)}, u32[]{:S(2)}) collective-permute-start(f32[4,16,24,256]{3,2,1,0:T(8,128)S(1)} %pad_maximum_fusion.refs_0_), channel_id=1, source_target_pairs={{0,12},{4,0},{8,4},{12,8},{1,13},{5,1},{9,5},{13,9},{2,14},{6,2},{... | collective-permute-start | bytes 4718600 | tf_op jit(solution)/shard_map/ppermute | solution.py:177
  92.0 37.7 %collective-permute-start.12 = (f32[4,16,24,256]{3,2,1,0:T(8,128)S(1)}, f32[4,16,24,256]{3,2,1,0:T(8,128)}, u32[]{:S(2)}, u32[]{:S(2)}) collective-permute-start(f32[4,16,24,256]{3,2,1,0:T(8,128)S(1)} %pad_maximum_fusion.refs_0_), channel_id=1, source_target_pairs={{0,4},{4,8},{8,12},{12,0},{1,5},{5,9},{9,13},{13,1},{2,6},{6,10},{... | collective-permute-start | bytes 4718600 | tf_op jit(solution)/shard_map/ppermute | solution.py:177
  94.2 3.5 %copy-start.7 = (s32[128]{0:T(128)S(1)}, s32[128]{0:T(128)}, u32[]{:S(2)}) copy-start(s32[128]{0:T(128)} %param.9) | copy-start | bytes 1540
  94.3 4.3 %copy-start.6 = (s32[16,16]{1,0:T(8,128)S(1)}, s32[16,16]{1,0:T(8,128)}, u32[]{:S(2)}) copy-start(s32[16,16]{1,0:T(8,128)} %param.11) | copy-start | bytes 3076
  94.3 4.8 %copy-start.8 = (s32[32]{0:T(128)S(1)}, s32[32]{0:T(128)}, u32[]{:S(2)}) copy-start(s32[32]{0:T(128)} %param.10) | copy-start | bytes 388
  94.4 37.4 %copy-start.1 = (f32[4,16,24,256]{3,2,1,0:T(8,128)}, f32[4,16,24,256]{3,2,1,0:T(8,128)S(1)}, u32[]{:S(2)}) copy-start(f32[4,16,24,256]{3,2,1,0:T(8,128)S(1)} %pad_maximum_fusion.1.refs_5_) | copy-start | bytes 4718596
  94.4 40.6 %collective-permute-start.18 = (f32[4,16,24,256]{3,2,1,0:T(8,128)S(1)}, f32[4,16,24,256]{3,2,1,0:T(8,128)}, u32[]{:S(2)}, u32[]{:S(2)}) collective-permute-start(f32[4,16,24,256]{3,2,1,0:T(8,128)S(1)} %pad_maximum_fusion.1.refs_5_), channel_id=1, source_target_pairs={{0,3},{1,0},{2,1},{3,2},{4,7},{5,4},{6,5},{7,6},{8,11},{9,8},{10,9... | collective-permute-start | bytes 4718600 | tf_op jit(solution)/shard_map/ppermute | solution.py:177
  94.5 42.6 %collective-permute-start.20 = (f32[4,16,24,256]{3,2,1,0:T(8,128)S(1)}, f32[4,16,24,256]{3,2,1,0:T(8,128)}, u32[]{:S(2)}, u32[]{:S(2)}) collective-permute-start(f32[4,16,24,256]{3,2,1,0:T(8,128)S(1)} %pad_maximum_fusion.1.refs_5_), channel_id=1, source_target_pairs={{0,1},{1,2},{2,3},{3,0},{4,5},{5,6},{6,7},{7,4},{8,9},{9,10},{10,1... | collective-permute-start | bytes 4718600 | tf_op jit(solution)/shard_map/ppermute | solution.py:177
  129.7 35.6 %collective-permute-start.11 = (f32[2,16,24,256]{3,2,1,0:T(8,128)}, f32[2,16,24,256]{3,2,1,0:T(8,128)}, u32[]{:S(2)}, u32[]{:S(2)}) collective-permute-start(f32[2,16,24,256]{3,2,1,0:T(8,128)} %slice.61), channel_id=1, source_target_pairs={{0,12},{4,0},{8,4},{12,8},{1,13},{5,1},{9,5},{13,9},{2,14},{6,2},{... | collective-permute-start | bytes 2359304 | tf_op jit(solution)/shard_map/ppermute | solution.py:177
  131.8 33.5 %collective-permute-start.13 = (f32[2,16,24,256]{3,2,1,0:T(8,128)}, f32[2,16,24,256]{3,2,1,0:T(8,128)S(1)}, u32[]{:S(2)}, u32[]{:S(2)}) collective-permute-start(f32[2,16,24,256]{3,2,1,0:T(8,128)} %slice.62), channel_id=1, source_target_pairs={{0,4},{4,8},{8,12},{12,0},{1,5},{5,9},{9,13},{13,1},{2,6},{6,10},{... | collective-permute-start | bytes 2359304 | tf_op jit(solution)/shard_map/ppermute | solution.py:177
  137.1 28.2 %collective-permute-start.19 = (f32[2,16,24,256]{3,2,1,0:T(8,128)}, f32[2,16,24,256]{3,2,1,0:T(8,128)S(1)}, u32[]{:S(2)}, u32[]{:S(2)}) collective-permute-start(f32[2,16,24,256]{3,2,1,0:T(8,128)} %slice.66), channel_id=1, source_target_pairs={{0,3},{1,0},{2,1},{3,2},{4,7},{5,4},{6,5},{7,6},{8,11},{9,8},{10,9... | collective-permute-start | bytes 2359304 | tf_op jit(solution)/shard_map/ppermute | solution.py:177
  138.3 27.0 %collective-permute-start.21 = (f32[2,16,24,256]{3,2,1,0:T(8,128)S(1)}, f32[2,16,24,256]{3,2,1,0:T(8,128)S(1)}, u32[]{:S(2)}, u32[]{:S(2)}) collective-permute-start(f32[2,16,24,256]{3,2,1,0:T(8,128)S(1)} %slice.67), channel_id=1, source_target_pairs={{0,1},{1,2},{2,3},{3,0},{4,5},{5,6},{6,7},{7,4},{8,9},{9,10},{10,1... | collective-permute-start | bytes 2359304 | tf_op jit(solution)/shard_map/ppermute | solution.py:177
  165.3 0.9 copy-start.2
  165.3 1.1 copy-start.3
  165.3 1.4 copy-start.4
  185.3 3.0 %collective-permute-start.22 = (f32[8,32,1024]{2,1,0:T(8,128)}, f32[8,32,1024]{2,1,0:T(8,128)S(1)}, u32[]{:S(2)}, u32[]{:S(2)}) collective-permute-start(f32[8,32,1024]{2,1,0:T(8,128)} %get-tuple-element.16), channel_id=1, source_target_pairs={{0,16},{16,0},{1,17},{17,1},{2,18},{18,2},{3,19},{19,3},{4,20},{20... | collective-permute-start | bytes 3145736 | tf_op jit(solution)/shard_map/ppermute | solution.py:255
Sparse Core Ops, SparseCore 0:
  9.2 41.5 all-gather.6
  52.6 54.7 all-gather.8
  109.2 53.3 all-gather.10

commit v5 on v1

--- a/solution.py
+++ b/solution.py
@@ -227,6 +227,7 @@
     )
     plan = make_plan(tile_sector, term_charge, block_home, home, core, x, y)
 
+    env_other, column = lax.optimization_barrier((env_other, column))
     mine = lax.dynamic_index_in_dim(column, core, axis=1, keepdims=False)
     parts = []
     for at, (first, then) in enumerate((("x", "y"), ("y", "x"))):

time: 235 us -> 232 us (0.987)
  transfers between devices with their start and end apart: 24 -> 24, of which waited for: 9 -> 8; matrix products, arithmetic and copies ran while one was open for 9% -> 10% of each run, Pallas kernels for 10% -> 10%
where the time goes in v5:
time: 232 us; the launch traced here: 229 us
  waiting for transfers between devices  77.5 us (33%)
  Pallas kernels  41.8 us (18%)
  starting transfers between devices  35.7 us (15%)
  blocking collectives  33.5 us (14%)
  local copies, waits for them, and re-layouts  20.7 us (9%)
  between operations  13.7 us (6%)
  other arithmetic  6.52 us (3%)
    ppermute x16, waiting for transfers between devices, ring(): lax.ppermute(value, axis, [(i, (i - steps) % count) for i in range(count)])  51.8 us
    all_to_all x1, blocking collectives, on_device(): shares = lax.all_to_all(total, 'z', split_axis=0, concat_axis=0, tiled=True)  33.5 us
    pallas_call x1, Pallas kernels, left_products(): pl.pallas_call(left_kernel, grid_spec=grid, out_shape=jax.ShapeDtypeStruc...  23.1 us
    ppermute x16, starting transfers between devices, ring(): lax.ppermute(value, axis, [(i, (i - steps) % count) for i in range(count)])  21.5 us
    pallas_call x1, Pallas kernels, right_products(): pl.pallas_call(right_kernel, grid_spec=grid, out_shape=[out, out], compil...  18.7 us
    all_gather x1, waiting for transfers between devices, on_device(): column = lax.all_gather(jnp.stack([by_y, by_x], axis=1), ('z', 'core'))  17.3 us
    ppermute x4, starting transfers between devices, wide_shift(): lax.ppermute(value, ('y', 'x'), [(i, i + steps) for i in range(max(0, -st...  14.1 us
    ppermute x4, waiting for transfers between devices, wide_shift(): lax.ppermute(value, ('y', 'x'), [(i, i + steps) for i in range(max(0, -st...  5.52 us
  transfers between devices with their start and end apart: 24, of which 8 were waited for; matrix products, arithmetic and copies ran while one was open for 10% of the time, Pallas kernels for 10%

profile of v5, /device:TPU:6, one launch (start us, length us, event | category | flops | bytes accessed | tf_op | source)
XLA Modules:
  0.0 229.4 jit_solution(8541179888848532324)
XLA Ops:
  6.5 0.9 dynamic-slice_bitcast_fusion.2
  7.4 0.7 pad_maximum_fusion.3
  8.1 0.0 all-gather.7.cloned.1.call-update
  8.1 0.0 all-gather.5.cloned.1.call-start
  8.2 0.9 constant_dynamic-slice_fusion
  9.1 3.3 %collective-permute-start.3 = (f32[64,512]{1,0:T(8,128)S(1)}, f32[64,512]{1,0:T(8,128)S(1)}, u32[]{:S(2)}, u32[]{:S(2)}) collective-permute-start(f32[64,512]{1,0:T(8,128)S(1)} %constant_dynamic-slice_fusion), channel_id=1, source_target_pairs={{2,0},{3,1},{4,2},{5,3},{6,4},{7,5},{8,6},{9,7},{10,8},{11,9},{12,... | collective-permute-start | bytes 393224 | tf_op jit(solution)/shard_map/ppermute | solution.py:183
  12.4 3.6 %collective-permute-start.2 = (f32[64,512]{1,0:T(8,128)S(1)}, f32[64,512]{1,0:T(8,128)S(1)}, u32[]{:S(2)}, u32[]{:S(2)}) collective-permute-start(f32[64,512]{1,0:T(8,128)S(1)} %constant_dynamic-slice_fusion), channel_id=1, source_target_pairs={{1,0},{2,1},{3,2},{4,3},{5,4},{6,5},{7,6},{8,7},{9,8},{10,9},{11,1... | collective-permute-start | bytes 393224 | tf_op jit(solution)/shard_map/ppermute | solution.py:183
  16.0 4.4 %collective-permute-start.1 = (f32[64,512]{1,0:T(8,128)S(1)}, f32[64,512]{1,0:T(8,128)S(1)}, u32[]{:S(2)}, u32[]{:S(2)}) collective-permute-start(f32[64,512]{1,0:T(8,128)S(1)} %constant_dynamic-slice_fusion), channel_id=1, source_target_pairs={{0,1},{1,2},{2,3},{3,4},{4,5},{5,6},{6,7},{7,8},{8,9},{9,10},{10,1... | collective-permute-start | bytes 393224 | tf_op jit(solution)/shard_map/ppermute | solution.py:183
  20.4 2.8 %collective-permute-start = (f32[64,512]{1,0:T(8,128)S(1)}, f32[64,512]{1,0:T(8,128)S(1)}, u32[]{:S(2)}, u32[]{:S(2)}) collective-permute-start(f32[64,512]{1,0:T(8,128)S(1)} %constant_dynamic-slice_fusion), channel_id=1, source_target_pairs={{0,2},{1,3},{2,4},{3,5},{4,6},{5,7},{6,8},{7,9},{8,10},{9,11},{10,... | collective-permute-start | bytes 393224 | tf_op jit(solution)/shard_map/ppermute | solution.py:183
  23.2 1.1 collective-permute-done.1
  24.3 4.5 %collective-permute-done = f32[64,512]{1,0:T(8,128)S(1)} collective-permute-done((f32[64,512]{1,0:T(8,128)S(1)}, f32[64,512]{1,0:T(8,128)S(1)}, u32[]{:S(2)}, u32[]{:S(2)}) %collective-permute-start) | collective-permute-done | bytes 131104 | tf_op jit(solution)/shard_map/ppermute | solution.py:183
  28.7 0.8 pad_maximum_fusion.2
  29.6 0.0 all-gather.5.cloned.1.call-update
  29.6 4.8 %dynamic-slice_bitcast_fusion = f32[8,128,1024]{2,1,0:T(8,128)} fusion(f32[8,2,128,1024]{3,2,1,0:T(8,128)} %bitcast.40, s32[]{:T(128)S(6)} %select_n.52), kind=kLoop, calls=%fused_computation | loop fusion | bytes 8388612 | tf_op jit(solution)/shard_map/jit(dynamic_index_in_dim)/squeeze | solution.py:226
  34.4 17.3 %all-gather.7.cloned.1.call-done = f32[32,2,32,256]{3,2,1,0:T(8,128)} async-done(((f32[2,2,32,256]{3,2,1,0:T(8,128)}), f32[32,2,32,256]{3,2,1,0:T(8,128)}) %all-gather.7.cloned.1.call-update) | async-done | bytes 2097168 | tf_op jit(solution)/shard_map/all_gather | solution.py:218
  51.7 1.3 copy_bitcast_fusion
  53.0 0.1 slice_bitcast_fusion.1
  53.2 1.6 collective-permute-start.15
  54.7 1.8 collective-permute-start.13
  56.5 0.7 collective-permute-start.7
  57.2 1.3 collective-permute-start.5
  58.5 10.0 %collective-permute-done.15 = f32[16,32,256]{2,1,0:T(8,128)S(1)} collective-permute-done((f32[16,32,256]{2,1,0:T(8,128)S(1)}, f32[16,32,256]{2,1,0:T(8,128)S(1)}, u32[]{:S(2)}, u32[]{:S(2)}) %collective-permute-start.15) | collective-permute-done | bytes 524320 | tf_op jit(solution)/shard_map/ppermute | solution.py:171
  68.6 0.4 collective-permute-start.16
  68.9 3.0 %collective-permute-start.14 = (f32[8,32,256]{2,1,0:T(8,128)S(1)}, f32[8,32,256]{2,1,0:T(8,128)S(1)}, u32[]{:S(2)}, u32[]{:S(2)}) collective-permute-start(f32[8,32,256]{2,1,0:T(8,128)S(1)} %slice.60), channel_id=1, source_target_pairs={{0,12},{4,0},{8,4},{12,8},{1,13},{5,1},{9,5},{13,9},{2,14},{6,2},{... | collective-permute-start | bytes 786440 | tf_op jit(solution)/shard_map/ppermute | solution.py:171
  72.0 0.8 collective-permute-start.8
  72.8 1.4 collective-permute-start.6
  74.2 3.4 %collective-permute-done.16 = f32[8,32,256]{2,1,0:T(8,128)S(1)} collective-permute-done((f32[8,32,256]{2,1,0:T(8,128)S(1)}, f32[8,32,256]{2,1,0:T(8,128)S(1)}, u32[]{:S(2)}, u32[]{:S(2)}) %collective-permute-start.16) | collective-permute-done | bytes 262176 | tf_op jit(solution)/shard_map/ppermute | solution.py:171
  77.7 0.1 pad_maximum_fusion.1.refs_5_
  77.8 0.8 collective-permute-start.19
  78.6 1.3 collective-permute-start.17
  79.9 1.2 collective-permute-done.6
  81.2 1.5 pad_maximum_fusion.refs_0_
  82.7 3.2 %collective-permute-start.9 = (f32[4,16,32,256]{3,2,1,0:T(8,128)}, f32[4,16,32,256]{3,2,1,0:T(8,128)}, u32[]{:S(2)}, u32[]{:S(2)}) collective-permute-start(f32[4,16,32,256]{3,2,1,0:T(8,128)} %pad_maximum_fusion.refs_0_), channel_id=1, source_target_pairs={{0,12},{4,0},{8,4},{12,8},{1,13},{5,1},{9,5},{13,9},{2,14},{6,2},{... | collective-permute-start | bytes 6291464 | tf_op jit(solution)/shard_map/ppermute | solution.py:171
  85.9 0.6 slice.41
  86.5 0.1 dynamic_slice.20
  86.6 0.1 broadcast_in_dim.28
  86.6 0.1 reshape.33
  86.7 0.1 copy.17
  86.8 0.2 select_reduce_fusion.1
  87.0 0.1 copy.18
  87.1 0.1 reshape.35
  87.2 37.1 %collective-permute-done.19.refs_9_ = f32[4,16,32,256]{3,2,1,0:T(8,128)} collective-permute-done((f32[4,16,32,256]{3,2,1,0:T(8,128)S(1)}, f32[4,16,32,256]{3,2,1,0:T(8,128)}, u32[]{:S(2)}, u32[]{:S(2)}) %collective-permute-start.19) | collective-permute-done | bytes 2097184 | tf_op jit(solution)/shard_map/ppermute | solution.py:171
  124.3 2.3 %slice.63 = f32[2,16,32,256]{3,2,1,0:T(8,128)} slice(f32[4,16,32,256]{3,2,1,0:T(8,128)} %collective-permute-done.19.refs_9_), slice={[2:4], [0:16], [0:32], [0:256]} | slice | bytes 2097152 | tf_op jit(solution)/shard_map/slice | solution.py:177
  126.7 1.9 collective-permute-start.20
  128.6 2.4 %slice.62 = f32[2,16,32,256]{3,2,1,0:T(8,128)} slice(f32[4,16,32,256]{3,2,1,0:T(8,128)} %collective-permute-done.17.refs_6_), slice={[0:2], [0:16], [0:32], [0:256]} | slice | bytes 2097152 | tf_op jit(solution)/shard_map/slice | solution.py:176
  130.9 0.1 collective-permute-start.18
  131.1 2.3 %slice.58 = f32[2,16,32,256]{3,2,1,0:T(8,128)} slice(f32[4,16,32,256]{3,2,1,0:T(8,128)} %collective-permute-done.11.refs_4_), slice={[2:4], [0:16], [0:32], [0:256]} | slice | bytes 2097152 | tf_op jit(solution)/shard_map/slice | solution.py:177
  133.4 0.0 collective-permute-start.12
  133.4 2.3 %slice.57 = f32[2,16,32,256]{3,2,1,0:T(8,128)} slice(f32[4,16,32,256]{3,2,1,0:T(8,128)} %collective-permute-done.9.refs_1_), slice={[0:2], [0:16], [0:32], [0:256]} | slice | bytes 2097152 | tf_op jit(solution)/shard_map/slice | solution.py:176
  135.7 3.2 %collective-permute-start.10 = (f32[2,16,32,256]{3,2,1,0:T(8,128)}, f32[2,16,32,256]{3,2,1,0:T(8,128)}, u32[]{:S(2)}, u32[]{:S(2)}) collective-permute-start(f32[2,16,32,256]{3,2,1,0:T(8,128)} %slice.57), channel_id=1, source_target_pairs={{0,12},{4,0},{8,4},{12,8},{1,13},{5,1},{9,5},{13,9},{2,14},{6,2},{... | collective-permute-start | bytes 3145736 | tf_op jit(solution)/shard_map/ppermute | solution.py:171
  139.0 0.2 select_reduce_fusion
  139.1 0.2 convert_reduce_fusion
  139.3 0.7 broadcast_select_fusion.1
  140.0 0.6 concatenate.9.plan
  140.6 23.1 %left_products.1.left = f32[16,128,512]{2,1,0:T(8,128)} custom-call(s32[51]{0:T(128)} %concatenate.9.plan, f32[1024,512]{1,0:T(8,128)} %own.1, f32[16,4,64,512]{3,2,1,0:T(8,128)} %bitcast.41, f32[16,128,1024]{2,1,0:T(8,128)} %env_own.1, f32[8,128,1024]{2,1,0:T(8,128)} %collective-permute-done.4.env_other), custom_call_target="tpu_custom_call" | custom-call | flops 6442450944 | bytes 25165824 | tf_op jit(solution)/shard_map/left_products/pallas_call | solution.py:96
  163.7 0.9 copy-done.1
  164.7 0.3 copy-done.2
  165.0 0.3 copy-done.3
  165.3 18.7 %right_products.1 = (f32[8,32,1024]{2,1,0:T(8,128)}, f32[8,32,1024]{2,1,0:T(8,128)}) custom-call(s32[51]{0:T(128)} %concatenate.9.plan, f32[16,128,512]{2,1,0:T(8,128)} %left_products.1.left, f32[4,16,32,256]{3,2,1,0:T(8,128)} %pad_maximum_fusion.refs_0_, f32[4,16,32,256]{3,2,1,0:T(8,128)} %collective-permute-done.9.refs_1_, ...), custom_call_target="tpu_custom_call" | custom-call | flops 3221225472 | bytes 23068672 | tf_op jit(solution)/shard_map/right_products/pallas_call | solution.py:157
  184.0 0.1 collective-permute-start.21
  184.1 2.9 %collective-permute-done.21 = f32[8,32,1024]{2,1,0:T(8,128)S(1)} collective-permute-done((f32[8,32,1024]{2,1,0:T(8,128)}, f32[8,32,1024]{2,1,0:T(8,128)S(1)}, u32[]{:S(2)}, u32[]{:S(2)}) %collective-permute-start.21) | collective-permute-done | bytes 1048608 | tf_op jit(solution)/shard_map/ppermute | solution.py:240
  187.0 1.4 add.79
  188.4 33.5 %all_to_all.5 = f32[8,32,1024]{2,1,0:T(8,128)S(1)} all-to-all(f32[8,32,1024]{2,1,0:T(8,128)S(1)} %add.79), channel_id=1, replica_groups=mesh['z'=8,'core'=2,'y'=4,'x'=4] {'z'}, dimensions={0} | all-to-all | bytes 2097152 | tf_op jit(solution)/shard_map/all_to_all | solution.py:241
  221.9 0.7 reduce_sum.49
  (40 shorter events, 0.2 us)
Async XLA Ops:
  6.5 45.2 %all-gather.7.cloned.1.call-start = ((), (), s32[]{:S(2)}) async-start(), calls=%async_computation.2 | async-start | bytes 2228224 | tf_op jit(solution)/shard_map/all_gather | solution.py:218
  8.1 132.5 %all-gather.5.cloned.1.call-start = ((), (), s32[]{:S(2)}) async-start(), calls=%async_computation.1 | async-start | bytes 8912896 | tf_op jit(solution)/shard_map/all_gather | solution.py:222
  9.1 14.1 %collective-permute-start.3 = (f32[64,512]{1,0:T(8,128)S(1)}, f32[64,512]{1,0:T(8,128)S(1)}, u32[]{:S(2)}, u32[]{:S(2)}) collective-permute-start(f32[64,512]{1,0:T(8,128)S(1)} %constant_dynamic-slice_fusion), channel_id=1, source_target_pairs={{2,0},{3,1},{4,2},{5,3},{6,4},{7,5},{8,6},{9,7},{10,8},{11,9},{12,... | collective-permute-start | bytes 393224 | tf_op jit(solution)/shard_map/ppermute | solution.py:183
  12.4 10.8 %collective-permute-start.2 = (f32[64,512]{1,0:T(8,128)S(1)}, f32[64,512]{1,0:T(8,128)S(1)}, u32[]{:S(2)}, u32[]{:S(2)}) collective-permute-start(f32[64,512]{1,0:T(8,128)S(1)} %constant_dynamic-slice_fusion), channel_id=1, source_target_pairs={{1,0},{2,1},{3,2},{4,3},{5,4},{6,5},{7,6},{8,7},{9,8},{10,9},{11,1... | collective-permute-start | bytes 393224 | tf_op jit(solution)/shard_map/ppermute | solution.py:183
  16.0 8.3 %collective-permute-start.1 = (f32[64,512]{1,0:T(8,128)S(1)}, f32[64,512]{1,0:T(8,128)S(1)}, u32[]{:S(2)}, u32[]{:S(2)}) collective-permute-start(f32[64,512]{1,0:T(8,128)S(1)} %constant_dynamic-slice_fusion), channel_id=1, source_target_pairs={{0,1},{1,2},{2,3},{3,4},{4,5},{5,6},{6,7},{7,8},{8,9},{9,10},{10,1... | collective-permute-start | bytes 393224 | tf_op jit(solution)/shard_map/ppermute | solution.py:183
  20.4 8.4 %collective-permute-start = (f32[64,512]{1,0:T(8,128)S(1)}, f32[64,512]{1,0:T(8,128)S(1)}, u32[]{:S(2)}, u32[]{:S(2)}) collective-permute-start(f32[64,512]{1,0:T(8,128)S(1)} %constant_dynamic-slice_fusion), channel_id=1, source_target_pairs={{0,2},{1,3},{2,4},{3,5},{4,6},{5,7},{6,8},{7,9},{8,10},{9,11},{10,... | collective-permute-start | bytes 393224 | tf_op jit(solution)/shard_map/ppermute | solution.py:183
  34.4 17.3 %collective-permute-start.4 = (f32[8,128,1024]{2,1,0:T(8,128)}, f32[8,128,1024]{2,1,0:T(8,128)}, u32[]{:S(2)}, u32[]{:S(2)}) collective-permute-start(f32[8,128,1024]{2,1,0:T(8,128)} %dynamic-slice_bitcast_fusion), channel_id=1, source_target_pairs={{0,16},{16,0},{1,17},{17,1},{2,18},{18,2},{3,19},{19,3},{4,20},{20... | collective-permute-start | bytes 12582920 | tf_op jit(solution)/shard_map/ppermute | solution.py:225
  53.2 15.4 %collective-permute-start.15 = (f32[16,32,256]{2,1,0:T(8,128)S(1)}, f32[16,32,256]{2,1,0:T(8,128)S(1)}, u32[]{:S(2)}, u32[]{:S(2)}) collective-permute-start(f32[16,32,256]{2,1,0:T(8,128)S(1)} %get-tuple-element.19), channel_id=1, source_target_pairs={{0,4},{4,8},{8,12},{12,0},{1,5},{5,9},{9,13},{13,1},{2,6},{6,10},{... | collective-permute-start | bytes 1572872 | tf_op jit(solution)/shard_map/ppermute | solution.py:171
  54.7 14.2 %collective-permute-start.13 = (f32[16,32,256]{2,1,0:T(8,128)S(1)}, f32[16,32,256]{2,1,0:T(8,128)S(1)}, u32[]{:S(2)}, u32[]{:S(2)}) collective-permute-start(f32[16,32,256]{2,1,0:T(8,128)S(1)} %get-tuple-element.19), channel_id=1, source_target_pairs={{0,12},{4,0},{8,4},{12,8},{1,13},{5,1},{9,5},{13,9},{2,14},{6,2},{... | collective-permute-start | bytes 1572872 | tf_op jit(solution)/shard_map/ppermute | solution.py:171
  56.5 15.5 %collective-permute-start.7 = (f32[16,32,256]{2,1,0:T(8,128)S(1)}, f32[16,32,256]{2,1,0:T(8,128)S(1)}, u32[]{:S(2)}, u32[]{:S(2)}) collective-permute-start(f32[16,32,256]{2,1,0:T(8,128)S(1)} %get-tuple-element.18), channel_id=1, source_target_pairs={{0,1},{1,2},{2,3},{3,0},{4,5},{5,6},{6,7},{7,4},{8,9},{9,10},{10,1... | collective-permute-start | bytes 1572872 | tf_op jit(solution)/shard_map/ppermute | solution.py:171
  57.2 15.6 %collective-permute-start.5 = (f32[16,32,256]{2,1,0:T(8,128)S(1)}, f32[16,32,256]{2,1,0:T(8,128)S(1)}, u32[]{:S(2)}, u32[]{:S(2)}) collective-permute-start(f32[16,32,256]{2,1,0:T(8,128)S(1)} %get-tuple-element.18), channel_id=1, source_target_pairs={{0,3},{1,0},{2,1},{3,2},{4,7},{5,4},{6,5},{7,6},{8,11},{9,8},{10,9... | collective-permute-start | bytes 1572872 | tf_op jit(solution)/shard_map/ppermute | solution.py:171
  68.6 9.0 %collective-permute-start.16 = (f32[8,32,256]{2,1,0:T(8,128)S(1)}, f32[8,32,256]{2,1,0:T(8,128)S(1)}, u32[]{:S(2)}, u32[]{:S(2)}) collective-permute-start(f32[8,32,256]{2,1,0:T(8,128)S(1)} %slice.61), channel_id=1, source_target_pairs={{0,4},{4,8},{8,12},{12,0},{1,5},{5,9},{9,13},{13,1},{2,6},{6,10},{... | collective-permute-start | bytes 786440 | tf_op jit(solution)/shard_map/ppermute | solution.py:171
  68.9 8.7 %collective-permute-start.14 = (f32[8,32,256]{2,1,0:T(8,128)S(1)}, f32[8,32,256]{2,1,0:T(8,128)S(1)}, u32[]{:S(2)}, u32[]{:S(2)}) collective-permute-start(f32[8,32,256]{2,1,0:T(8,128)S(1)} %slice.60), channel_id=1, source_target_pairs={{0,12},{4,0},{8,4},{12,8},{1,13},{5,1},{9,5},{13,9},{2,14},{6,2},{... | collective-permute-start | bytes 786440 | tf_op jit(solution)/shard_map/ppermute | solution.py:171
  72.0 7.9 %collective-permute-start.8 = (f32[8,32,256]{2,1,0:T(8,128)S(1)}, f32[8,32,256]{2,1,0:T(8,128)S(1)}, u32[]{:S(2)}, u32[]{:S(2)}) collective-permute-start(f32[8,32,256]{2,1,0:T(8,128)S(1)} %slice.56), channel_id=1, source_target_pairs={{0,1},{1,2},{2,3},{3,0},{4,5},{5,6},{6,7},{7,4},{8,9},{9,10},{10,1... | collective-permute-start | bytes 786440 | tf_op jit(solution)/shard_map/ppermute | solution.py:171
  72.8 8.3 %collective-permute-start.6 = (f32[8,32,256]{2,1,0:T(8,128)S(1)}, f32[8,32,256]{2,1,0:T(8,128)S(1)}, u32[]{:S(2)}, u32[]{:S(2)}) collective-permute-start(f32[8,32,256]{2,1,0:T(8,128)S(1)} %slice.55), channel_id=1, source_target_pairs={{0,3},{1,0},{2,1},{3,2},{4,7},{5,4},{6,5},{7,6},{8,11},{9,8},{10,9... | collective-permute-start | bytes 786440 | tf_op jit(solution)/shard_map/ppermute | solution.py:171
  77.8 4.9 %copy-start = (f32[4,16,32,256]{3,2,1,0:T(8,128)}, f32[4,16,32,256]{3,2,1,0:T(8,128)S(1)}, u32[]{:S(2)}) copy-start(f32[4,16,32,256]{3,2,1,0:T(8,128)S(1)} %pad_maximum_fusion.1.refs_5_) | copy-start | bytes 6291460
  77.8 46.5 %collective-permute-start.19 = (f32[4,16,32,256]{3,2,1,0:T(8,128)S(1)}, f32[4,16,32,256]{3,2,1,0:T(8,128)}, u32[]{:S(2)}, u32[]{:S(2)}) collective-permute-start(f32[4,16,32,256]{3,2,1,0:T(8,128)S(1)} %pad_maximum_fusion.1.refs_5_), channel_id=1, source_target_pairs={{0,1},{1,2},{2,3},{3,0},{4,5},{5,6},{6,7},{7,4},{8,9},{9,10},{10,1... | collective-permute-start | bytes 6291464 | tf_op jit(solution)/shard_map/ppermute | solution.py:171
  78.6 50.0 %collective-permute-start.17 = (f32[4,16,32,256]{3,2,1,0:T(8,128)S(1)}, f32[4,16,32,256]{3,2,1,0:T(8,128)}, u32[]{:S(2)}, u32[]{:S(2)}) collective-permute-start(f32[4,16,32,256]{3,2,1,0:T(8,128)S(1)} %pad_maximum_fusion.1.refs_5_), channel_id=1, source_target_pairs={{0,3},{1,0},{2,1},{3,2},{4,7},{5,4},{6,5},{7,6},{8,11},{9,8},{10,9... | collective-permute-start | bytes 6291464 | tf_op jit(solution)/shard_map/ppermute | solution.py:171
  81.2 4.7 %copy-start.5 = (s32[128]{0:T(128)S(1)}, s32[128]{0:T(128)}, u32[]{:S(2)}) copy-start(s32[128]{0:T(128)} %param.9) | copy-start | bytes 1540
  81.2 5.5 %copy-start.4 = (s32[16,16]{1,0:T(8,128)S(1)}, s32[16,16]{1,0:T(8,128)}, u32[]{:S(2)}) copy-start(s32[16,16]{1,0:T(8,128)} %param.11) | copy-start | bytes 3076
  82.7 48.4 %collective-permute-start.11 = (f32[4,16,32,256]{3,2,1,0:T(8,128)}, f32[4,16,32,256]{3,2,1,0:T(8,128)}, u32[]{:S(2)}, u32[]{:S(2)}) collective-permute-start(f32[4,16,32,256]{3,2,1,0:T(8,128)} %pad_maximum_fusion.refs_0_), channel_id=1, source_target_pairs={{0,4},{4,8},{8,12},{12,0},{1,5},{5,9},{9,13},{13,1},{2,6},{6,10},{... | collective-permute-start | bytes 6291464 | tf_op jit(solution)/shard_map/ppermute | solution.py:171
  82.7 50.8 %collective-permute-start.9 = (f32[4,16,32,256]{3,2,1,0:T(8,128)}, f32[4,16,32,256]{3,2,1,0:T(8,128)}, u32[]{:S(2)}, u32[]{:S(2)}) collective-permute-start(f32[4,16,32,256]{3,2,1,0:T(8,128)} %pad_maximum_fusion.refs_0_), channel_id=1, source_target_pairs={{0,12},{4,0},{8,4},{12,8},{1,13},{5,1},{9,5},{13,9},{2,14},{6,2},{... | collective-permute-start | bytes 6291464 | tf_op jit(solution)/shard_map/ppermute | solution.py:171
  126.7 37.0 %collective-permute-start.20 = (f32[2,16,32,256]{3,2,1,0:T(8,128)}, f32[2,16,32,256]{3,2,1,0:T(8,128)S(1)}, u32[]{:S(2)}, u32[]{:S(2)}) collective-permute-start(f32[2,16,32,256]{3,2,1,0:T(8,128)} %slice.63), channel_id=1, source_target_pairs={{0,1},{1,2},{2,3},{3,0},{4,5},{5,6},{6,7},{7,4},{8,9},{9,10},{10,1... | collective-permute-start | bytes 3145736 | tf_op jit(solution)/shard_map/ppermute | solution.py:171
  130.9 8.0 %copy-start.6 = (s32[32]{0:T(128)S(1)}, s32[32]{0:T(128)}, u32[]{:S(2)}) copy-start(s32[32]{0:T(128)} %param.10) | copy-start | bytes 388
  130.9 32.8 %collective-permute-start.18 = (f32[2,16,32,256]{3,2,1,0:T(8,128)}, f32[2,16,32,256]{3,2,1,0:T(8,128)S(1)}, u32[]{:S(2)}, u32[]{:S(2)}) collective-permute-start(f32[2,16,32,256]{3,2,1,0:T(8,128)} %slice.62), channel_id=1, source_target_pairs={{0,3},{1,0},{2,1},{3,2},{4,7},{5,4},{6,5},{7,6},{8,11},{9,8},{10,9... | collective-permute-start | bytes 3145736 | tf_op jit(solution)/shard_map/ppermute | solution.py:171
  133.4 30.3 %collective-permute-start.12 = (f32[2,16,32,256]{3,2,1,0:T(8,128)}, f32[2,16,32,256]{3,2,1,0:T(8,128)S(1)}, u32[]{:S(2)}, u32[]{:S(2)}) collective-permute-start(f32[2,16,32,256]{3,2,1,0:T(8,128)} %slice.58), channel_id=1, source_target_pairs={{0,4},{4,8},{8,12},{12,0},{1,5},{5,9},{9,13},{13,1},{2,6},{6,10},{... | collective-permute-start | bytes 3145736 | tf_op jit(solution)/shard_map/ppermute | solution.py:171
  135.7 28.0 %collective-permute-start.10 = (f32[2,16,32,256]{3,2,1,0:T(8,128)}, f32[2,16,32,256]{3,2,1,0:T(8,128)}, u32[]{:S(2)}, u32[]{:S(2)}) collective-permute-start(f32[2,16,32,256]{3,2,1,0:T(8,128)} %slice.57), channel_id=1, source_target_pairs={{0,12},{4,0},{8,4},{12,8},{1,13},{5,1},{9,5},{13,9},{2,14},{6,2},{... | collective-permute-start | bytes 3145736 | tf_op jit(solution)/shard_map/ppermute | solution.py:171
  163.7 1.0 copy-start.1
  163.7 1.3 copy-start.2
  163.7 1.6 copy-start.3
  184.0 3.0 %collective-permute-start.21 = (f32[8,32,1024]{2,1,0:T(8,128)}, f32[8,32,1024]{2,1,0:T(8,128)S(1)}, u32[]{:S(2)}, u32[]{:S(2)}) collective-permute-start(f32[8,32,1024]{2,1,0:T(8,128)} %get-tuple-element.12), channel_id=1, source_target_pairs={{0,16},{16,0},{1,17},{17,1},{2,18},{18,2},{3,19},{19,3},{4,20},{20... | collective-permute-start | bytes 3145736 | tf_op jit(solution)/shard_map/ppermute | solution.py:240
Sparse Core Ops, SparseCore 0:
  9.2 42.4 all-gather.6
  53.5 54.3 all-gather.4
